TPU v7x, 128 devices: a whole 4x4x4 slice. The times are simulated.
128 devices in a mesh: gx: 16 (over z_hi, y, core), gy: 8 (over z_lo, x).
Axes of the slice: x: 4, y: 4, z: 4 (z_hi: 2, z_lo: 2; z = z_hi * 2 + z_lo), core: 2. Of those that a mesh axis runs over, the one named last changes fastest.
Arguments:
- slide_tokens: bfloat16 [128, 1024, 768], P('gy', 'gx'), may hold values from -9 to 9
- tissue: int32 [128, 1024], P('gy', 'gx'), may hold values 0 or 1
- grad_tokens: bfloat16 [128, 1024, 768], P('gy', 'gx'), may hold values from -6 to 6
- w_qkv: bfloat16 [768, 2304], replicated, may hold values from -1 to 1
- w_out: bfloat16 [768, 768], replicated, may hold values from -0.21875 to 0.21875
Outputs:
- block_out: bfloat16 [128, 1024, 768], P('gy', 'gx')
- grad_in: bfloat16 [128, 1024, 768], P('gy', 'gx')
- grad_wqkv: float32 [768, 2304], replicated
- grad_wout: float32 [768, 768], replicated
All inputs are finite; a program needn't handle non-finite values. No bound on the sum of `tissue` on one device may be relied on, other than what follows from the above.
Results may differ from a plain program's by a relative error of at most 0.013.
Values may be sent and summed in bfloat16 or wider, within the bound.
No kernel may reach another device: no remote copies, remote signals or barrier semaphores. Data moves between devices by JAX's collectives and lax.ppermute only.
A program may use at most 256 MiB of HBM per device.

v0:
```python
import math

import jax
import jax.numpy as jnp
from jax import lax
from jax.sharding import PartitionSpec as P

HEADS = 24
WIN = 8
SHIFT = 4


epsilon = 1e-05


def shifted_2(block, axis, distance):
    devices = range(lax.axis_size(axis))
    route = [((i - distance) % len(devices), i) for i in devices]
    return lax.ppermute(block, axis, route)


def windows(tensor):
    row_count, col_count, feature_dim = tensor.shape
    tensor = tensor.reshape(row_count // WIN, WIN, col_count // WIN, WIN, feature_dim)
    return tensor.transpose(0, 2, 1, 3, 4).reshape(-1, WIN * WIN, feature_dim)


def unwindows(tensor, row_count, col_count):
    feature_dim = tensor.shape[-1]
    tensor = tensor.reshape(row_count // WIN, col_count // WIN, WIN, WIN, feature_dim)
    return tensor.transpose(0, 2, 1, 3, 4).reshape(row_count, col_count, feature_dim)


def split_heads(tensor):
    return tensor.reshape(tensor.shape[0], tensor.shape[1], HEADS, -1)


def attend(qkv_win, keep_win):
    model_dim = qkv_win.shape[-1] // 3
    queries = split_heads(qkv_win[..., :model_dim])
    keys_part = split_heads(qkv_win[..., model_dim : 2 * model_dim])
    values_part = split_heads(qkv_win[..., 2 * model_dim :])
    score_scale = 1.0 / math.sqrt(model_dim // HEADS)
    scores = (
        jnp.einsum("wqhd,wkhd->whqk", queries, keys_part, preferred_element_type=jnp.float32)
        * score_scale
    )
    win_tokens = qkv_win.shape[1]
    itself = jnp.eye(win_tokens, dtype=bool)
    allowed = jnp.logical_or(keep_win[:, None, None, :] > 0.5, itself[None, None])
    scores = jnp.where(allowed, scores, -1e30)
    maximum = jnp.max(scores, -1, keepdims=True)
    exponent = jnp.exp(scores - maximum)
    attn_probs = exponent / jnp.sum(exponent, -1, keepdims=True)
    weights_half = attn_probs.astype(jnp.bfloat16)
    mixed_out = jnp.einsum(
        "whqk,wkhd->wqhd", weights_half, values_part, preferred_element_type=jnp.float32
    ).astype(jnp.bfloat16)
    return (mixed_out.reshape(qkv_win.shape[0], win_tokens, model_dim), attn_probs)


def attend_back(qkv_win, attn_probs, grad_mixed):
    model_dim = qkv_win.shape[-1] // 3
    window_count, win_tokens = (qkv_win.shape[0], qkv_win.shape[1])
    queries = split_heads(qkv_win[..., :model_dim])
    keys_part = split_heads(qkv_win[..., model_dim : 2 * model_dim])
    values_part = split_heads(qkv_win[..., 2 * model_dim :])
    score_scale = 1.0 / math.sqrt(model_dim // HEADS)
    grad_heads = split_heads(grad_mixed)
    grad_prob = jnp.einsum(
        "wqhd,wkhd->whqk", grad_heads, values_part, preferred_element_type=jnp.float32
    )
    weights_half = attn_probs.astype(jnp.bfloat16)
    grad_value = jnp.einsum(
        "whqk,wqhd->wkhd", weights_half, grad_heads, preferred_element_type=jnp.float32
    ).astype(jnp.bfloat16)
    grad_score = (
        attn_probs * (grad_prob - jnp.sum(grad_prob * attn_probs, -1, keepdims=True)) * score_scale
    )
    score_half = grad_score.astype(jnp.bfloat16)
    grad_query = jnp.einsum(
        "whqk,wkhd->wqhd", score_half, keys_part, preferred_element_type=jnp.float32
    ).astype(jnp.bfloat16)
    grad_key = jnp.einsum(
        "whqk,wqhd->wkhd", score_half, queries, preferred_element_type=jnp.float32
    ).astype(jnp.bfloat16)
    shape_out = (window_count, win_tokens, model_dim)
    return jnp.concatenate(
        [grad_query.reshape(shape_out), grad_key.reshape(shape_out), grad_value.reshape(shape_out)],
        -1,
    )


def layer_region(shifted, keep_mask, grad_shift, owned_mask, w_qkv, w_out):
    row_count, col_count, model_dim = shifted.shape
    flat_in = shifted.reshape(-1, model_dim).astype(jnp.float32)
    centered = flat_in - jnp.mean(flat_in, -1, keepdims=True)
    inv_sigma = lax.rsqrt(jnp.mean(centered * centered, -1, keepdims=True) + epsilon)
    normed = centered * inv_sigma
    hidden = normed.astype(jnp.bfloat16)
    qkv = jnp.dot(hidden, w_qkv, preferred_element_type=jnp.float32).astype(jnp.bfloat16)
    qkv_win = windows(qkv.reshape(row_count, col_count, -1))
    keep_win = windows(keep_mask[..., None])[..., 0]
    mixed_out, attn_probs = attend(qkv_win, keep_win)
    mixed_flat = unwindows(mixed_out, row_count, col_count).reshape(-1, model_dim)
    output = jnp.dot(mixed_flat, w_out, preferred_element_type=jnp.float32).astype(jnp.bfloat16)
    grad_flat = grad_shift.reshape(-1, model_dim)
    grad_mixed = jnp.dot(grad_flat, w_out.T, preferred_element_type=jnp.float32).astype(
        jnp.bfloat16
    )
    grad_qkv = attend_back(
        qkv_win, attn_probs, windows(grad_mixed.reshape(row_count, col_count, model_dim))
    )
    grad_qkv = unwindows(grad_qkv, row_count, col_count).reshape(-1, 3 * model_dim)
    own_column = owned_mask.reshape(-1, 1).astype(jnp.bfloat16)
    contract = (((0,), (0,)), ((), ()))
    grad_wout = lax.dot_general(
        mixed_flat * own_column, grad_flat, contract, preferred_element_type=jnp.float32
    )
    grad_wqkv = lax.dot_general(
        hidden * own_column, grad_qkv, contract, preferred_element_type=jnp.float32
    )
    grad_hidden = jnp.dot(grad_qkv, w_qkv.T, preferred_element_type=jnp.float32)
    grad_shifted = inv_sigma * (
        grad_hidden
        - jnp.mean(grad_hidden, -1, keepdims=True)
        - normed * jnp.mean(grad_hidden * normed, -1, keepdims=True)
    )
    shape_out = (row_count, col_count, model_dim)
    return (
        output.reshape(shape_out),
        grad_shifted.astype(jnp.bfloat16).reshape(shape_out),
        grad_wqkv,
        grad_wout,
    )


def local(slide_tokens, tissue, grad_tokens, w_qkv, w_out):
    row_count, col_count, model_dim = slide_tokens.shape
    keep_mask = tissue.astype(jnp.bfloat16)
    from_below = shifted_2((slide_tokens[:SHIFT], keep_mask[:SHIFT], grad_tokens[:SHIFT]), "gy", -1)
    tall_x = jnp.concatenate([slide_tokens[SHIFT:], from_below[0]], 0)
    tall_k = jnp.concatenate([keep_mask[SHIFT:], from_below[1]], 0)
    tall_g = jnp.concatenate([grad_tokens[SHIFT:], from_below[2]], 0)
    from_right = shifted_2((tall_x[:, :SHIFT], tall_k[:, :SHIFT], tall_g[:, :SHIFT]), "gx", -1)
    shifted_x = jnp.concatenate([tall_x[:, SHIFT:], from_right[0]], 1)
    shifted_k = jnp.concatenate([tall_k[:, SHIFT:], from_right[1]], 1)
    shifted_g = jnp.concatenate([tall_g[:, SHIFT:], from_right[2]], 1)
    owned_mask = jnp.ones((row_count, col_count), jnp.float32)
    attn_shift, grad_shift, part_qkv, part_out = layer_region(
        shifted_x, shifted_k, shifted_g, owned_mask, w_qkv, w_out
    )
    edge = col_count - SHIFT
    from_left = shifted_2((attn_shift[:, edge:], grad_shift[:, edge:]), "gx", 1)
    wide_attn = jnp.concatenate([from_left[0], attn_shift[:, :edge]], 1)
    wide_grad = jnp.concatenate([from_left[1], grad_shift[:, :edge]], 1)
    bottom = row_count - SHIFT
    from_above = shifted_2((wide_attn[bottom:], wide_grad[bottom:]), "gy", 1)
    attn_tile = jnp.concatenate([from_above[0], wide_attn[:bottom]], 0)
    grad_tile = jnp.concatenate([from_above[1], wide_grad[:bottom]], 0)
    grad_wqkv, grad_wout = lax.psum((part_qkv, part_out), ("gx", "gy"))
    block_out = (slide_tokens.astype(jnp.float32) + attn_tile.astype(jnp.float32)).astype(
        jnp.bfloat16
    )
    grad_in = (grad_tokens.astype(jnp.float32) + grad_tile.astype(jnp.float32)).astype(jnp.bfloat16)
    return (block_out, grad_in, grad_wqkv, grad_wout)


def solution(mesh):
    placed = (P("gy", "gx", None), P("gy", "gx"), P("gy", "gx", None), P(), P())
    return jax.shard_map(
        local,
        mesh=mesh,
        in_specs=placed,
        out_specs=(P("gy", "gx", None), P("gy", "gx", None), P(), P()),
        check_vma=False,
    )
```

profile of v0, /device:TPU:0, one launch (start us, length us, event | category | flops | bytes accessed | tf_op | source)
XLA Modules:
  0.0 433.2 jit_solution(9250790033228147858)
XLA Ops:
  8.1 4.2 collective-permute-start.2
  21.4 4.7 %collective-permute-start.3 = (bf16[16,4]{1,0:T(8,128)(2,1)S(1)}, bf16[16,4]{1,0:T(8,128)(2,1)S(1)}, u32[]{:S(2)}, u32[]{:S(2)}) collective-permute-start(bf16[16,4]{1,0:T(8,128)(2,1)S(1)} %pad_maximum_fusion.8), channel_id=1, source_target_pairs={{8,0},{16,8},{24,16},{32,24},{40,32},{48,40},{56,48},{64,56},{72,6... | collective-permute-start | bytes 392 | tf_op jit(solution)/shard_map/ppermute | solution.py:19
  34.4 4.4 %collective-permute-start.1 = (bf16[16,4,768]{2,1,0:T(4,128)(2,1)S(1)}, bf16[16,4,768]{2,1,0:T(4,128)(2,1)S(1)}, u32[]{:S(2)}, u32[]{:S(2)}) collective-permute-start(bf16[16,4,768]{2,1,0:T(4,128)(2,1)S(1)} %pad_maximum_fusion.7), channel_id=1, source_target_pairs={{8,0},{16,8},{24,16},{32,24},{40,32},{48,40},{56,48},{64,56},{72,6... | collective-permute-start | bytes 294920 | tf_op jit(solution)/shard_map/ppermute | solution.py:19
  55.9 4.5 %convolution_convert_fusion = bf16[1024,2304]{1,0:T(8,128)(2,1)S(1)} fusion(bf16[1024,768]{1,0:T(8,128)(2,1)S(1)} %fusion.20, bf16[768,2304]{1,0:T(8,128)(2,1)S(1)} %copy-done), kind=kOutput, calls=%fused_computation.12 | convolution fusion | flops 3626237952 | bytes 9830400 | tf_op jit(solution)/shard_map/dot_general | solution.py:101
  63.2 4.1 copy.18
  67.3 4.2 copy.17
  71.5 4.2 copy.15
  75.7 8.2 %reshape_reshape.22 = bf16[16,64,24,32]{3,2,1,0:T(8,128)(2,1)} reshape(bf16[2,8,8,8,768]{4,3,2,1,0:T(8,128)(2,1)} %bitcast.88) | data formatting | bytes 3145728 | tf_op jit(solution)/shard_map/reshape;reshape | solution.py:35
  83.9 7.0 %copy.23 = bf16[16,64,24,32]{1,3,2,0:T(8,128)(2,1)} copy(bf16[16,64,24,32]{3,2,1,0:T(8,128)(2,1)} %reshape_reshape.22) | data formatting | bytes 3145728 | tf_op jit(solution)/shard_map/reshape;reshape | solution.py:35
  91.0 9.2 %fusion.42 = f32[16,24,64,64]{2,3,1,0:T(8,128)} fusion(bf16[16,64,24,32]{1,3,2,0:T(8,128)(2,1)} %copy.23, bf16[16,64,24,32]{1,3,2,0:T(8,128)(2,1)} %bitcast.83), kind=kOutput, calls=%fused_computation.69 | convolution fusion | flops 100663296 | bytes 9437184 | tf_op jit(solution)/shard_map/wqhd,wkhd->whqk/dot_general | solution.py:70
  100.2 10.5 %fusion.41 = (f32[16,24,64]{2,1,0:T(8,128)}, f32[16,24,64,64]{2,3,1,0:T(8,128)}) fusion(pred[16,64,64]{1,2,0:T(8,128)(4,1)} %broadcast_or_fusion, bf16[16,64,24,32]{1,3,2,0:T(8,128)(2,1)} %bitcast.95, bf16[16,64,24,32]{1,3,2,0:T(8,128)(2,1)} %bitcast.93), kind=kOutput, calls=%fused_computation.68 | convolution fusion | flops 106954816 | bytes 9601024 | tf_op jit(solution)/shard_map/sub | solution.py:53
  110.6 19.8 %convert_bitcast_fusion.2 = bf16[16,64,24,32]{1,3,2,0:T(8,128)(2,1)} fusion(bf16[16,64,24,32]{1,3,2,0:T(8,128)(2,1)} %bitcast.94, f32[16,24,64,64]{2,3,1,0:T(8,128)} %fusion.42, f32[16,24,64,64]{2,3,1,0:T(8,128)} %get-tuple-element.12, f32[16,24,64]{2,1,0:T(8,128)} %get-tuple-element.11), kind=kOutput, calls=%fused_computation.24 | convolution fusion | flops 112484416 | bytes 15826944 | tf_op jit(solution)/shard_map/whqk,wkhd->wqhd/dot_general | solution.py:81
  130.4 20.0 %convert_bitcast_fusion.1 = bf16[16,64,24,32]{1,3,2,0:T(8,128)(2,1)} fusion(bf16[16,64,24,32]{1,3,2,0:T(8,128)(2,1)} %bitcast.96, f32[16,24,64,64]{2,3,1,0:T(8,128)} %fusion.42, f32[16,24,64,64]{2,3,1,0:T(8,128)} %get-tuple-element.12, f32[16,24,64]{2,1,0:T(8,128)} %get-tuple-element.11), kind=kOutput, calls=%fused_computation.23 | convolution fusion | flops 112484416 | bytes 15826944 | tf_op jit(solution)/shard_map/whqk,wqhd->wkhd/dot_general | solution.py:84
  150.5 10.7 %convert_bitcast_fusion = bf16[16,64,24,32]{1,3,2,0:T(8,128)(2,1)} fusion(bf16[16,64,24,32]{1,3,2,0:T(8,128)(2,1)} %copy.23, f32[16,24,64,64]{2,3,1,0:T(8,128)} %get-tuple-element.12, f32[16,24,64]{2,1,0:T(8,128)} %get-tuple-element.11), kind=kOutput, calls=%fused_computation.22 | convolution fusion | flops 104595456 | bytes 9535488 | tf_op jit(solution)/shard_map/whqk,wqhd->wkhd/dot_general | solution.py:74
  161.2 8.1 %convert_bitcast_fusion.3 = bf16[16,64,24,32]{1,3,2,0:T(8,128)(2,1)} fusion(bf16[16,64,24,32]{1,3,2,0:T(8,128)(2,1)S(1)} %bitcast.84, f32[16,24,64,64]{2,3,1,0:T(8,128)} %get-tuple-element.12, f32[16,24,64]{2,1,0:T(8,128)S(1)} %copy-done.26), kind=kOutput, calls=%fused_computation.26 | convolution fusion | flops 104595456 | bytes 9535488 | tf_op jit(solution)/shard_map/whqk,wkhd->wqhd/dot_general | solution.py:56
  169.4 6.9 %copy.20 = bf16[16,64,24,32]{3,2,1,0:T(8,128)(2,1)} copy(bf16[16,64,24,32]{1,3,2,0:T(8,128)(2,1)} %convert_bitcast_fusion.3) | data formatting | bytes 3145728 | tf_op jit(solution)/shard_map/convert_element_type | solution.py:58
  176.3 8.2 %reshape_reshape.19 = bf16[2,8,8,8,768]{4,3,2,1,0:T(8,128)(2,1)} reshape(bf16[16,64,24,32]{3,2,1,0:T(8,128)(2,1)} %copy.20) | data formatting | bytes 3145728 | tf_op jit(solution)/shard_map/reshape;reshape | solution.py:30
  190.2 6.9 %copy.30 = bf16[16,64,24,32]{3,2,1,0:T(8,128)(2,1)} copy(bf16[16,64,24,32]{1,3,2,0:T(8,128)(2,1)} %convert_bitcast_fusion) | data formatting | bytes 3145728 | tf_op jit(solution)/shard_map/convert_element_type | solution.py:76
  197.1 8.2 %concatenate.50 = bf16[2,8,8,8,768]{4,3,2,1,0:T(8,128)(2,1)} reshape(bf16[16,64,24,32]{3,2,1,0:T(8,128)(2,1)} %copy.30) | data formatting | bytes 3145728 | tf_op jit(solution)/shard_map/concatenate | solution.py:88
  205.3 6.9 %copy.27 = bf16[16,64,24,32]{3,2,1,0:T(8,128)(2,1)} copy(bf16[16,64,24,32]{1,3,2,0:T(8,128)(2,1)} %convert_bitcast_fusion.1) | data formatting | bytes 3145728 | tf_op jit(solution)/shard_map/convert_element_type | solution.py:86
  212.2 8.2 %concatenate.49 = bf16[2,8,8,8,768]{4,3,2,1,0:T(8,128)(2,1)} reshape(bf16[16,64,24,32]{3,2,1,0:T(8,128)(2,1)} %copy.27) | data formatting | bytes 3145728 | tf_op jit(solution)/shard_map/concatenate | solution.py:88
  220.4 6.9 %copy.25 = bf16[16,64,24,32]{3,2,1,0:T(8,128)(2,1)} copy(bf16[16,64,24,32]{1,3,2,0:T(8,128)(2,1)} %convert_bitcast_fusion.2) | data formatting | bytes 3145728 | tf_op jit(solution)/shard_map/convert_element_type | solution.py:83
  227.4 8.2 %concatenate.48 = bf16[2,8,8,8,768]{4,3,2,1,0:T(8,128)(2,1)} reshape(bf16[16,64,24,32]{3,2,1,0:T(8,128)(2,1)} %copy.25) | data formatting | bytes 3145728 | tf_op jit(solution)/shard_map/concatenate | solution.py:88
  241.7 6.2 %fusion.43 = f32[768,2304]{1,0:T(8,128)} fusion(bf16[1024,768]{1,0:T(8,128)(2,1)S(1)} %bitcast.101, bf16[1024,2304]{1,0:T(8,128)(2,1)S(1)} %bitcast.90), kind=kOutput, calls=%fused_computation.70 | convolution fusion | flops 3623878656 | bytes 13369344 | tf_op jit(solution)/shard_map/dot_general | solution.py:120
  247.9 3.3 convolution_convert_fusion.2
  251.6 4.1 fusion.39
  255.7 4.3 collective-permute-done.4
  261.4 8.6 %collective-permute-done.8 = bf16[16,4,768]{2,1,0:T(4,128)(2,1)S(1)} collective-permute-done((bf16[16,4,768]{2,1,0:T(4,128)(2,1)S(1)}, bf16[16,4,768]{2,1,0:T(4,128)(2,1)S(1)}, u32[]{:S(2)}, u32[]{:S(2)}) %collective-permute-start.8) | collective-permute-done | bytes 98336 | tf_op jit(solution)/shard_map/ppermute | solution.py:19
  270.2 7.0 %collective-permute-done.5 = bf16[4,64,768]{2,1,0:T(8,128)(2,1)S(1)} collective-permute-done((bf16[4,64,768]{2,1,0:T(8,128)(2,1)S(1)}, bf16[4,64,768]{2,1,0:T(8,128)(2,1)S(1)}, u32[]{:S(2)}, u32[]{:S(2)}) %collective-permute-start.5) | collective-permute-done | bytes 393248 | tf_op jit(solution)/shard_map/ppermute | solution.py:19
  279.1 6.5 %collective-permute-done.9 = bf16[4,64,768]{2,1,0:T(8,128)(2,1)S(1)} collective-permute-done((bf16[4,64,768]{2,1,0:T(8,128)(2,1)S(1)}, bf16[4,64,768]{2,1,0:T(8,128)(2,1)S(1)}, u32[]{:S(2)}, u32[]{:S(2)}) %collective-permute-start.9) | collective-permute-done | bytes 393248 | tf_op jit(solution)/shard_map/ppermute | solution.py:19
  287.5 130.6 %all-reduce.3.cloned.1.call-done = (f32[768,2304]{1,0:T(8,128)}, f32[768,768]{1,0:T(8,128)}) async-done(((f32[768,2304]{1,0:T(8,128)}, f32[768,768]{1,0:T(8,128)}), (f32[768,2304]{1,0:T(8,128)}, f32[768,768]{1,0:T(8,128)})) %all-reduce.3.cloned.1.call-update) | async-done | bytes 9437200 | tf_op jit(solution)/shard_map/psum | solution.py:161
  418.1 6.6 %copy.42 = f32[768,2304]{1,0:T(8,128)} copy(f32[768,2304]{1,0:T(8,128)} %get-tuple-element.18) | data formatting | bytes 14155776
  (114 shorter events, 56.8 us)
Async XLA Ops:
  7.2 48.7 %copy-start = (bf16[768,2304]{1,0:T(8,128)(2,1)S(1)}, bf16[768,2304]{1,0:T(8,128)(2,1)}, u32[]{:S(2)}) copy-start(bf16[768,2304]{1,0:T(8,128)(2,1)} %param.8) | copy-start | bytes 10616836
  7.2 410.9 %all-reduce.3.cloned.1.call-start = ((), (), s32[]{:S(2)}) async-start(), calls=%async_computation | async-start | bytes 18874368 | tf_op jit(solution)/shard_map/psum | solution.py:161
  7.2 13.0 %copy-start.9 = (bf16[16,64,768]{2,1,0:T(8,128)(2,1)S(1)}, bf16[16,64,768]{2,1,0:T(8,128)(2,1)}, u32[]{:S(2)}) copy-start(bf16[16,64,768]{2,1,0:T(8,128)(2,1)} %param.7) | copy-start | bytes 4718596
  8.1 13.2 %collective-permute-start.2 = (bf16[4,64]{1,0:T(4,128)(2,1)S(1)}, bf16[4,64]{1,0:T(4,128)(2,1)S(1)}, u32[]{:S(2)}, u32[]{:S(2)}) collective-permute-start(bf16[4,64]{1,0:T(4,128)(2,1)S(1)} %slice.99), channel_id=1, source_target_pairs={{1,0},{2,1},{3,2},{4,3},{5,4},{6,5},{7,6},{0,7},{9,8},{10,9},{11,1... | collective-permute-start | bytes 1544 | tf_op jit(solution)/shard_map/ppermute | solution.py:19
  14.1 24.6 %collective-permute-start.6 = (bf16[4,64,768]{2,1,0:T(8,128)(2,1)}, bf16[4,64,768]{2,1,0:T(8,128)(2,1)}, u32[]{:S(2)}, u32[]{:S(2)}) collective-permute-start(bf16[4,64,768]{2,1,0:T(8,128)(2,1)} %slice.88), channel_id=1, source_target_pairs={{1,0},{2,1},{3,2},{4,3},{5,4},{6,5},{7,6},{0,7},{9,8},{10,9},{11,1... | collective-permute-start | bytes 1179656 | tf_op jit(solution)/shard_map/ppermute | solution.py:19
  16.7 16.7 %collective-permute-start = (bf16[4,64,768]{2,1,0:T(8,128)(2,1)}, bf16[4,64,768]{2,1,0:T(8,128)(2,1)}, u32[]{:S(2)}, u32[]{:S(2)}) collective-permute-start(bf16[4,64,768]{2,1,0:T(8,128)(2,1)} %slice.73), channel_id=1, source_target_pairs={{1,0},{2,1},{3,2},{4,3},{5,4},{6,5},{7,6},{0,7},{9,8},{10,9},{11,1... | collective-permute-start | bytes 1179656 | tf_op jit(solution)/shard_map/ppermute | solution.py:19
  21.4 6.1 %collective-permute-start.3 = (bf16[16,4]{1,0:T(8,128)(2,1)S(1)}, bf16[16,4]{1,0:T(8,128)(2,1)S(1)}, u32[]{:S(2)}, u32[]{:S(2)}) collective-permute-start(bf16[16,4]{1,0:T(8,128)(2,1)S(1)} %pad_maximum_fusion.8), channel_id=1, source_target_pairs={{8,0},{16,8},{24,16},{32,24},{40,32},{48,40},{56,48},{64,56},{72,6... | collective-permute-start | bytes 392 | tf_op jit(solution)/shard_map/ppermute | solution.py:19
  30.3 11.9 %copy-start.7 = (bf16[12,64,768]{2,1,0:T(8,128)(2,1)S(1)}, bf16[12,64,768]{2,1,0:T(8,128)(2,1)}, u32[]{:S(2)}) copy-start(bf16[12,64,768]{2,1,0:T(8,128)(2,1)} %slice.72) | copy-start | bytes 3538948
  31.9 11.6 %copy-start.6 = (bf16[12,64,768]{2,1,0:T(8,128)(2,1)S(1)}, bf16[12,64,768]{2,1,0:T(8,128)(2,1)}, u32[]{:S(2)}) copy-start(bf16[12,64,768]{2,1,0:T(8,128)(2,1)} %slice.87) | copy-start | bytes 3538948
  34.4 12.1 %collective-permute-start.1 = (bf16[16,4,768]{2,1,0:T(4,128)(2,1)S(1)}, bf16[16,4,768]{2,1,0:T(4,128)(2,1)S(1)}, u32[]{:S(2)}, u32[]{:S(2)}) collective-permute-start(bf16[16,4,768]{2,1,0:T(4,128)(2,1)S(1)} %pad_maximum_fusion.7), channel_id=1, source_target_pairs={{8,0},{16,8},{24,16},{32,24},{40,32},{48,40},{56,48},{64,56},{72,6... | collective-permute-start | bytes 294920 | tf_op jit(solution)/shard_map/ppermute | solution.py:19
  40.3 8.8 %collective-permute-start.7 = (bf16[16,4,768]{2,1,0:T(4,128)(2,1)}, bf16[16,4,768]{2,1,0:T(4,128)(2,1)}, u32[]{:S(2)}, u32[]{:S(2)}) collective-permute-start(bf16[16,4,768]{2,1,0:T(4,128)(2,1)} %pad_maximum_fusion.6), channel_id=1, source_target_pairs={{8,0},{16,8},{24,16},{32,24},{40,32},{48,40},{56,48},{64,56},{72,6... | collective-permute-start | bytes 294920 | tf_op jit(solution)/shard_map/ppermute | solution.py:19
  43.6 4.1 copy-start.1
  49.1 2.9 copy-start.25
  53.4 2.0 copy-start.2
  53.4 2.0 copy-start.14
  53.4 2.0 copy-start.21
  150.5 10.8 %copy-start.5 = (bf16[16,64,768]{1,2,0:T(8,128)(2,1)S(1)}, bf16[16,64,768]{1,2,0:T(8,128)(2,1)}, u32[]{:S(2)}) copy-start(bf16[16,64,768]{1,2,0:T(8,128)(2,1)} %copy.15) | copy-start | bytes 4718596
  150.5 10.8 %copy-start.26 = (f32[16,24,64]{2,1,0:T(8,128)S(1)}, f32[16,24,64]{2,1,0:T(8,128)}, u32[]{:S(2)}) copy-start(f32[16,24,64]{2,1,0:T(8,128)} %get-tuple-element.11) | copy-start | bytes 294916
  184.5 2.8 copy-start.19
  239.5 2.2 copy-start.11
  247.9 3.5 copy-start.4
  247.9 3.6 copy-start.12
  247.9 3.6 copy-start.16
  247.9 3.6 copy-start.22
  247.9 3.6 copy-start.24
  251.3 8.7 %collective-permute-start.4 = (bf16[16,4,768]{2,1,0:T(4,128)(2,1)S(1)}, bf16[16,4,768]{2,1,0:T(4,128)(2,1)S(1)}, u32[]{:S(2)}, u32[]{:S(2)}) collective-permute-start(bf16[16,4,768]{2,1,0:T(4,128)(2,1)S(1)} %slice.104), channel_id=1, source_target_pairs={{120,0},{0,8},{8,16},{16,24},{24,32},{32,40},{40,48},{48,56},{56,6... | collective-permute-start | bytes 294920 | tf_op jit(solution)/shard_map/ppermute | solution.py:19
  260.1 17.2 %collective-permute-start.5 = (bf16[4,64,768]{2,1,0:T(8,128)(2,1)S(1)}, bf16[4,64,768]{2,1,0:T(8,128)(2,1)S(1)}, u32[]{:S(2)}, u32[]{:S(2)}) collective-permute-start(bf16[4,64,768]{2,1,0:T(8,128)(2,1)S(1)} %pad_maximum_fusion.5), channel_id=1, source_target_pairs={{7,0},{0,1},{1,2},{2,3},{3,4},{4,5},{5,6},{6,7},{15,8},{8,9},{9,10... | collective-permute-start | bytes 1179656 | tf_op jit(solution)/shard_map/ppermute | solution.py:19
  260.2 17.1 %copy-start.8 = (bf16[16,64,768]{2,1,0:T(8,128)(2,1)S(1)}, bf16[16,64,768]{2,1,0:T(8,128)(2,1)}, u32[]{:S(2)}) copy-start(bf16[16,64,768]{2,1,0:T(8,128)(2,1)} %param.5) | copy-start | bytes 4718596
  261.4 8.7 %collective-permute-start.8 = (bf16[16,4,768]{2,1,0:T(4,128)(2,1)S(1)}, bf16[16,4,768]{2,1,0:T(4,128)(2,1)S(1)}, u32[]{:S(2)}, u32[]{:S(2)}) collective-permute-start(bf16[16,4,768]{2,1,0:T(4,128)(2,1)S(1)} %slice.108), channel_id=1, source_target_pairs={{120,0},{0,8},{8,16},{16,24},{24,32},{32,40},{40,48},{48,56},{56,6... | collective-permute-start | bytes 294920 | tf_op jit(solution)/shard_map/ppermute | solution.py:19
  270.0 15.6 %copy-start.10 = (bf16[16,64,768]{2,1,0:T(8,128)(2,1)S(1)}, bf16[16,64,768]{2,1,0:T(8,128)(2,1)}, u32[]{:S(2)}) copy-start(bf16[16,64,768]{2,1,0:T(8,128)(2,1)} %param.7) | copy-start | bytes 4718596
  270.1 15.5 %collective-permute-start.9 = (bf16[4,64,768]{2,1,0:T(8,128)(2,1)S(1)}, bf16[4,64,768]{2,1,0:T(8,128)(2,1)S(1)}, u32[]{:S(2)}, u32[]{:S(2)}) collective-permute-start(bf16[4,64,768]{2,1,0:T(8,128)(2,1)S(1)} %pad_maximum_fusion.4), channel_id=1, source_target_pairs={{7,0},{0,1},{1,2},{2,3},{3,4},{4,5},{5,6},{6,7},{15,8},{8,9},{9,10... | collective-permute-start | bytes 1179656 | tf_op jit(solution)/shard_map/ppermute | solution.py:19
  418.1 6.6 %copy-start.17 = (f32[768,768]{1,0:T(8,128)S(1)}, f32[768,768]{1,0:T(8,128)}, u32[]{:S(2)}) copy-start(f32[768,768]{1,0:T(8,128)} %get-tuple-element.19) | copy-start | bytes 7077892
  (6 other events, 7.8 us)
Sparse Core Ops, SparseCore 0:
  248.0 170.0 all-reduce.2
where the time goes:
time: 441 us; the launch traced here: 433 us
  waiting for transfers between devices  160 us (36%)
  local copies, waits for them, and re-layouts  119 us (27%)
  matrix products  101 us (23%)
  other arithmetic  21.9 us (5%)
  starting transfers between devices  16.9 us (4%)
  between operations  14.7 us (3%)
    psum x1, waiting for transfers between devices, local(): grad_wqkv, grad_wout = lax.psum((part_qkv, part_out), ('gx', 'gy'))  131 us
    ppermute x10, waiting for transfers between devices, shifted_2(): return lax.ppermute(block, axis, route)  29.1 us
    concatenate x3, local copies, waits for them, and re-layouts, attend_back(): jnp.concatenate([grad_query.reshape(shape_out), grad_key.reshape(shape_ou...  24.6 us
    dot_general x1, matrix products, attend_back(): jnp.einsum('whqk,wqhd->wkhd', score_half, queries, preferred_element_type...  20 us
    dot_general x1, matrix products, attend_back(): jnp.einsum('whqk,wkhd->wqhd', score_half, keys_part, preferred_element_ty...  19.8 us
    ppermute x10, starting transfers between devices, shifted_2(): return lax.ppermute(block, axis, route)  16.9 us
    another operation x2, local copies, waits for them, and re-layouts, split_heads(): return tensor.reshape(tensor.shape[0], tensor.shape[1], HEADS, -1)  15.2 us
    unnamed x56, local copies, waits for them, and re-layouts  14.1 us
  transfers between devices with their start and end apart: 11, of which 7 were waited for; matrix products, arithmetic and copies ran while one was open for 8% of the time, Pallas kernels for 0%

commit v1 on v0

v1 whole, which is shorter than its diff:
```python
import functools
import math
import jax
import jax.numpy as jnp
from jax import lax
from jax.experimental import pallas as pl
from jax.experimental.pallas import tpu as pltpu
from jax.sharding import PartitionSpec as P

HEADS = 24
WIN = 8
SHIFT = 4
D = 768
GD = 256
EPS = 1e-05
SCALE = 1.0 / math.sqrt(32)
LOG2E = math.log2(math.e)
NT = (((1,), (1,)), ((), ()))
NN = (((1,), (0,)), ((), ()))
F32 = jnp.float32
BF16 = jnp.bfloat16


def mm(a, b, dims=NN):
    return lax.dot_general(a, b, dims, preferred_element_type=F32)


def spread(t, head_lane):
    zero = jnp.zeros_like(t)
    return jnp.concatenate([jnp.where(head_lane == h, t, zero) for h in range(4)], 0)


def gather_diag(full, head_lane):
    out = full[0:64]
    for h in range(1, 4):
        out = jnp.where(head_lane == h, full[64 * h : 64 * h + 64], out)
    return out


def attn_body(nwin, x_ref, g_ref, bias_ref, wq_ref, wk_ref, wv_ref, wo_ref,
              mixed_ref, dq_ref, dk_ref, dv_ref, part_ref,
              hid, hid_t, qs, ks, vs, gm, mix_t):
    tokens = nwin * 64
    tile = 256

    @pl.when(pl.program_id(0) == 0)
    def _():
        @pl.loop(0, tokens // 128)
        def _(i):
            rows = pl.ds(pl.multiple_of(i * 128, 128), 128)
            x = x_ref[rows, :].astype(F32)
            c = x - jnp.mean(x, -1, keepdims=True)
            inv = lax.rsqrt(jnp.mean(c * c, -1, keepdims=True) + EPS)
            n = c * inv
            hid[rows, :] = n.astype(BF16)
            hid_t[:, rows] = jnp.transpose(n).astype(BF16)

    @pl.loop(0, tokens // tile)
    def _(i):
        rows = pl.ds(pl.multiple_of(i * tile, tile), tile)
        h = hid[rows, :]
        qs[rows, :] = mm(h, wq_ref[...]).astype(BF16)
        ks[rows, :] = mm(h, wk_ref[...]).astype(BF16)
        vs[rows, :] = mm(h, wv_ref[...]).astype(BF16)
        gm[rows, :] = mm(g_ref[rows, :], wo_ref[...], NT).astype(BF16)

    head_lane = lax.broadcasted_iota(jnp.int32, (64, 128), 1) // 32

    def chain(rows, lanes, bias):
        q, k, v, g = qs[rows, lanes], ks[rows, lanes], vs[rows, lanes], gm[rows, lanes]
        qb = spread(q, head_lane)
        gb = spread(g, head_lane)
        s = mm(k, qb, NT) * (SCALE * LOG2E) + bias
        e = jnp.exp2(s - jnp.max(s, 0, keepdims=True))
        p = e * (1.0 / jnp.sum(e, 0, keepdims=True))
        pb = p.astype(BF16)
        dp = mm(v, gb, NT)
        ds = p * ((dp - jnp.sum(dp * p, 0, keepdims=True)) * SCALE)
        db = ds.astype(BF16)
        dk_ref[rows, lanes] = mm(db, qb).astype(BF16)
        dv_ref[rows, lanes] = mm(pb, gb).astype(BF16)
        mixed_ref[rows, lanes] = gather_diag(mm(jnp.transpose(p).astype(BF16), v), head_lane).astype(BF16)
        dq_ref[rows, lanes] = gather_diag(mm(jnp.transpose(ds).astype(BF16), k), head_lane).astype(BF16)

    @pl.loop(0, nwin)
    def _(w):
        rows = pl.ds(pl.multiple_of(w * 64, 64), 64)
        b = bias_ref[rows, :]
        b = jnp.concatenate([b, b], 1)
        for s in range(GD // 128):
            chain(rows, slice(128 * s, 128 * s + 128), b)

    @pl.loop(0, tokens // 128)
    def _(i):
        rows = pl.ds(pl.multiple_of(i * 128, 128), 128)
        mix_t[:, rows] = jnp.transpose(mixed_ref[rows, :].astype(F32)).astype(BF16)

    @pl.loop(0, D // tile)
    def _(i):
        rows = pl.ds(pl.multiple_of(i * tile, tile), tile)
        h = hid_t[rows, :]
        part_ref[0, rows, 0:256] = mm(h, dq_ref[...]).astype(BF16)
        part_ref[0, rows, 256:512] = mm(h, dk_ref[...]).astype(BF16)
        part_ref[0, rows, 512:768] = mm(h, dv_ref[...]).astype(BF16)

    for j in range(3):
        cols = slice(256 * j, 256 * j + 256)
        part_ref[0, 768:1024, cols] = mm(mix_t[...], g_ref[:, cols]).astype(BF16)


def attn_call(x, g, bias, w_qkv, w_out):
    tokens = x.shape[0]
    nwin = tokens // 64
    whole = lambda i: (0, 0)
    cols = pl.BlockSpec((tokens, GD), lambda i: (0, i))
    wblock = lambda p: pl.BlockSpec((D, GD), lambda i: (0, 3 * p + i))
    tok = jax.ShapeDtypeStruct((tokens, D), BF16)
    return pl.pallas_call(
        functools.partial(attn_body, nwin),
        grid=(3,),
        in_specs=[
            pl.BlockSpec((tokens, D), whole),
            pl.BlockSpec((tokens, D), whole),
            pl.BlockSpec((tokens, 128), whole),
            wblock(0), wblock(1), wblock(2),
            pl.BlockSpec((GD, D), lambda i: (i, 0)),
        ],
        out_specs=[cols, cols, cols, cols, pl.BlockSpec((1, 1024, D), lambda i: (i, 0, 0))],
        out_shape=[tok, tok, tok, tok, jax.ShapeDtypeStruct((3, 1024, D), BF16)],
        scratch_shapes=[
            pltpu.VMEM((tokens, D), BF16),
            pltpu.VMEM((D, tokens), BF16),
            pltpu.VMEM((tokens, GD), BF16),
            pltpu.VMEM((tokens, GD), BF16),
            pltpu.VMEM((tokens, GD), BF16),
            pltpu.VMEM((tokens, GD), BF16),
            pltpu.VMEM((GD, tokens), BF16),
        ],
        compiler_params=pltpu.CompilerParams(
            dimension_semantics=("arbitrary",), vmem_limit_bytes=48 << 20
        ),
        cost_estimate=pl.CostEstimate(
            flops=14_000_000_000, bytes_accessed=20_000_000, transcendentals=1_600_000
        ),
        name="attention",
    )(x, g, bias, w_qkv, w_qkv, w_qkv, w_out)


def finish_body(x_ref, mixed_ref, dq_ref, dk_ref, dv_ref, wqkv_ref, wo_ref, attn_ref, gs_ref):
    attn_ref[...] = mm(mixed_ref[...], wo_ref[...]).astype(BF16)
    dh = mm(dq_ref[...], wqkv_ref[:, 0:768], NT)
    dh += mm(dk_ref[...], wqkv_ref[:, 768:1536], NT)
    dh += mm(dv_ref[...], wqkv_ref[:, 1536:2304], NT)
    x = x_ref[...].astype(F32)
    c = x - jnp.mean(x, -1, keepdims=True)
    inv = lax.rsqrt(jnp.mean(c * c, -1, keepdims=True) + EPS)
    n = c * inv
    back = dh - jnp.mean(dh, -1, keepdims=True) - n * jnp.mean(dh * n, -1, keepdims=True)
    gs_ref[...] = (inv * back).astype(BF16)


def finish_call(x, mixed, dq, dk, dv, w_qkv, w_out):
    tokens = x.shape[0]
    tile = 128
    t = pl.BlockSpec((tile, D), lambda i: (i, 0))
    tok = jax.ShapeDtypeStruct((tokens, D), BF16)
    return pl.pallas_call(
        finish_body,
        grid=(tokens // tile,),
        in_specs=[t, t, t, t, t,
                  pl.BlockSpec((D, 3 * D), lambda i: (0, 0), pipeline_mode=pl.Buffered(1)),
                  pl.BlockSpec((D, D), lambda i: (0, 0), pipeline_mode=pl.Buffered(1))],
        out_specs=[t, t],
        out_shape=[tok, tok],
        compiler_params=pltpu.CompilerParams(
            dimension_semantics=("arbitrary",), vmem_limit_bytes=32 << 20
        ),
        cost_estimate=pl.CostEstimate(
            flops=4_800_000_000, bytes_accessed=16_000_000, transcendentals=0
        ),
        name="finish",
    )(x, mixed, dq, dk, dv, w_qkv, w_out)


AXES = ("gx", "gy")


def place(i):
    gx, gy = divmod(i, 8)
    z_hi, y, core = gx // 8, gx // 2 % 4, gx % 2
    z_lo, x = divmod(gy, 4)
    return {"core": core, "x": x, "y": y, "z": 2 * z_hi + z_lo}


def number(d):
    z_hi, z_lo = divmod(d["z"], 2)
    return ((z_hi * 4 + d["y"]) * 2 + d["core"]) * 8 + z_lo * 4 + d["x"]


def exchange(v, axis, first):
    pairs = []
    for i in range(128):
        d = place(i)
        if axis == "core":
            d["core"] ^= 1
        elif (d["core"] == 0) == first:
            d[axis] ^= 1
        else:
            d[axis] = 3 - d[axis]
        pairs.append((i, number(d)))
    return lax.ppermute(v, AXES, pairs)


def half_of(axis, first):
    gx, gy = lax.axis_index("gx"), lax.axis_index("gy")
    core = gx % 2
    if axis == "core":
        return core
    p = {"x": gy % 4, "y": gx // 2 % 4, "z": gx // 8 * 2 + gy // 4}[axis]
    inner = ((p == 1) | (p == 2)).astype(jnp.int32)
    upper = (p >= 2).astype(jnp.int32)
    return jnp.where((core == 0) == first, inner, upper)


def add(a, b):
    return (a.astype(F32) + b.astype(F32)).astype(BF16)


def scatter_half(v, axis, first=True):
    n = v.shape[0] // 2
    b = half_of(axis, first)
    keep = lax.dynamic_slice_in_dim(v, b * n, n, 0)
    send = lax.dynamic_slice_in_dim(v, (1 - b) * n, n, 0)
    return add(keep, exchange(send, axis, first))


def gather_half(v, axis, first=True):
    b = half_of(axis, first)
    o = exchange(v, axis, first)
    return jnp.where(b == 0, jnp.concatenate([v, o], 0), jnp.concatenate([o, v], 0))


def total(parts):
    order = [["core"] + ["xyz"[(k + s) % 3] for s in range(3)] for k in range(3)]
    for s in range(4):
        parts = [scatter_half(p, o[s]) for p, o in zip(parts, order)]
    n = parts[0].shape[0]
    v = jnp.concatenate(parts, 0)
    v = scatter_half(v, "x", False)
    for axis in "yz":
        v = add(v, exchange(v, axis, False))
    v = gather_half(v, "x", False)
    parts = [v[n * k : n * k + n] for k in range(3)]
    for s in (3, 2, 1, 0):
        parts = [gather_half(p, o[s]) for p, o in zip(parts, order)]
    return parts


def neighbour(block, axis, distance):
    n = lax.axis_size(axis)
    return lax.ppermute(block, axis, [((i - distance) % n, i) for i in range(n)])


def windows(t):
    r, c, f = t.shape
    t = t.reshape(r // WIN, WIN, c // WIN, WIN, f)
    return t.transpose(0, 2, 1, 3, 4).reshape(r * c, f)


def unwindows(t, r, c):
    t = t.reshape(r // WIN, c // WIN, WIN, WIN, t.shape[-1])
    return t.transpose(0, 2, 1, 3, 4).reshape(r, c, t.shape[-1])


def local(slide_tokens, tissue, grad_tokens, w_qkv, w_out):
    rows, cols, _ = slide_tokens.shape
    keep = tissue.astype(BF16)
    xg = jnp.stack([slide_tokens, grad_tokens])
    below = neighbour(xg[:, :SHIFT], "gy", -1)
    below_k = neighbour(keep[:SHIFT], "gy", -1)
    xg = jnp.concatenate([xg[:, SHIFT:], below], 1)
    keep = jnp.concatenate([keep[SHIFT:], below_k], 0)
    right = neighbour(xg[:, :, :SHIFT], "gx", -1)
    right_k = neighbour(keep[:, :SHIFT], "gx", -1)
    xg = jnp.concatenate([xg[:, :, SHIFT:], right], 2)
    keep = jnp.concatenate([keep[:, SHIFT:], right_k], 1)

    x, g = windows(xg[0]), windows(xg[1])
    keep = windows(keep[..., None]).reshape(-1, 64, 1)
    lane = lax.broadcasted_iota(jnp.int32, (1, 64, 128), 2) % 64
    row = lax.broadcasted_iota(jnp.int32, (1, 64, 128), 1)
    bias = jnp.where((keep > 0.5) | (lane == row), 0.0, -1e30).astype(F32).reshape(-1, 128)
    mixed, dq, dk, dv, part = attn_call(x, g, bias, w_qkv, w_out)
    attn, grad = finish_call(x, mixed, dq, dk, dv, w_qkv, w_out)

    back = jnp.stack([unwindows(attn, rows, cols), unwindows(grad, rows, cols)])
    edge = cols - SHIFT
    left = neighbour(back[:, :, edge:], "gx", 1)
    back = jnp.concatenate([left, back[:, :, :edge]], 2)
    bottom = rows - SHIFT
    above = neighbour(back[:, bottom:], "gy", 1)
    back = jnp.concatenate([above, back[:, :bottom]], 1)
    block_out = add(slide_tokens, back[0])
    grad_in = add(grad_tokens, back[1])

    parts = total([part[k] for k in range(3)])
    whole = jnp.stack(parts).astype(F32)
    grad_wqkv = whole[:, :D].reshape(3, D, 3, GD).transpose(1, 2, 0, 3).reshape(D, 3 * D)
    grad_wout = whole[:, D:].reshape(D, D)
    return block_out, grad_in, grad_wqkv, grad_wout


def solution(mesh):
    tile = P("gy", "gx", None)
    return jax.shard_map(
        local,
        mesh=mesh,
        in_specs=(tile, P("gy", "gx"), tile, P(), P()),
        out_specs=(tile, tile, P(), P()),
        check_vma=False,
    )
```

time: 441 us -> 247 us (0.56); the launches traced: 433 us -> 245 us
  matrix products: 101 us -> 0 us
  waiting for transfers between devices: 160 us -> 67.7 us
  local copies, waits for them, and re-layouts: 119 us -> 44.3 us
  Pallas kernels: 0 us -> 71.9 us
  starting transfers between devices: 16.9 us -> 39.3 us
  between operations: 14.7 us -> 1.23 us
    psum x1 -> x0, waiting for transfers between devices: 131 us -> none  [local(): grad_wqkv, grad_wout = lax.psum((part_qkv, part_out), ('gx', 'gy'))]
    dot_general x11 -> x0, matrix products: 90.3 us -> none  [the longest x1 20 us: attend_back(): jnp.einsum('whqk,wqhd->wkhd', score_half, queries, preferred_element_type...]
    pallas_call x0 -> x2, Pallas kernels: none -> 71.9 us  [the longest x1 60.8 us: attn_call(): pl.pallas_call(functools.partial(attn_body, nwin), grid=(3,), in_specs=[p...]
    ppermute x10 -> x34, waiting for transfers between devices: 29.1 us -> 67.7 us  [the longest x28 54.5 us: exchange(): return lax.ppermute(v, AXES, pairs)]
    convert_element_type x4 -> x0, local copies, waits for them, and re-layouts: 27.7 us -> none  [the longest x1 6.92 us: attend(): mixed_out = jnp.einsum('whqk,wkhd->wqhd', weights_half, values_part, pref...]
    concatenate x3 -> x0, local copies, waits for them, and re-layouts: 24.6 us -> none  [attend_back(): jnp.concatenate([grad_query.reshape(shape_out), grad_key.reshape(shape_ou...]
    another operation x5 -> x2, local copies, waits for them, and re-layouts: 25.2 us -> 2.61 us  [windows(): t = t.reshape(r // WIN, WIN, c // WIN, WIN, f)]
    ppermute x10 -> x34, starting transfers between devices: 16.9 us -> 39.3 us  [the longest x28 23.8 us: exchange(): return lax.ppermute(v, AXES, pairs)]
  transfers between devices with their start and end apart: 11 -> 34, of which waited for: 7 -> 19; matrix products, arithmetic and copies ran while one was open for 8% -> 8% of each run, Pallas kernels for 0% -> 5%
where the time goes in v1:
time: 247 us; the launch traced here: 245 us
  Pallas kernels  71.9 us (29%)
  waiting for transfers between devices  67.7 us (27%)
  local copies, waits for them, and re-layouts  44.3 us (18%)
  starting transfers between devices  39.3 us (16%)
  other arithmetic  20.3 us (8%)
    pallas_call x1, Pallas kernels, attn_call(): pl.pallas_call(functools.partial(attn_body, nwin), grid=(3,), in_specs=[p...  60.8 us
    ppermute x28, waiting for transfers between devices, exchange(): return lax.ppermute(v, AXES, pairs)  54.5 us
    ppermute x28, starting transfers between devices, exchange(): return lax.ppermute(v, AXES, pairs)  23.8 us
    unnamed x29, local copies, waits for them, and re-layouts  16.1 us
    ppermute x6, starting transfers between devices, neighbour(): lax.ppermute(block, axis, [((i - distance) % n, i) for i in range(n)])  15.4 us
    ppermute x6, waiting for transfers between devices, neighbour(): lax.ppermute(block, axis, [((i - distance) % n, i) for i in range(n)])  13.2 us
    slice x2, local copies, waits for them, and re-layouts, local(): whole[:, :D].reshape(3, D, 3, GD).transpose(1, 2, 0, 3).reshape(D, 3 * D)  11.5 us
    pallas_call x1, Pallas kernels, finish_call(): pl.pallas_call(finish_body, grid=(tokens // tile,), in_specs=[t, t, t, t,...  11.1 us
  transfers between devices with their start and end apart: 34, of which 19 were waited for; matrix products, arithmetic and copies ran while one was open for 8% of the time, Pallas kernels for 5%

profile of v1, /device:TPU:0, one launch (start us, length us, event | category | flops | bytes accessed | tf_op | source)
XLA Modules:
  0.0 244.8 jit_solution(8815591783434966971)
XLA Ops:
  1.3 4.2 %collective-permute-start.2 = (bf16[4,64]{1,0:T(4,128)(2,1)S(1)}, bf16[4,64]{1,0:T(4,128)(2,1)S(1)}, u32[]{:S(2)}, u32[]{:S(2)}) collective-permute-start(bf16[4,64]{1,0:T(4,128)(2,1)S(1)} %slice.103), channel_id=1, source_target_pairs={{1,0},{2,1},{3,2},{4,3},{5,4},{6,5},{7,6},{0,7},{9,8},{10,9},{11,1... | collective-permute-start | bytes 1544 | tf_op jit(solution)/shard_map/ppermute | solution.py:261
  5.5 2.1 pad_maximum_fusion.4
  10.4 5.0 %collective-permute-start.3 = (bf16[16,4]{1,0:T(8,128)(2,1)S(1)}, bf16[16,4]{1,0:T(8,128)(2,1)S(1)}, u32[]{:S(2)}, u32[]{:S(2)}) collective-permute-start(bf16[16,4]{1,0:T(8,128)(2,1)S(1)} %pad_maximum_fusion.8), channel_id=1, source_target_pairs={{8,0},{16,8},{24,16},{32,24},{40,32},{48,40},{56,48},{64,56},{72,6... | collective-permute-start | bytes 392 | tf_op jit(solution)/shard_map/ppermute | solution.py:261
  17.2 9.6 %collective-permute-done = bf16[2,4,64,768]{3,2,1,0:T(8,128)(2,1)S(1)} collective-permute-done((bf16[2,4,64,768]{3,2,1,0:T(8,128)(2,1)}, bf16[2,4,64,768]{3,2,1,0:T(8,128)(2,1)S(1)}, u32[]{:S(2)}, u32[]{:S(2)}) %collective-permute-start) | collective-permute-done | bytes 786464 | tf_op jit(solution)/shard_map/ppermute | solution.py:261
  26.9 4.4 %collective-permute-start.1 = (bf16[2,16,4,768]{3,2,1,0:T(4,128)(2,1)S(1)}, bf16[2,16,4,768]{3,2,1,0:T(4,128)(2,1)S(1)}, u32[]{:S(2)}, u32[]{:S(2)}) collective-permute-start(bf16[2,16,4,768]{3,2,1,0:T(4,128)(2,1)S(1)} %pad_maximum_fusion.7), channel_id=1, source_target_pairs={{8,0},{16,8},{24,16},{32,24},{40,32},{48,40},{56,48},{64,56},{72,6... | collective-permute-start | bytes 589832 | tf_op jit(solution)/shard_map/ppermute | solution.py:261
  32.1 2.3 collective-permute-done.1
  37.8 60.8 %attention.1 = (bf16[1024,768]{1,0:T(8,128)(2,1)S(1)}, bf16[1024,768]{1,0:T(8,128)(2,1)S(1)}, bf16[1024,768]{1,0:T(8,128)(2,1)}, bf16[1024,768]{1,0:T(8,128)(2,1)}, bf16[3,1024,768]{2,1,0:T(8,128)(2,1)}) custom-call(bf16[1024,768]{1,0:T(8,128)(2,1)} %bitcast.65, bf16[1024,768]{1,0:T(8,128)(2,1)} %bitcast.87, f32[1024,128]{1,0:T(8,128)S(1)} %fusion.8.bias_ref, ...), custom_call_target="tpu_custom_call" | custom-call | flops 14000000000 | bytes 20000000 | tf_op jit(solution)/shard_map/attention/pallas_call | solution.py:118
  98.6 3.8 %fusion.9 = (bf16[1,1024,768]{2,1,0:T(8,128)(2,1)S(1)}, bf16[1,1024,768]{2,1,0:T(8,128)(2,1)S(1)}, bf16[1,1024,768]{2,1,0:T(8,128)(2,1)S(1)}) fusion(bf16[3,1024,768]{2,1,0:T(8,128)(2,1)} %get-tuple-element.17), kind=kLoop, calls=%fused_computation.78 | loop fusion | bytes 9437184 | tf_op jit(solution)/shard_map/slice | solution.py:306
  109.8 5.9 %collective-permute-done.11 = bf16[256,768]{1,0:T(8,128)(2,1)S(1)} collective-permute-done((bf16[256,768]{1,0:T(8,128)(2,1)S(1)}, bf16[256,768]{1,0:T(8,128)(2,1)S(1)}, u32[]{:S(2)}, u32[]{:S(2)}) %collective-permute-start.11) | collective-permute-done | bytes 393248 | tf_op jit(solution)/shard_map/ppermute | solution.py:211
  117.7 2.1 collective-permute-start.8
  123.2 2.1 collective-permute-start.17
  127.9 2.1 collective-permute-done.9
  130.2 2.0 collective-permute-start.18
  132.1 4.5 %collective-permute-done.18 = bf16[96,768]{1,0:T(8,128)(2,1)S(1)} collective-permute-done((bf16[96,768]{1,0:T(8,128)(2,1)S(1)}, bf16[96,768]{1,0:T(8,128)(2,1)S(1)}, u32[]{:S(2)}, u32[]{:S(2)}) %collective-permute-start.18) | collective-permute-done | bytes 147488 | tf_op jit(solution)/shard_map/ppermute | solution.py:211
  136.6 2.8 %collective-permute-start.19 = (bf16[96,768]{1,0:T(8,128)(2,1)S(1)}, bf16[96,768]{1,0:T(8,128)(2,1)S(1)}, u32[]{:S(2)}, u32[]{:S(2)}) collective-permute-start(bf16[96,768]{1,0:T(8,128)(2,1)S(1)} %add_convert_fusion.8), channel_id=1, source_target_pairs={{0,48},{1,49},{2,50},{3,51},{4,52},{5,53},{6,54},{7,55},{8,24},{9,... | collective-permute-start | bytes 442376 | tf_op jit(solution)/shard_map/ppermute | solution.py:211
  139.5 3.6 %collective-permute-done.19 = bf16[96,768]{1,0:T(8,128)(2,1)S(1)} collective-permute-done((bf16[96,768]{1,0:T(8,128)(2,1)S(1)}, bf16[96,768]{1,0:T(8,128)(2,1)S(1)}, u32[]{:S(2)}, u32[]{:S(2)}) %collective-permute-start.19) | collective-permute-done | bytes 147488 | tf_op jit(solution)/shard_map/ppermute | solution.py:211
  143.1 2.1 collective-permute-start.20
  145.2 4.3 %collective-permute-done.20 = bf16[96,768]{1,0:T(8,128)(2,1)S(1)} collective-permute-done((bf16[96,768]{1,0:T(8,128)(2,1)S(1)}, bf16[96,768]{1,0:T(8,128)(2,1)S(1)}, u32[]{:S(2)}, u32[]{:S(2)}) %collective-permute-start.20) | collective-permute-done | bytes 147488 | tf_op jit(solution)/shard_map/ppermute | solution.py:211
  149.6 2.2 collective-permute-start.21
  151.8 2.0 copy-done.1
  159.4 11.1 %finish.1 = (bf16[1024,768]{1,0:T(8,128)(2,1)S(1)}, bf16[1024,768]{1,0:T(8,128)(2,1)S(1)}) custom-call(bf16[1024,768]{1,0:T(8,128)(2,1)S(1)} %bitcast.66, bf16[1024,768]{1,0:T(8,128)(2,1)S(1)} %copy-done.4, bf16[1024,768]{1,0:T(8,128)(2,1)S(1)} %copy-done.6, bf16[1024,768]{1,0:T(8,128)(2,1)S(1)} %copy-done.7, bf16[1024,768]{1,0:T(8,128)(2,1)S(1)} %copy-done.8, ...), custom_call_target="tpu_custom_call" | custom-call | flops 4800000000 | bytes 16000000 | tf_op jit(solution)/shard_map/finish/pallas_call | solution.py:167
  172.3 3.3 %collective-permute-done.26 = bf16[64,768]{1,0:T(8,128)(2,1)S(1)} collective-permute-done((bf16[64,768]{1,0:T(8,128)(2,1)S(1)}, bf16[64,768]{1,0:T(8,128)(2,1)S(1)}, u32[]{:S(2)}, u32[]{:S(2)}) %collective-permute-start.26) | collective-permute-done | bytes 98336 | tf_op jit(solution)/shard_map/ppermute | solution.py:211
  176.0 2.1 collective-permute-start.31
  178.2 2.0 collective-permute-start.23
  180.2 2.4 collective-permute-done.27
  186.1 4.5 %collective-permute-done.28 = bf16[256,768]{1,0:T(8,128)(2,1)S(1)} collective-permute-done((bf16[256,768]{1,0:T(8,128)(2,1)S(1)}, bf16[256,768]{1,0:T(8,128)(2,1)S(1)}, u32[]{:S(2)}, u32[]{:S(2)}) %collective-permute-start.28) | collective-permute-done | bytes 393248 | tf_op jit(solution)/shard_map/ppermute | solution.py:211
  191.9 16.8 %collective-permute-done.32 = bf16[256,768]{1,0:T(8,128)(2,1)S(1)} collective-permute-done((bf16[256,768]{1,0:T(8,128)(2,1)S(1)}, bf16[256,768]{1,0:T(8,128)(2,1)S(1)}, u32[]{:S(2)}, u32[]{:S(2)}) %collective-permute-start.32) | collective-permute-done | bytes 393248 | tf_op jit(solution)/shard_map/ppermute | solution.py:211
  211.7 2.8 %fusion.1 = (bf16[16,64,768]{2,1,0:T(8,128)(2,1)}, bf16[16,64,768]{2,1,0:T(8,128)(2,1)}) fusion(bf16[16,64,768]{2,1,0:T(8,128)(2,1)S(1)} %copy-done.9, bf16[2,16,64,768]{3,2,1,0:T(8,128)(2,1)S(1)} %fusion, bf16[16,64,768]{2,1,0:T(8,128)(2,1)S(1)} %copy-done.10), kind=kLoop, calls=%fused_computation.10 | loop fusion | flops 6291456 | bytes 9437184 | tf_op jit(solution)/shard_map/convert_element_type | solution.py:226
  219.0 3.4 %slice.111 = f32[3,768,768]{2,1,0:T(8,128)} slice(f32[3,1024,768]{2,1,0:T(8,128)S(1)} %maximum_convert_fusion), slice={[0:3], [0:768], [0:768]} | slice | bytes 14155776 | tf_op jit(solution)/shard_map/slice | solution.py:308
  222.4 8.0 %copy.19 = f32[3,768,768]{1,2,0:T(8,128)} copy(f32[3,768,768]{2,1,0:T(8,128)} %slice.111) | data formatting | bytes 14155776 | tf_op jit(solution)/shard_map/slice | solution.py:308
  230.4 6.4 %copy.20 = f32[768,3,3,256]{0,3,2,1:T(8,128)} copy(f32[768,3,3,256]{0,3,1,2:T(8,128)} %bitcast.69) | data formatting | bytes 14155776 | tf_op jit(solution)/shard_map/transpose | solution.py:308
  236.8 8.0 %copy.21 = f32[768,2304]{1,0:T(8,128)} copy(f32[768,2304]{0,1:T(8,128)} %bitcast.70) | data formatting | bytes 14155776
  (142 shorter events, 44.8 us)
Async XLA Ops:
  1.3 9.0 %collective-permute-start.2 = (bf16[4,64]{1,0:T(4,128)(2,1)S(1)}, bf16[4,64]{1,0:T(4,128)(2,1)S(1)}, u32[]{:S(2)}, u32[]{:S(2)}) collective-permute-start(bf16[4,64]{1,0:T(4,128)(2,1)S(1)} %slice.103), channel_id=1, source_target_pairs={{1,0},{2,1},{3,2},{4,3},{5,4},{6,5},{7,6},{0,7},{9,8},{10,9},{11,1... | collective-permute-start | bytes 1544 | tf_op jit(solution)/shard_map/ppermute | solution.py:261
  7.6 19.2 %collective-permute-start = (bf16[2,4,64,768]{3,2,1,0:T(8,128)(2,1)}, bf16[2,4,64,768]{3,2,1,0:T(8,128)(2,1)S(1)}, u32[]{:S(2)}, u32[]{:S(2)}) collective-permute-start(bf16[2,4,64,768]{3,2,1,0:T(8,128)(2,1)} %pad_maximum_fusion.4), channel_id=1, source_target_pairs={{1,0},{2,1},{3,2},{4,3},{5,4},{6,5},{7,6},{0,7},{9,8},{10,9},{11,1... | collective-permute-start | bytes 2359304 | tf_op jit(solution)/shard_map/ppermute | solution.py:261
  10.4 6.3 %collective-permute-start.3 = (bf16[16,4]{1,0:T(8,128)(2,1)S(1)}, bf16[16,4]{1,0:T(8,128)(2,1)S(1)}, u32[]{:S(2)}, u32[]{:S(2)}) collective-permute-start(bf16[16,4]{1,0:T(8,128)(2,1)S(1)} %pad_maximum_fusion.8), channel_id=1, source_target_pairs={{8,0},{16,8},{24,16},{32,24},{40,32},{48,40},{56,48},{64,56},{72,6... | collective-permute-start | bytes 392 | tf_op jit(solution)/shard_map/ppermute | solution.py:261
  26.9 7.5 %collective-permute-start.1 = (bf16[2,16,4,768]{3,2,1,0:T(4,128)(2,1)S(1)}, bf16[2,16,4,768]{3,2,1,0:T(4,128)(2,1)S(1)}, u32[]{:S(2)}, u32[]{:S(2)}) collective-permute-start(bf16[2,16,4,768]{3,2,1,0:T(4,128)(2,1)S(1)} %pad_maximum_fusion.7), channel_id=1, source_target_pairs={{8,0},{16,8},{24,16},{32,24},{40,32},{48,40},{56,48},{64,56},{72,6... | collective-permute-start | bytes 589832 | tf_op jit(solution)/shard_map/ppermute | solution.py:261
  106.0 3.5 %collective-permute-start.6 = (bf16[512,768]{1,0:T(8,128)(2,1)}, bf16[512,768]{1,0:T(8,128)(2,1)S(1)}, u32[]{:S(2)}, u32[]{:S(2)}) collective-permute-start(bf16[512,768]{1,0:T(8,128)(2,1)} %dynamic-slice_bitcast_fusion.2), channel_id=1, source_target_pairs={{0,8},{1,9},{2,10},{3,11},{4,12},{5,13},{6,14},{7,15},{8,0},{9,1},... | collective-permute-start | bytes 2359304 | tf_op jit(solution)/shard_map/ppermute | solution.py:211
  107.9 7.9 %collective-permute-start.11 = (bf16[256,768]{1,0:T(8,128)(2,1)S(1)}, bf16[256,768]{1,0:T(8,128)(2,1)S(1)}, u32[]{:S(2)}, u32[]{:S(2)}) collective-permute-start(bf16[256,768]{1,0:T(8,128)(2,1)S(1)} %constant_dynamic-slice_fusion.6), channel_id=1, source_target_pairs={{0,16},{1,17},{2,18},{3,19},{4,20},{5,21},{6,22},{7,23},{8,56},{9,... | collective-permute-start | bytes 1179656 | tf_op jit(solution)/shard_map/ppermute | solution.py:211
  109.4 7.9 %collective-permute-start.15 = (bf16[256,768]{1,0:T(8,128)(2,1)S(1)}, bf16[256,768]{1,0:T(8,128)(2,1)S(1)}, u32[]{:S(2)}, u32[]{:S(2)}) collective-permute-start(bf16[256,768]{1,0:T(8,128)(2,1)S(1)} %constant_dynamic-slice_fusion.3), channel_id=1, source_target_pairs={{0,4},{1,5},{2,6},{3,7},{4,0},{5,1},{6,2},{7,3},{8,76},{9,77},{10,... | collective-permute-start | bytes 1179656 | tf_op jit(solution)/shard_map/ppermute | solution.py:211
  109.7 7.9 %collective-permute-start.7 = (bf16[256,768]{1,0:T(8,128)(2,1)S(1)}, bf16[256,768]{1,0:T(8,128)(2,1)S(1)}, u32[]{:S(2)}, u32[]{:S(2)}) collective-permute-start(bf16[256,768]{1,0:T(8,128)(2,1)S(1)} %constant_dynamic-slice_fusion.9), channel_id=1, source_target_pairs={{0,1},{1,0},{2,3},{3,2},{4,5},{5,4},{6,7},{7,6},{8,11},{9,10},{10,... | collective-permute-start | bytes 1179656 | tf_op jit(solution)/shard_map/ppermute | solution.py:211
  115.9 5.8 %collective-permute-start.12 = (bf16[128,768]{1,0:T(8,128)(2,1)S(1)}, bf16[128,768]{1,0:T(8,128)(2,1)S(1)}, u32[]{:S(2)}, u32[]{:S(2)}) collective-permute-start(bf16[128,768]{1,0:T(8,128)(2,1)S(1)} %constant_dynamic-slice_fusion.5), channel_id=1, source_target_pairs={{0,4},{1,5},{2,6},{3,7},{4,0},{5,1},{6,2},{7,3},{8,76},{9,77},{10,... | collective-permute-start | bytes 589832 | tf_op jit(solution)/shard_map/ppermute | solution.py:211
  117.4 5.7 %collective-permute-start.16 = (bf16[128,768]{1,0:T(8,128)(2,1)S(1)}, bf16[128,768]{1,0:T(8,128)(2,1)S(1)}, u32[]{:S(2)}, u32[]{:S(2)}) collective-permute-start(bf16[128,768]{1,0:T(8,128)(2,1)S(1)} %constant_dynamic-slice_fusion.2), channel_id=1, source_target_pairs={{0,1},{1,0},{2,3},{3,2},{4,5},{5,4},{6,7},{7,6},{8,11},{9,10},{10,... | collective-permute-start | bytes 589832 | tf_op jit(solution)/shard_map/ppermute | solution.py:211
  117.7 7.5 %collective-permute-start.8 = (bf16[128,768]{1,0:T(8,128)(2,1)S(1)}, bf16[128,768]{1,0:T(8,128)(2,1)S(1)}, u32[]{:S(2)}, u32[]{:S(2)}) collective-permute-start(bf16[128,768]{1,0:T(8,128)(2,1)S(1)} %constant_dynamic-slice_fusion.8), channel_id=1, source_target_pairs={{0,16},{1,17},{2,18},{3,19},{4,20},{5,21},{6,22},{7,23},{8,56},{9,... | collective-permute-start | bytes 589832 | tf_op jit(solution)/shard_map/ppermute | solution.py:211
  121.7 4.7 %collective-permute-start.13 = (bf16[64,768]{1,0:T(8,128)(2,1)S(1)}, bf16[64,768]{1,0:T(8,128)(2,1)S(1)}, u32[]{:S(2)}, u32[]{:S(2)}) collective-permute-start(bf16[64,768]{1,0:T(8,128)(2,1)S(1)} %constant_dynamic-slice_fusion.4), channel_id=1, source_target_pairs={{0,1},{1,0},{2,3},{3,2},{4,5},{5,4},{6,7},{7,6},{8,11},{9,10},{10,... | collective-permute-start | bytes 294920 | tf_op jit(solution)/shard_map/ppermute | solution.py:211
  123.2 4.7 %collective-permute-start.17 = (bf16[64,768]{1,0:T(8,128)(2,1)S(1)}, bf16[64,768]{1,0:T(8,128)(2,1)S(1)}, u32[]{:S(2)}, u32[]{:S(2)}) collective-permute-start(bf16[64,768]{1,0:T(8,128)(2,1)S(1)} %constant_dynamic-slice_fusion.1), channel_id=1, source_target_pairs={{0,16},{1,17},{2,18},{3,19},{4,20},{5,21},{6,22},{7,23},{8,56},{9,... | collective-permute-start | bytes 294920 | tf_op jit(solution)/shard_map/ppermute | solution.py:211
  125.4 4.7 %collective-permute-start.9 = (bf16[64,768]{1,0:T(8,128)(2,1)S(1)}, bf16[64,768]{1,0:T(8,128)(2,1)S(1)}, u32[]{:S(2)}, u32[]{:S(2)}) collective-permute-start(bf16[64,768]{1,0:T(8,128)(2,1)S(1)} %constant_dynamic-slice_fusion.7), channel_id=1, source_target_pairs={{0,4},{1,5},{2,6},{3,7},{4,0},{5,1},{6,2},{7,3},{8,76},{9,77},{10,... | collective-permute-start | bytes 294920 | tf_op jit(solution)/shard_map/ppermute | solution.py:211
  130.2 6.4 %collective-permute-start.18 = (bf16[96,768]{1,0:T(8,128)(2,1)S(1)}, bf16[96,768]{1,0:T(8,128)(2,1)S(1)}, u32[]{:S(2)}, u32[]{:S(2)}) collective-permute-start(bf16[96,768]{1,0:T(8,128)(2,1)S(1)} %constant_dynamic-slice_fusion), channel_id=1, source_target_pairs={{0,3},{1,2},{2,1},{3,0},{4,7},{5,6},{6,5},{7,4},{8,9},{9,8},{10,11... | collective-permute-start | bytes 442376 | tf_op jit(solution)/shard_map/ppermute | solution.py:211
  136.6 6.4 %collective-permute-start.19 = (bf16[96,768]{1,0:T(8,128)(2,1)S(1)}, bf16[96,768]{1,0:T(8,128)(2,1)S(1)}, u32[]{:S(2)}, u32[]{:S(2)}) collective-permute-start(bf16[96,768]{1,0:T(8,128)(2,1)S(1)} %add_convert_fusion.8), channel_id=1, source_target_pairs={{0,48},{1,49},{2,50},{3,51},{4,52},{5,53},{6,54},{7,55},{8,24},{9,... | collective-permute-start | bytes 442376 | tf_op jit(solution)/shard_map/ppermute | solution.py:211
  143.1 6.4 %collective-permute-start.20 = (bf16[96,768]{1,0:T(8,128)(2,1)S(1)}, bf16[96,768]{1,0:T(8,128)(2,1)S(1)}, u32[]{:S(2)}, u32[]{:S(2)}) collective-permute-start(bf16[96,768]{1,0:T(8,128)(2,1)S(1)} %add_convert_fusion.7), channel_id=1, source_target_pairs={{0,68},{1,69},{2,70},{3,71},{4,64},{5,65},{6,66},{7,67},{8,12},{9,... | collective-permute-start | bytes 442376 | tf_op jit(solution)/shard_map/ppermute | solution.py:211
  149.6 21.2 %collective-permute-start.21 = (bf16[96,768]{1,0:T(8,128)(2,1)S(1)}, bf16[96,768]{1,0:T(8,128)(2,1)S(1)}, u32[]{:S(2)}, u32[]{:S(2)}) collective-permute-start(bf16[96,768]{1,0:T(8,128)(2,1)S(1)} %add_convert_fusion.6), channel_id=1, source_target_pairs={{0,3},{1,2},{2,1},{3,0},{4,7},{5,6},{6,5},{7,4},{8,9},{9,8},{10,11... | collective-permute-start | bytes 442376 | tf_op jit(solution)/shard_map/ppermute | solution.py:211
  170.9 4.7 %collective-permute-start.26 = (bf16[64,768]{1,0:T(8,128)(2,1)S(1)}, bf16[64,768]{1,0:T(8,128)(2,1)S(1)}, u32[]{:S(2)}, u32[]{:S(2)}) collective-permute-start(bf16[64,768]{1,0:T(8,128)(2,1)S(1)} %get-tuple-element.31), channel_id=1, source_target_pairs={{0,1},{1,0},{2,3},{3,2},{4,5},{5,4},{6,7},{7,6},{8,11},{9,10},{10,... | collective-permute-start | bytes 294920 | tf_op jit(solution)/shard_map/ppermute | solution.py:211
  171.1 11.6 %collective-permute-start.4 = (bf16[2,16,4,768]{3,2,1,0:T(4,128)(2,1)S(1)}, bf16[2,16,4,768]{3,2,1,0:T(4,128)(2,1)S(1)}, u32[]{:S(2)}, u32[]{:S(2)}) collective-permute-start(bf16[2,16,4,768]{3,2,1,0:T(4,128)(2,1)S(1)} %pad_maximum_fusion.6), channel_id=1, source_target_pairs={{120,0},{0,8},{8,16},{16,24},{24,32},{32,40},{40,48},{48,56},{56,6... | collective-permute-start | bytes 589832 | tf_op jit(solution)/shard_map/ppermute | solution.py:261
  171.2 6.9 %collective-permute-start.22 = (bf16[64,768]{1,0:T(8,128)(2,1)S(1)}, bf16[64,768]{1,0:T(8,128)(2,1)S(1)}, u32[]{:S(2)}, u32[]{:S(2)}) collective-permute-start(bf16[64,768]{1,0:T(8,128)(2,1)S(1)} %get-tuple-element.29), channel_id=1, source_target_pairs={{0,4},{1,5},{2,6},{3,7},{4,0},{5,1},{6,2},{7,3},{8,76},{9,77},{10,... | collective-permute-start | bytes 294920 | tf_op jit(solution)/shard_map/ppermute | solution.py:211
  171.3 4.7 %collective-permute-start.30 = (bf16[64,768]{1,0:T(8,128)(2,1)S(1)}, bf16[64,768]{1,0:T(8,128)(2,1)S(1)}, u32[]{:S(2)}, u32[]{:S(2)}) collective-permute-start(bf16[64,768]{1,0:T(8,128)(2,1)S(1)} %get-tuple-element.30), channel_id=1, source_target_pairs={{0,16},{1,17},{2,18},{3,19},{4,20},{5,21},{6,22},{7,23},{8,56},{9,... | collective-permute-start | bytes 294920 | tf_op jit(solution)/shard_map/ppermute | solution.py:211
  175.7 6.9 %collective-permute-start.27 = (bf16[128,768]{1,0:T(8,128)(2,1)S(1)}, bf16[128,768]{1,0:T(8,128)(2,1)S(1)}, u32[]{:S(2)}, u32[]{:S(2)}) collective-permute-start(bf16[128,768]{1,0:T(8,128)(2,1)S(1)} %maximum_select_fusion.11), channel_id=1, source_target_pairs={{0,4},{1,5},{2,6},{3,7},{4,0},{5,1},{6,2},{7,3},{8,76},{9,77},{10,... | collective-permute-start | bytes 589832 | tf_op jit(solution)/shard_map/ppermute | solution.py:211
  176.0 8.0 %collective-permute-start.31 = (bf16[128,768]{1,0:T(8,128)(2,1)S(1)}, bf16[128,768]{1,0:T(8,128)(2,1)S(1)}, u32[]{:S(2)}, u32[]{:S(2)}) collective-permute-start(bf16[128,768]{1,0:T(8,128)(2,1)S(1)} %maximum_select_fusion.12), channel_id=1, source_target_pairs={{0,1},{1,0},{2,3},{3,2},{4,5},{5,4},{6,7},{7,6},{8,11},{9,10},{10,... | collective-permute-start | bytes 589832 | tf_op jit(solution)/shard_map/ppermute | solution.py:211
  178.2 6.4 %collective-permute-start.23 = (bf16[128,768]{1,0:T(8,128)(2,1)S(1)}, bf16[128,768]{1,0:T(8,128)(2,1)S(1)}, u32[]{:S(2)}, u32[]{:S(2)}) collective-permute-start(bf16[128,768]{1,0:T(8,128)(2,1)S(1)} %maximum_select_fusion.10), channel_id=1, source_target_pairs={{0,16},{1,17},{2,18},{3,19},{4,20},{5,21},{6,22},{7,23},{8,56},{9,... | collective-permute-start | bytes 589832 | tf_op jit(solution)/shard_map/ppermute | solution.py:211
  182.7 7.9 %collective-permute-start.28 = (bf16[256,768]{1,0:T(8,128)(2,1)S(1)}, bf16[256,768]{1,0:T(8,128)(2,1)S(1)}, u32[]{:S(2)}, u32[]{:S(2)}) collective-permute-start(bf16[256,768]{1,0:T(8,128)(2,1)S(1)} %maximum_select_fusion.7), channel_id=1, source_target_pairs={{0,16},{1,17},{2,18},{3,19},{4,20},{5,21},{6,22},{7,23},{8,56},{9,... | collective-permute-start | bytes 1179656 | tf_op jit(solution)/shard_map/ppermute | solution.py:211
  183.0 27.4 %collective-permute-start.5 = (bf16[2,4,64,768]{3,2,1,0:T(8,128)(2,1)S(1)}, bf16[2,4,64,768]{3,2,1,0:T(8,128)(2,1)S(1)}, u32[]{:S(2)}, u32[]{:S(2)}) collective-permute-start(bf16[2,4,64,768]{3,2,1,0:T(8,128)(2,1)S(1)} %pad_maximum_fusion.3), channel_id=1, source_target_pairs={{7,0},{0,1},{1,2},{2,3},{3,4},{4,5},{5,6},{6,7},{15,8},{8,9},{9,10... | collective-permute-start | bytes 2359304 | tf_op jit(solution)/shard_map/ppermute | solution.py:261
  184.1 24.7 %collective-permute-start.32 = (bf16[256,768]{1,0:T(8,128)(2,1)S(1)}, bf16[256,768]{1,0:T(8,128)(2,1)S(1)}, u32[]{:S(2)}, u32[]{:S(2)}) collective-permute-start(bf16[256,768]{1,0:T(8,128)(2,1)S(1)} %maximum_select_fusion.8), channel_id=1, source_target_pairs={{0,4},{1,5},{2,6},{3,7},{4,0},{5,1},{6,2},{7,3},{8,76},{9,77},{10,... | collective-permute-start | bytes 1179656 | tf_op jit(solution)/shard_map/ppermute | solution.py:211
  184.6 24.6 %collective-permute-start.24 = (bf16[256,768]{1,0:T(8,128)(2,1)S(1)}, bf16[256,768]{1,0:T(8,128)(2,1)S(1)}, u32[]{:S(2)}, u32[]{:S(2)}) collective-permute-start(bf16[256,768]{1,0:T(8,128)(2,1)S(1)} %maximum_select_fusion.6), channel_id=1, source_target_pairs={{0,1},{1,0},{2,3},{3,2},{4,5},{5,4},{6,7},{7,6},{8,11},{9,10},{10,... | collective-permute-start | bytes 1179656 | tf_op jit(solution)/shard_map/ppermute | solution.py:211
  190.8 23.7 %collective-permute-start.29 = (bf16[512,768]{1,0:T(8,128)(2,1)S(1)}, bf16[512,768]{1,0:T(8,128)(2,1)S(1)}, u32[]{:S(2)}, u32[]{:S(2)}) collective-permute-start(bf16[512,768]{1,0:T(8,128)(2,1)S(1)} %maximum_select_fusion.4), channel_id=1, source_target_pairs={{0,8},{1,9},{2,10},{3,11},{4,12},{5,13},{6,14},{7,15},{8,0},{9,1},... | collective-permute-start | bytes 2359304 | tf_op jit(solution)/shard_map/ppermute | solution.py:211
  209.1 6.1 %collective-permute-start.33 = (bf16[512,768]{1,0:T(8,128)(2,1)S(1)}, bf16[512,768]{1,0:T(8,128)(2,1)S(1)}, u32[]{:S(2)}, u32[]{:S(2)}) collective-permute-start(bf16[512,768]{1,0:T(8,128)(2,1)S(1)} %maximum_select_fusion.5), channel_id=1, source_target_pairs={{0,8},{1,9},{2,10},{3,11},{4,12},{5,13},{6,14},{7,15},{8,0},{9,1},... | collective-permute-start | bytes 2359304 | tf_op jit(solution)/shard_map/ppermute | solution.py:211
  209.6 6.4 %collective-permute-start.25 = (bf16[512,768]{1,0:T(8,128)(2,1)S(1)}, bf16[512,768]{1,0:T(8,128)(2,1)S(1)}, u32[]{:S(2)}, u32[]{:S(2)}) collective-permute-start(bf16[512,768]{1,0:T(8,128)(2,1)S(1)} %maximum_select_fusion.3), channel_id=1, source_target_pairs={{0,8},{1,9},{2,10},{3,11},{4,12},{5,13},{6,14},{7,15},{8,0},{9,1},... | collective-permute-start | bytes 2359304 | tf_op jit(solution)/shard_map/ppermute | solution.py:211
  (16 other events, 59.9 us)

commit v2 on v1

v2 whole, which is shorter than its diff:
```python
import functools
import math
import jax
import jax.numpy as jnp
from jax import lax
from jax.experimental import pallas as pl
from jax.experimental.pallas import tpu as pltpu
from jax.sharding import PartitionSpec as P

HEADS = 24
WIN = 8
SHIFT = 4
D = 768
GD = 256
EPS = 1e-05
SCALE = 1.0 / math.sqrt(32)
LOG2E = math.log2(math.e)
NT = (((1,), (1,)), ((), ()))
NN = (((1,), (0,)), ((), ()))
F32 = jnp.float32
BF16 = jnp.bfloat16


def mm(a, b, dims=NN):
    return lax.dot_general(a, b, dims, preferred_element_type=F32)


def spread(t, head_lane):
    zero = jnp.zeros_like(t)
    return jnp.concatenate([jnp.where(head_lane == h, t, zero) for h in range(4)], 0)


def gather_diag(full, head_lane):
    out = full[0:64]
    for h in range(1, 4):
        out = jnp.where(head_lane == h, full[64 * h : 64 * h + 64], out)
    return out


TOKENS = 1024
F = 2 * D + 128


def right_half(shape):
    return lax.broadcasted_iota(jnp.int32, shape, 1) >= 4


def seam(a, b):
    return jnp.where(right_half(a.shape), a, b)


def tile_of(t, j):
    return t[:, 8 * j : 8 * j + 8, :]


def pack_body(*refs):
    ins, (up, down, left, corner) = refs[:9], refs[9:]
    lane = 0
    for top, bottom, strip in (ins[0:3], ins[3:6], ins[6:9]):
        width = top.shape[-1]
        lanes = slice(lane, lane + width)
        lane += width
        for j in range(4):
            up[:, 8 * j : 8 * j + 8, lanes] = seam(tile_of(top, j), tile_of(top, j + 1))
        for j in range(3):
            down[:, 8 * j : 8 * j + 8, lanes] = seam(tile_of(bottom, j + 4), tile_of(bottom, j + 5))
        down[:, 24:32, lanes] = tile_of(bottom, 7)
        left[:, :, lanes] = strip[...]
        corner[:, :, lanes] = tile_of(bottom, 0)


def pack_call(x, g, kb):
    specs = []
    for t in (x, g, kb):
        w = t.shape[-1]
        specs += [
            pl.BlockSpec((4, 64, w), lambda i: (0, 0, 0)),
            pl.BlockSpec((4, 64, w), lambda i: (3, 0, 0)),
            pl.BlockSpec((16, 8, w), lambda i: (0, 0, 0)),
        ]
    shapes = [(4, 32, F), (4, 32, F), (16, 8, F), (4, 8, F)]
    return pl.pallas_call(
        pack_body,
        grid=(1,),
        in_specs=specs,
        out_specs=[pl.BlockSpec(sh, lambda i: (0, 0, 0)) for sh in shapes],
        out_shape=[jax.ShapeDtypeStruct(sh, BF16) for sh in shapes],
        compiler_params=pltpu.CompilerParams(vmem_limit_bytes=16 << 20),
        cost_estimate=pl.CostEstimate(flops=0, bytes_accessed=4_000_000, transcendentals=0),
        name="pack",
    )(x, x, x, g, g, g, kb, kb, kb)


def window_pieces(src, below, above, right, corner, lanes):
    out = []
    for j in range(8):
        nxt = tile_of(src[4:12], j + 1) if j < 7 else right[4:12, :, lanes]
        out.append(seam(tile_of(src[4:12], j), nxt))
    for j in range(4):
        own = seam(tile_of(src[12:16], j), tile_of(src[12:16], j + 1))
        out.append(jnp.concatenate([own, tile_of(below, j)[:, :, lanes]], 0))
    for j in range(4):
        nxt = tile_of(src[0:4], j + 5) if j < 3 else right[0:4, :, lanes]
        own = seam(tile_of(src[0:4], j + 4), nxt)
        top = tile_of(above, j)[:, :, lanes]
        if j == 3:
            top = seam(top, corner[:, :, lanes])
        out.append(jnp.concatenate([top, own], 0))
    return out


def attn_body(x_ref, g_ref, kb_ref, below, above, right, corner, wq_ref, wk_ref, wv_ref, wo_ref,
              mixed_ref, dq_ref, dk_ref, dv_ref, xw, part_ref,
              gw, bias, hid, hid_t, qs, ks, vs, gm, mix_t):

    @pl.when(pl.program_id(0) == 0)
    def _():
        halo = (below, above, right, corner)
        for w, t in enumerate(window_pieces(x_ref, *halo, slice(0, D))):
            xw[64 * w : 64 * w + 64, :] = t.astype(F32).reshape(64, D).astype(BF16)
        for w, t in enumerate(window_pieces(g_ref, *halo, slice(D, 2 * D))):
            gw[64 * w : 64 * w + 64, :] = t.astype(F32).reshape(64, D).astype(BF16)
        lane = lax.broadcasted_iota(jnp.int32, (64, 128), 1) % 64
        itself = lane == lax.broadcasted_iota(jnp.int32, (64, 128), 0)
        for w, t in enumerate(window_pieces(kb_ref, *halo, slice(2 * D, F))):
            keep = t.astype(F32).reshape(64, 128) > 0.5
            bias[64 * w : 64 * w + 64, :] = jnp.where(keep | itself, 0.0, -1e30)

        @pl.loop(0, TOKENS // 128)
        def _(i):
            rows = pl.ds(pl.multiple_of(i * 128, 128), 128)
            x = xw[rows, :].astype(F32)
            c = x - jnp.mean(x, -1, keepdims=True)
            inv = lax.rsqrt(jnp.mean(c * c, -1, keepdims=True) + EPS)
            n = c * inv
            hid[rows, :] = n.astype(BF16)
            hid_t[:, rows] = jnp.transpose(n).astype(BF16)

    @pl.loop(0, 1)
    def _(i):
        rows = pl.ds(0, TOKENS)
        h = hid[rows, :]
        qs[rows, :] = mm(h, wq_ref[...]).astype(BF16)
        ks[rows, :] = mm(h, wk_ref[...]).astype(BF16)
        vs[rows, :] = mm(h, wv_ref[...]).astype(BF16)
        gm[rows, :] = mm(gw[rows, :], wo_ref[...], NT).astype(BF16)

    head_lane = lax.broadcasted_iota(jnp.int32, (64, 128), 1) // 32

    U = 4
    TN = (((0,), (0,)), ((), ()))

    @pl.loop(0, 16 // U)
    def _(w):
        keys = []
        for u in range(U):
            rows = pl.ds(pl.multiple_of(w * 64 * U + 64 * u, 64), 64)
            for s in range(GD // 128):
                keys.append((rows, slice(128 * s, 128 * s + 128)))
        ch = [(qs[c], ks[c], vs[c], gm[c]) for c in keys]
        allow = []
        for u in range(U):
            bb = bias[keys[2 * u][0], :]
            allow += [jnp.concatenate([bb, bb], 1)] * 2
        qb = [spread(c[0], head_lane) for c in ch]
        sc = [mm(c[1], b, NT) for c, b in zip(ch, qb)]
        gb = [spread(c[3], head_lane) for c in ch]
        dp = [mm(c[2], b, NT) for c, b in zip(ch, gb)]
        ps, pbs, dbs = [], [], []
        for s, b in zip(sc, allow):
            s = s * (SCALE * LOG2E) + b
            e = jnp.exp2(s - jnp.max(s, 0, keepdims=True))
            p = e * (1.0 / jnp.sum(e, 0, keepdims=True))
            ps.append(p)
            pbs.append(p.astype(BF16))
        for p, d in zip(ps, dp):
            ds = p * ((d - jnp.sum(d * p, 0, keepdims=True)) * SCALE)
            dbs.append(ds.astype(BF16))
        dv = [mm(p, b) for p, b in zip(pbs, gb)]
        mx = [mm(p, c[2], TN) for p, c in zip(pbs, ch)]
        dk = [mm(d, b) for d, b in zip(dbs, qb)]
        dq = [mm(d, c[1], TN) for d, c in zip(dbs, ch)]
        for i, c in enumerate(keys):
            dv_ref[c] = dv[i].astype(BF16)
            mixed_ref[c] = gather_diag(mx[i], head_lane).astype(BF16)
            dk_ref[c] = dk[i].astype(BF16)
            dq_ref[c] = gather_diag(dq[i], head_lane).astype(BF16)

    @pl.loop(0, TOKENS // 128)
    def _(i):
        rows = pl.ds(pl.multiple_of(i * 128, 128), 128)
        mix_t[:, rows] = jnp.transpose(mixed_ref[rows, :].astype(F32)).astype(BF16)

    @pl.loop(0, 1)
    def _(i):
        rows = pl.ds(0, 768)
        h = hid_t[rows, :]
        part_ref[0, rows, 0:256] = mm(h, dq_ref[...]).astype(BF16)
        part_ref[0, rows, 256:512] = mm(h, dk_ref[...]).astype(BF16)
        part_ref[0, rows, 512:768] = mm(h, dv_ref[...]).astype(BF16)

    for j in range(3):
        cols = slice(256 * j, 256 * j + 256)
        part_ref[0, 768:1024, cols] = mm(mix_t[...], gw[:, cols]).astype(BF16)


def attn_call(x, g, kb, halo, w_qkv, w_out):
    fixed = lambda t: pl.BlockSpec(t.shape, lambda i: (0,) * t.ndim, pipeline_mode=pl.Buffered(1))
    cols = pl.BlockSpec((TOKENS, GD), lambda i: (0, i))
    wblock = lambda p: pl.BlockSpec((D, GD), lambda i: (0, 3 * p + i))
    tok = jax.ShapeDtypeStruct((TOKENS, D), BF16)
    return pl.pallas_call(
        attn_body,
        grid=(3,),
        in_specs=[fixed(t) for t in (x, g, kb, *halo)]
        + [wblock(0), wblock(1), wblock(2), pl.BlockSpec((GD, D), lambda i: (i, 0))],
        out_specs=[cols, cols, cols, cols, fixed(tok), pl.BlockSpec((1, 1024, D), lambda i: (i, 0, 0))],
        out_shape=[tok, tok, tok, tok, tok, jax.ShapeDtypeStruct((3, 1024, D), BF16)],
        scratch_shapes=[
            pltpu.VMEM((TOKENS, D), BF16),
            pltpu.VMEM((TOKENS, 128), F32),
            pltpu.VMEM((TOKENS, D), BF16),
            pltpu.VMEM((D, TOKENS), BF16),
            pltpu.VMEM((TOKENS, GD), BF16),
            pltpu.VMEM((TOKENS, GD), BF16),
            pltpu.VMEM((TOKENS, GD), BF16),
            pltpu.VMEM((TOKENS, GD), BF16),
            pltpu.VMEM((GD, TOKENS), BF16),
        ],
        compiler_params=pltpu.CompilerParams(
            dimension_semantics=("arbitrary",), vmem_limit_bytes=48 << 20
        ),
        cost_estimate=pl.CostEstimate(
            flops=14_000_000_000, bytes_accessed=20_000_000, transcendentals=1_600_000
        ),
        name="attention",
    )(x, g, kb, *halo, w_qkv, w_qkv, w_qkv, w_out)


def finish_body(x_ref, mixed_ref, dq_ref, dk_ref, dv_ref, wqkv_ref, wo_ref, attn_ref, gs_ref):
    attn_ref[...] = mm(mixed_ref[...], wo_ref[...]).astype(BF16)
    dh = mm(dq_ref[...], wqkv_ref[:, 0:768], NT)
    dh += mm(dk_ref[...], wqkv_ref[:, 768:1536], NT)
    dh += mm(dv_ref[...], wqkv_ref[:, 1536:2304], NT)
    x = x_ref[...].astype(F32)
    c = x - jnp.mean(x, -1, keepdims=True)
    inv = lax.rsqrt(jnp.mean(c * c, -1, keepdims=True) + EPS)
    n = c * inv
    back = dh - jnp.mean(dh, -1, keepdims=True) - n * jnp.mean(dh * n, -1, keepdims=True)
    gs_ref[...] = (inv * back).astype(BF16)


def finish_call(x, mixed, dq, dk, dv, w_qkv, w_out):
    tokens = x.shape[0]
    tile = 512
    t = pl.BlockSpec((tile, D), lambda i: (i, 0))
    tok = jax.ShapeDtypeStruct((tokens, D), BF16)
    return pl.pallas_call(
        finish_body,
        grid=(tokens // tile,),
        in_specs=[t, t, t, t, t,
                  pl.BlockSpec((D, 3 * D), lambda i: (0, 0), pipeline_mode=pl.Buffered(1)),
                  pl.BlockSpec((D, D), lambda i: (0, 0), pipeline_mode=pl.Buffered(1))],
        out_specs=[t, t],
        out_shape=[tok, tok],
        compiler_params=pltpu.CompilerParams(
            dimension_semantics=("arbitrary",), vmem_limit_bytes=32 << 20
        ),
        cost_estimate=pl.CostEstimate(
            flops=4_800_000_000, bytes_accessed=16_000_000, transcendentals=0
        ),
        name="finish",
    )(x, mixed, dq, dk, dv, w_qkv, w_out)


def merge_body(x_ref, g_ref, attn_ref, grad_ref, below, above, left, corner, out_ref, gin_ref):
    for src, win, dst, lanes in (
        (x_ref, attn_ref, out_ref, slice(0, D)),
        (g_ref, grad_ref, gin_ref, slice(D, 2 * D)),
    ):
        piece = lambda w: win[64 * w : 64 * w + 64, :].astype(F32).reshape(8, 8, D)
        far = lambda t, j: tile_of(t, j)[:, :, lanes].astype(F32)
        mids = [left[4:12, :, lanes].astype(F32)] + [piece(j) for j in range(8)]
        lows = [corner[:, :, lanes].astype(F32)] + [piece(8 + j)[0:4] for j in range(4)] + [far(below, j) for j in range(4)]
        tops = [left[0:4, :, lanes].astype(F32)] + [far(above, j) for j in range(4)] + [piece(12 + j)[4:8] for j in range(4)]
        for j in range(8):
            cols = slice(8 * j, 8 * j + 8)
            for rows, t in ((slice(4, 12), mids), (slice(12, 16), lows), (slice(0, 4), tops)):
                add = seam(t[j + 1], t[j])
                dst[rows, cols, :] = (src[rows, cols, :].astype(F32) + add).astype(BF16)


def merge_call(x, g, attn, grad, halo):
    tile = jax.ShapeDtypeStruct(x.shape, BF16)
    return pl.pallas_call(
        merge_body,
        out_shape=[tile, tile],
        compiler_params=pltpu.CompilerParams(vmem_limit_bytes=32 << 20),
        cost_estimate=pl.CostEstimate(flops=3_000_000, bytes_accessed=11_000_000, transcendentals=0),
        name="merge",
    )(x, g, attn, grad, *halo)


def split_body(attn_ref, grad_ref, up, down, side, corner):
    for win, lanes in ((attn_ref, slice(0, D)), (grad_ref, slice(D, 2 * D))):
        piece = lambda w: win[64 * w : 64 * w + 64, :].astype(F32).reshape(8, 8, D).astype(BF16)
        for j in range(4):
            cols = slice(8 * j, 8 * j + 8)
            up[:, cols, lanes] = piece(12 + j)[0:4]
            down[:, cols, lanes] = piece(8 + j)[4:8]
        side[0:4, :, lanes] = piece(15)[4:8]
        side[4:12, :, lanes] = piece(7)
        corner[:, :, lanes] = piece(15)[0:4]


def split_call(attn, grad):
    shapes = [(4, 32, 2 * D), (4, 32, 2 * D), (12, 8, 2 * D), (4, 8, 2 * D)]
    return pl.pallas_call(
        split_body,
        out_shape=[jax.ShapeDtypeStruct(sh, BF16) for sh in shapes],
        compiler_params=pltpu.CompilerParams(vmem_limit_bytes=16 << 20),
        cost_estimate=pl.CostEstimate(flops=0, bytes_accessed=5_000_000, transcendentals=0),
        name="split",
    )(attn, grad)


def widen_body(core_ref, *refs):
    own, other, (wqkv, wout) = refs[0:3], refs[3:6], refs[6:8]
    j = pl.program_id(0)
    here = core_ref[0]

    def put(srcs):
        rows = pl.ds(pl.multiple_of(j % 2 * 256, 256), 256)

        @pl.when(j < 3)
        def _():
            for k in range(3):
                for p in range(3):
                    wqkv[:, D * p + GD * k : D * p + GD * k + GD] = srcs[k][rows, GD * p : GD * p + GD].astype(F32)

        @pl.when(j == 3)
        def _():
            for k in range(3):
                wout[GD * k : GD * k + GD, :] = srcs[k][256:512, :].astype(F32)

    @pl.when(j // 2 == here)
    def _():
        put(own)

    @pl.when(j // 2 != here)
    def _():
        put(other)


def widen_call(core, own, other):
    half = pl.BlockSpec((512, D), lambda j, c: (0, 0), pipeline_mode=pl.Buffered(1))
    return pl.pallas_call(
        widen_body,
        grid_spec=pltpu.PrefetchScalarGridSpec(
            num_scalar_prefetch=1,
            grid=(4,),
            in_specs=[half] * 6,
            out_specs=[
                pl.BlockSpec((256, 3 * D), lambda j, c: (jnp.minimum(j, 2), 0)),
                pl.BlockSpec((D, D), lambda j, c: (0, 0)),
            ],
        ),
        out_shape=[jax.ShapeDtypeStruct((D, 3 * D), F32), jax.ShapeDtypeStruct((D, D), F32)],
        compiler_params=pltpu.CompilerParams(
            dimension_semantics=("arbitrary",), vmem_limit_bytes=32 << 20
        ),
        cost_estimate=pl.CostEstimate(flops=0, bytes_accessed=14_000_000, transcendentals=0),
        name="widen",
    )(core, *own, *other)

AXES = ("gx", "gy")


def place(i):
    gx, gy = divmod(i, 8)
    z_hi, y, core = gx // 8, gx // 2 % 4, gx % 2
    z_lo, x = divmod(gy, 4)
    return {"core": core, "x": x, "y": y, "z": 2 * z_hi + z_lo}


def number(d):
    z_hi, z_lo = divmod(d["z"], 2)
    return ((z_hi * 4 + d["y"]) * 2 + d["core"]) * 8 + z_lo * 4 + d["x"]


def exchange(v, axis, first):
    pairs = []
    for i in range(128):
        d = place(i)
        if axis == "core":
            d["core"] ^= 1
        elif (d["core"] == 0) == first:
            d[axis] ^= 1
        else:
            d[axis] = 3 - d[axis]
        pairs.append((i, number(d)))
    return lax.ppermute(v, AXES, pairs)


def half_of(axis, first):
    gx, gy = lax.axis_index("gx"), lax.axis_index("gy")
    core = gx % 2
    if axis == "core":
        return core
    p = {"x": gy % 4, "y": gx // 2 % 4, "z": gx // 8 * 2 + gy // 4}[axis]
    inner = ((p == 1) | (p == 2)).astype(jnp.int32)
    upper = (p >= 2).astype(jnp.int32)
    return jnp.where((core == 0) == first, inner, upper)


def add(a, b):
    return (a.astype(F32) + b.astype(F32)).astype(BF16)


def scatter_half(v, axis, first=True):
    n = v.shape[0] // 2
    b = half_of(axis, first)
    keep = lax.dynamic_slice_in_dim(v, b * n, n, 0)
    send = lax.dynamic_slice_in_dim(v, (1 - b) * n, n, 0)
    return add(keep, exchange(send, axis, first))


def gather_half(v, axis, first=True):
    b = half_of(axis, first)
    o = exchange(v, axis, first)
    return jnp.where(b == 0, jnp.concatenate([v, o], 0), jnp.concatenate([o, v], 0))


def total(parts, gate):
    order = [["core"] + ["xyz"[(k + s) % 3] for s in range(3)] for k in range(3)]
    parts = [scatter_half(p, "core") for p in parts]
    parts, gate = lax.optimization_barrier((parts, gate))
    for s in range(1, 4):
        parts = [scatter_half(p, o[s]) for p, o in zip(parts, order)]
    n = parts[0].shape[0]
    v = jnp.concatenate(parts, 0)
    v = scatter_half(v, "x", False)
    for axis in "yz":
        v = add(v, exchange(v, axis, False))
    v = gather_half(v, "x", False)
    parts = [v[n * k : n * k + n] for k in range(3)]
    for s in (3, 2, 1):
        parts = [gather_half(p, o[s]) for p, o in zip(parts, order)]
    return gate, parts, [exchange(p, "core", True) for p in parts]


def shift(v, d_gy, d_gx):
    pairs = []
    for gx in range(16):
        for gy in range(8):
            pairs.append((gx * 8 + gy, (gx + d_gx) % 16 * 8 + (gy + d_gy) % 8))
    return lax.ppermute(v, AXES, pairs)


def local(slide_tokens, tissue, grad_tokens, w_qkv, w_out):
    kb = jnp.broadcast_to(tissue.astype(BF16)[..., None], tissue.shape + (128,))
    up, down, left, corner = pack_call(slide_tokens, grad_tokens, kb)
    halo = (shift(up, -1, 0), shift(down, 1, 0), shift(left, 0, -1), shift(corner, 1, -1))
    mixed, dq, dk, dv, x, part = attn_call(slide_tokens, grad_tokens, kb, halo, w_qkv, w_out)
    attn, grad = finish_call(x, mixed, dq, dk, dv, w_qkv, w_out)
    (attn, grad), own, other = total([part[k] for k in range(3)], (attn, grad))

    up, down, side, corner = split_call(attn, grad)
    halo = (shift(up, -1, 0), shift(down, 1, 0), shift(side, 0, 1), shift(corner, -1, 1))
    block_out, grad_in = merge_call(slide_tokens, grad_tokens, attn, grad, halo)

    core = lax.axis_index("gx") % 2
    grad_wqkv, grad_wout = widen_call(core.astype(jnp.int32).reshape(1), own, other)
    return block_out, grad_in, grad_wqkv, grad_wout


def solution(mesh):
    tile = P("gy", "gx", None)
    return jax.shard_map(
        local,
        mesh=mesh,
        in_specs=(tile, P("gy", "gx"), tile, P(), P()),
        out_specs=(tile, tile, P(), P()),
        check_vma=False,
    )
```

time: 247 us -> 192 us (0.78)
  Pallas kernels: 71.9 us -> 46.8 us
  local copies, waits for them, and re-layouts: 44.3 us -> 23.3 us
  other arithmetic: 20.3 us -> 7.19 us
  waiting for transfers between devices: 67.7 us -> 71.5 us
    pallas_call x1 -> x5, Pallas kernels: 60.8 us -> 40.9 us  [the longest x1 32.8 us: attn_call(): pl.pallas_call(attn_body, grid=(3,), in_specs=[fixed(t) for t in (x, g, k...]
    ppermute x6 -> x8, waiting for transfers between devices: 13.2 us -> 28.2 us  [shift(): return lax.ppermute(v, AXES, pairs)]
    slice x5 -> x1, local copies, waits for them, and re-layouts: 15.3 us -> 3.8 us  [local(): (attn, grad), own, other = total([part[k] for k in range(3)], (attn, grad))]
    ppermute x28, waiting for transfers between devices: 54.5 us -> 43.3 us  [exchange(): return lax.ppermute(v, AXES, pairs)]
    transpose x3 -> x0, local copies, waits for them, and re-layouts: 6.72 us -> none  [the longest x1 6.41 us: local(): whole[:, :D].reshape(3, D, 3, GD).transpose(1, 2, 0, 3).reshape(D, 3 * D)]
    pallas_call x1, Pallas kernels: 11.1 us -> 5.93 us  [finish_call(): pl.pallas_call(finish_body, grid=(tokens // tile,), in_specs=[t, t, t, t,...]
    ppermute x28, starting transfers between devices: 23.8 us -> 28.8 us  [exchange(): return lax.ppermute(v, AXES, pairs)]
    another operation x2 -> x0, other arithmetic: 3.91 us -> none  [local(): xg = jnp.stack([slide_tokens, grad_tokens])]
  transfers between devices with their start and end apart: 34 -> 36, of which waited for: 19 -> 23; matrix products, arithmetic and copies ran while one was open for 8% -> 4% of each run, Pallas kernels for 5% -> 4%
where the time goes in v2:
time: 192 us; the launch traced here: 191 us
  waiting for transfers between devices  71.5 us (37%)
  Pallas kernels  46.8 us (24%)
  starting transfers between devices  40.7 us (21%)
  local copies, waits for them, and re-layouts  23.3 us (12%)
  other arithmetic  7.19 us (4%)
    ppermute x28, waiting for transfers between devices, exchange(): return lax.ppermute(v, AXES, pairs)  43.3 us
    pallas_call x1, Pallas kernels, attn_call(): pl.pallas_call(attn_body, grid=(3,), in_specs=[fixed(t) for t in (x, g, k...  32.8 us
    ppermute x28, starting transfers between devices, exchange(): return lax.ppermute(v, AXES, pairs)  28.8 us
    ppermute x8, waiting for transfers between devices, shift(): return lax.ppermute(v, AXES, pairs)  28.2 us
    unnamed x48, local copies, waits for them, and re-layouts  14.1 us
    ppermute x8, starting transfers between devices, shift(): return lax.ppermute(v, AXES, pairs)  11.9 us
    pallas_call x1, Pallas kernels, finish_call(): pl.pallas_call(finish_body, grid=(tokens // tile,), in_specs=[t, t, t, t,...  5.93 us
    dynamic_slice x13, local copies, waits for them, and re-layouts, scatter_half(): send = lax.dynamic_slice_in_dim(v, (1 - b) * n, n, 0)  5.2 us
  transfers between devices with their start and end apart: 36, of which 23 were waited for; matrix products, arithmetic and copies ran while one was open for 4% of the time, Pallas kernels for 4%

profile of v2, /device:TPU:0, one launch (start us, length us, event | category | flops | bytes accessed | tf_op | source)
XLA Modules:
  0.0 190.6 jit_solution(15176470998820771008)
XLA Ops:
  5.4 4.2 %collective-permute-start = (bf16[4,32,1664]{2,1,0:T(8,128)(2,1)}, bf16[4,32,1664]{2,1,0:T(8,128)(2,1)S(1)}, u32[]{:S(2)}, u32[]{:S(2)}) collective-permute-start(bf16[4,32,1664]{2,1,0:T(8,128)(2,1)} %get-tuple-element.29), channel_id=1, source_target_pairs={{0,7},{1,0},{2,1},{3,2},{4,3},{5,4},{6,5},{7,6},{8,15},{9,8},{10,9... | collective-permute-start | bytes 1277960 | tf_op jit(solution)/shard_map/ppermute | solution.py:457
  9.6 5.2 %collective-permute-start.2 = (bf16[16,8,1664]{2,1,0:T(8,128)(2,1)S(1)}, bf16[16,8,1664]{2,1,0:T(8,128)(2,1)S(1)}, u32[]{:S(2)}, u32[]{:S(2)}) collective-permute-start(bf16[16,8,1664]{2,1,0:T(8,128)(2,1)S(1)} %get-tuple-element.31), channel_id=1, source_target_pairs={{0,120},{1,121},{2,122},{3,123},{4,124},{5,125},{6,126},{7,127},{8... | collective-permute-start | bytes 1277960 | tf_op jit(solution)/shard_map/ppermute | solution.py:457
  14.8 9.1 %collective-permute-done.3.corner = bf16[4,8,1664]{2,1,0:T(8,128)(2,1)S(1)} collective-permute-done((bf16[4,8,1664]{2,1,0:T(8,128)(2,1)S(1)}, bf16[4,8,1664]{2,1,0:T(8,128)(2,1)S(1)}, u32[]{:S(2)}, u32[]{:S(2)}) %collective-permute-start.3) | collective-permute-done | bytes 106528 | tf_op jit(solution)/shard_map/ppermute | solution.py:457
  24.3 32.8 %attention.1 = (bf16[1024,768]{1,0:T(8,128)(2,1)S(1)}, bf16[1024,768]{1,0:T(8,128)(2,1)S(1)}, bf16[1024,768]{1,0:T(8,128)(2,1)}, bf16[1024,768]{1,0:T(8,128)(2,1...) custom-call(bf16[16,64,768]{2,1,0:T(8,128)(2,1)} %x_ref.3, bf16[16,64,768]{2,1,0:T(8,128)(2,1)} %g_ref.3, ...), custom_call_target="tpu_custom_call" | custom-call | flops 14000000000 | bytes 20000000 | tf_op jit(solution)/shard_map/attention/pallas_call | solution.py:212
  57.1 3.8 %fusion.3 = (bf16[1,1024,768]{2,1,0:T(8,128)(2,1)S(1)}, bf16[1,1024,768]{2,1,0:T(8,128)(2,1)S(1)}, bf16[1,1024,768]{2,1,0:T(8,128)(2,1)S(1)}) fusion(bf16[3,1024,768]{2,1,0:T(8,128)(2,1)} %get-tuple-element.33), kind=kLoop, calls=%fused_computation.42 | loop fusion | bytes 9437184 | tf_op jit(solution)/shard_map/slice | solution.py:466
  63.4 2.0 %collective-permute-start.4 = (bf16[512,768]{1,0:T(8,128)(2,1)}, bf16[512,768]{1,0:T(8,128)(2,1)}, u32[]{:S(2)}, u32[]{:S(2)}) collective-permute-start(bf16[512,768]{1,0:T(8,128)(2,1)} %dynamic-slice_bitcast_fusion.2), channel_id=1, source_target_pairs={{0,8},{1,9},{2,10},{3,11},{4,12},{5,13},{6,14},{7,15},{8,0},{9,1},... | collective-permute-start | bytes 2359304 | tf_op jit(solution)/shard_map/ppermute | solution.py:402
  67.2 2.0 %copy-done.4 = bf16[768,2304]{1,0:T(8,128)(2,1)S(1)} copy-done((bf16[768,2304]{1,0:T(8,128)(2,1)S(1)}, bf16[768,2304]{1,0:T(8,128)(2,1)}, u32[]{:S(2)}) %copy-start.4) | copy-done | bytes 3538968
  69.2 1.4 copy-done.10
  74.9 5.9 %finish.1 = (bf16[1024,768]{1,0:T(8,128)(2,1)S(1)}, bf16[1024,768]{1,0:T(8,128)(2,1)S(1)}) custom-call(bf16[1024,768]{1,0:T(8,128)(2,1)S(1)} %copy-done.13, bf16[1024,768]{1,0:T(8,128)(2,1)S(1)} %copy-done.8, bf16[1024,768]{1,0:T(8,128)(2,1)S(1)} %copy-done.10, bf16[1024,768]{1,0:T(8,128)(2,1)S(1)} %copy-done.11, bf16[1024,768]{1,0:T(8,128)(2,1)S(1)} %copy-done.12, ...), custom_call_target="tpu_custom_call" | custom-call | flops 4800000000 | bytes 16000000 | tf_op jit(solution)/shard_map/finish/pallas_call | solution.py:258
  80.8 2.3 %fusion.2 = bf16[512,768]{1,0:T(8,128)(2,1)} fusion(bf16[512,768]{1,0:T(8,128)(2,1)} %collective-permute-done.4, bf16[1,1024,768]{2,1,0:T(8,128)(2,1)S(1)} %copy-done.19, s32[]{:T(128)S(6)} %select_n.277), kind=kLoop, calls=%fused_computation.5 | loop fusion | flops 1572864 | bytes 2359300 | tf_op jit(solution)/shard_map/convert_element_type | solution.py:417
  87.9 1.7 collective-permute-start.14
  90.7 4.0 %collective-permute-done.17 = bf16[256,768]{1,0:T(8,128)(2,1)S(1)} collective-permute-done((bf16[256,768]{1,0:T(8,128)(2,1)}, bf16[256,768]{1,0:T(8,128)(2,1)S(1)}, u32[]{:S(2)}, u32[]{:S(2)}) %collective-permute-start.17) | collective-permute-done | bytes 393248 | tf_op jit(solution)/shard_map/ppermute | solution.py:402
  95.9 2.0 %collective-permute-start.15 = (bf16[128,768]{1,0:T(8,128)(2,1)S(1)}, bf16[128,768]{1,0:T(8,128)(2,1)S(1)}, u32[]{:S(2)}, u32[]{:S(2)}) collective-permute-start(bf16[128,768]{1,0:T(8,128)(2,1)S(1)} %constant_dynamic-slice_fusion.5), channel_id=1, source_target_pairs={{0,4},{1,5},{2,6},{3,7},{4,0},{5,1},{6,2},{7,3},{8,76},{9,77},{10,... | collective-permute-start | bytes 589832 | tf_op jit(solution)/shard_map/ppermute | solution.py:402
  100.8 1.7 collective-permute-start.19
  104.5 2.0 %collective-permute-start.13 = (bf16[64,768]{1,0:T(8,128)(2,1)S(1)}, bf16[64,768]{1,0:T(8,128)(2,1)S(1)}, u32[]{:S(2)}, u32[]{:S(2)}) collective-permute-start(bf16[64,768]{1,0:T(8,128)(2,1)S(1)} %constant_dynamic-slice_fusion.7), channel_id=1, source_target_pairs={{0,4},{1,5},{2,6},{3,7},{4,0},{5,1},{6,2},{7,3},{8,76},{9,77},{10,... | collective-permute-start | bytes 294920 | tf_op jit(solution)/shard_map/ppermute | solution.py:402
  107.3 1.9 collective-permute-done.13
  110.5 6.0 %collective-permute-done.20 = bf16[96,768]{1,0:T(8,128)(2,1)} collective-permute-done((bf16[96,768]{1,0:T(8,128)(2,1)}, bf16[96,768]{1,0:T(8,128)(2,1)}, u32[]{:S(2)}, u32[]{:S(2)}) %collective-permute-start.20) | collective-permute-done | bytes 147488 | tf_op jit(solution)/shard_map/ppermute | solution.py:402
  117.5 6.4 %collective-permute-start.21 = (bf16[96,768]{1,0:T(8,128)(2,1)S(1)}, bf16[96,768]{1,0:T(8,128)(2,1)S(1)}, u32[]{:S(2)}, u32[]{:S(2)}) collective-permute-start(bf16[96,768]{1,0:T(8,128)(2,1)S(1)} %add_convert_fusion.8), channel_id=1, source_target_pairs={{0,48},{1,49},{2,50},{3,51},{4,52},{5,53},{6,54},{7,55},{8,24},{9,... | collective-permute-start | bytes 442376 | tf_op jit(solution)/shard_map/ppermute | solution.py:402
  123.9 3.1 %collective-permute-done.21 = bf16[96,768]{1,0:T(8,128)(2,1)S(1)} collective-permute-done((bf16[96,768]{1,0:T(8,128)(2,1)S(1)}, bf16[96,768]{1,0:T(8,128)(2,1)S(1)}, u32[]{:S(2)}, u32[]{:S(2)}) %collective-permute-start.21) | collective-permute-done | bytes 147488 | tf_op jit(solution)/shard_map/ppermute | solution.py:402
  127.0 3.2 %collective-permute-start.22 = (bf16[96,768]{1,0:T(8,128)(2,1)S(1)}, bf16[96,768]{1,0:T(8,128)(2,1)S(1)}, u32[]{:S(2)}, u32[]{:S(2)}) collective-permute-start(bf16[96,768]{1,0:T(8,128)(2,1)S(1)} %add_convert_fusion.7), channel_id=1, source_target_pairs={{0,68},{1,69},{2,70},{3,71},{4,64},{5,65},{6,66},{7,67},{8,12},{9,... | collective-permute-start | bytes 442376 | tf_op jit(solution)/shard_map/ppermute | solution.py:402
  130.3 3.2 %collective-permute-done.22 = bf16[96,768]{1,0:T(8,128)(2,1)S(1)} collective-permute-done((bf16[96,768]{1,0:T(8,128)(2,1)S(1)}, bf16[96,768]{1,0:T(8,128)(2,1)S(1)}, u32[]{:S(2)}, u32[]{:S(2)}) %collective-permute-start.22) | collective-permute-done | bytes 147488 | tf_op jit(solution)/shard_map/ppermute | solution.py:402
  133.6 7.4 %collective-permute-done.23 = bf16[96,768]{1,0:T(8,128)(2,1)S(1)} collective-permute-done((bf16[96,768]{1,0:T(8,128)(2,1)S(1)}, bf16[96,768]{1,0:T(8,128)(2,1)S(1)}, u32[]{:S(2)}, u32[]{:S(2)}) %collective-permute-start.23) | collective-permute-done | bytes 147488 | tf_op jit(solution)/shard_map/ppermute | solution.py:402
  141.9 3.9 %collective-permute-done.24 = bf16[64,768]{1,0:T(8,128)(2,1)S(1)} collective-permute-done((bf16[64,768]{1,0:T(8,128)(2,1)S(1)}, bf16[64,768]{1,0:T(8,128)(2,1)S(1)}, u32[]{:S(2)}, u32[]{:S(2)}) %collective-permute-start.24) | collective-permute-done | bytes 98336 | tf_op jit(solution)/shard_map/ppermute | solution.py:402
  146.5 1.5 collective-permute-start.28
  148.5 3.0 %collective-permute-done.25 = bf16[128,768]{1,0:T(8,128)(2,1)S(1)} collective-permute-done((bf16[128,768]{1,0:T(8,128)(2,1)S(1)}, bf16[128,768]{1,0:T(8,128)(2,1)S(1)}, u32[]{:S(2)}, u32[]{:S(2)}) %collective-permute-start.25) | collective-permute-done | bytes 196640 | tf_op jit(solution)/shard_map/ppermute | solution.py:402
  152.3 1.6 collective-permute-start.29
  154.7 4.9 %collective-permute-done.26 = bf16[256,768]{1,0:T(8,128)(2,1)S(1)} collective-permute-done((bf16[256,768]{1,0:T(8,128)(2,1)S(1)}, bf16[256,768]{1,0:T(8,128)(2,1)S(1)}, u32[]{:S(2)}, u32[]{:S(2)}) %collective-permute-start.26) | collective-permute-done | bytes 393248 | tf_op jit(solution)/shard_map/ppermute | solution.py:402
  163.1 9.1 %collective-permute-done.10.corner = bf16[4,8,1536]{2,1,0:T(8,128)(2,1)S(1)} collective-permute-done((bf16[4,8,1536]{2,1,0:T(8,128)(2,1)S(1)}, bf16[4,8,1536]{2,1,0:T(8,128)(2,1)S(1)}, u32[]{:S(2)}, u32[]{:S(2)}) %collective-permute-start.10) | collective-permute-done | bytes 98336 | tf_op jit(solution)/shard_map/ppermute | solution.py:457
  174.3 5.7 %collective-permute-done.7.below = bf16[4,32,1536]{2,1,0:T(8,128)(2,1)S(1)} collective-permute-done((bf16[4,32,1536]{2,1,0:T(8,128)(2,1)S(1)}, bf16[4,32,1536]{2,1,0:T(8,128)(2,1)S(1)}, u32[]{:S(2)}, u32[]{:S(2)}) %collective-permute-start.7) | collective-permute-done | bytes 393248 | tf_op jit(solution)/shard_map/ppermute | solution.py:457
  180.0 3.5 %collective-permute-done.8.above = bf16[4,32,1536]{2,1,0:T(8,128)(2,1)S(1)} collective-permute-done((bf16[4,32,1536]{2,1,0:T(8,128)(2,1)S(1)}, bf16[4,32,1536]{2,1,0:T(8,128)(2,1)S(1)}, u32[]{:S(2)}, u32[]{:S(2)}) %collective-permute-start.8) | collective-permute-done | bytes 393248 | tf_op jit(solution)/shard_map/ppermute | solution.py:457
  183.5 2.3 %merge.1 = (bf16[16,64,768]{2,1,0:T(8,128)(2,1)}, bf16[16,64,768]{2,1,0:T(8,128)(2,1)}) custom-call(bf16[16,64,768]{2,1,0:T(8,128)(2,1)S(1)} %copy-done.1, bf16[16,64,768]{2,1,0:T(8,128)(2,1)S(1)} %copy-done.3, bf16[1024,768]{1,0:T(8,128)(2,1)S(1)} %get-tuple-element.41.attn_ref, bf16[1024,768]{1,0:T(8,128)(2,1)S(1)} %get-tuple-element.42.grad_ref, ...), custom_call_target="tpu_custom_call" | custom-call | flops 3000000 | bytes 11000000 | tf_op jit(solution)/shard_map/merge/pallas_call | solution.py:295
  185.8 4.7 %widen.1 = (f32[768,2304]{1,0:T(8,128)}, f32[768,768]{1,0:T(8,128)}) custom-call(s32[1]{0:T(128)} %bitcast.6.core_ref, bf16[512,768]{1,0:T(8,128)(2,1)S(1)} %maximum_select_fusion.refs_0_, bf16[512,768]{1,0:T(8,128)(2,1)S(1)} %maximum_select_fusion.1.refs_1_, bf16[512,768]{1,0:T(8,128)(2,1)S(1)} %maximum_select_fusion.2.refs_2_, ...), custom_call_target="tpu_custom_call" | custom-call | bytes 14000000 | tf_op jit(solution)/shard_map/widen/pallas_call | solution.py:357
  (137 shorter events, 38.0 us)
Async XLA Ops:
  5.4 18.6 %collective-permute-start = (bf16[4,32,1664]{2,1,0:T(8,128)(2,1)}, bf16[4,32,1664]{2,1,0:T(8,128)(2,1)S(1)}, u32[]{:S(2)}, u32[]{:S(2)}) collective-permute-start(bf16[4,32,1664]{2,1,0:T(8,128)(2,1)} %get-tuple-element.29), channel_id=1, source_target_pairs={{0,7},{1,0},{2,1},{3,2},{4,3},{5,4},{6,5},{7,6},{8,15},{9,8},{10,9... | collective-permute-start | bytes 1277960 | tf_op jit(solution)/shard_map/ppermute | solution.py:457
  9.6 14.7 %collective-permute-start.1 = (bf16[4,32,1664]{2,1,0:T(8,128)(2,1)}, bf16[4,32,1664]{2,1,0:T(8,128)(2,1)S(1)}, u32[]{:S(2)}, u32[]{:S(2)}) collective-permute-start(bf16[4,32,1664]{2,1,0:T(8,128)(2,1)} %get-tuple-element.30), channel_id=1, source_target_pairs={{0,1},{1,2},{2,3},{3,4},{4,5},{5,6},{6,7},{7,0},{8,9},{9,10},{10,1... | collective-permute-start | bytes 1277960 | tf_op jit(solution)/shard_map/ppermute | solution.py:457
  9.6 14.7 %collective-permute-start.2 = (bf16[16,8,1664]{2,1,0:T(8,128)(2,1)S(1)}, bf16[16,8,1664]{2,1,0:T(8,128)(2,1)S(1)}, u32[]{:S(2)}, u32[]{:S(2)}) collective-permute-start(bf16[16,8,1664]{2,1,0:T(8,128)(2,1)S(1)} %get-tuple-element.31), channel_id=1, source_target_pairs={{0,120},{1,121},{2,122},{3,123},{4,124},{5,125},{6,126},{7,127},{8... | collective-permute-start | bytes 1277960 | tf_op jit(solution)/shard_map/ppermute | solution.py:457
  14.8 9.2 %collective-permute-start.3 = (bf16[4,8,1664]{2,1,0:T(8,128)(2,1)S(1)}, bf16[4,8,1664]{2,1,0:T(8,128)(2,1)S(1)}, u32[]{:S(2)}, u32[]{:S(2)}) collective-permute-start(bf16[4,8,1664]{2,1,0:T(8,128)(2,1)S(1)} %get-tuple-element.32), channel_id=1, source_target_pairs={{0,121},{1,122},{2,123},{3,124},{4,125},{5,126},{6,127},{7,120},{8... | collective-permute-start | bytes 319496 | tf_op jit(solution)/shard_map/ppermute | solution.py:457
  63.4 17.4 %collective-permute-start.4 = (bf16[512,768]{1,0:T(8,128)(2,1)}, bf16[512,768]{1,0:T(8,128)(2,1)}, u32[]{:S(2)}, u32[]{:S(2)}) collective-permute-start(bf16[512,768]{1,0:T(8,128)(2,1)} %dynamic-slice_bitcast_fusion.2), channel_id=1, source_target_pairs={{0,8},{1,9},{2,10},{3,11},{4,12},{5,13},{6,14},{7,15},{8,0},{9,1},... | collective-permute-start | bytes 2359304 | tf_op jit(solution)/shard_map/ppermute | solution.py:402
  65.5 17.6 %collective-permute-start.5 = (bf16[512,768]{1,0:T(8,128)(2,1)S(1)}, bf16[512,768]{1,0:T(8,128)(2,1)S(1)}, u32[]{:S(2)}, u32[]{:S(2)}) collective-permute-start(bf16[512,768]{1,0:T(8,128)(2,1)S(1)} %dynamic-slice_bitcast_fusion.1), channel_id=1, source_target_pairs={{0,8},{1,9},{2,10},{3,11},{4,12},{5,13},{6,14},{7,15},{8,0},{9,1},... | collective-permute-start | bytes 2359304 | tf_op jit(solution)/shard_map/ppermute | solution.py:402
  65.7 18.5 %collective-permute-start.6 = (bf16[512,768]{1,0:T(8,128)(2,1)S(1)}, bf16[512,768]{1,0:T(8,128)(2,1)S(1)}, u32[]{:S(2)}, u32[]{:S(2)}) collective-permute-start(bf16[512,768]{1,0:T(8,128)(2,1)S(1)} %dynamic-slice_bitcast_fusion), channel_id=1, source_target_pairs={{0,8},{1,9},{2,10},{3,11},{4,12},{5,13},{6,14},{7,15},{8,0},{9,1},... | collective-permute-start | bytes 2359304 | tf_op jit(solution)/shard_map/ppermute | solution.py:402
  86.7 8.0 %collective-permute-start.17 = (bf16[256,768]{1,0:T(8,128)(2,1)}, bf16[256,768]{1,0:T(8,128)(2,1)S(1)}, u32[]{:S(2)}, u32[]{:S(2)}) collective-permute-start(bf16[256,768]{1,0:T(8,128)(2,1)} %constant_dynamic-slice_fusion.3), channel_id=1, source_target_pairs={{0,4},{1,5},{2,6},{3,7},{4,0},{5,1},{6,2},{7,3},{8,76},{9,77},{10,... | collective-permute-start | bytes 1179656 | tf_op jit(solution)/shard_map/ppermute | solution.py:402
  87.9 7.9 %collective-permute-start.14 = (bf16[256,768]{1,0:T(8,128)(2,1)S(1)}, bf16[256,768]{1,0:T(8,128)(2,1)S(1)}, u32[]{:S(2)}, u32[]{:S(2)}) collective-permute-start(bf16[256,768]{1,0:T(8,128)(2,1)S(1)} %constant_dynamic-slice_fusion.6), channel_id=1, source_target_pairs={{0,16},{1,17},{2,18},{3,19},{4,20},{5,21},{6,22},{7,23},{8,56},{9,... | collective-permute-start | bytes 1179656 | tf_op jit(solution)/shard_map/ppermute | solution.py:402
  90.6 7.9 %collective-permute-start.11 = (bf16[256,768]{1,0:T(8,128)(2,1)S(1)}, bf16[256,768]{1,0:T(8,128)(2,1)S(1)}, u32[]{:S(2)}, u32[]{:S(2)}) collective-permute-start(bf16[256,768]{1,0:T(8,128)(2,1)S(1)} %constant_dynamic-slice_fusion.9), channel_id=1, source_target_pairs={{0,1},{1,0},{2,3},{3,2},{4,5},{5,4},{6,7},{7,6},{8,11},{9,10},{10,... | collective-permute-start | bytes 1179656 | tf_op jit(solution)/shard_map/ppermute | solution.py:402
  94.8 5.9 %collective-permute-start.18 = (bf16[128,768]{1,0:T(8,128)(2,1)S(1)}, bf16[128,768]{1,0:T(8,128)(2,1)S(1)}, u32[]{:S(2)}, u32[]{:S(2)}) collective-permute-start(bf16[128,768]{1,0:T(8,128)(2,1)S(1)} %constant_dynamic-slice_fusion.2), channel_id=1, source_target_pairs={{0,1},{1,0},{2,3},{3,2},{4,5},{5,4},{6,7},{7,6},{8,11},{9,10},{10,... | collective-permute-start | bytes 589832 | tf_op jit(solution)/shard_map/ppermute | solution.py:402
  95.9 6.6 %collective-permute-start.15 = (bf16[128,768]{1,0:T(8,128)(2,1)S(1)}, bf16[128,768]{1,0:T(8,128)(2,1)S(1)}, u32[]{:S(2)}, u32[]{:S(2)}) collective-permute-start(bf16[128,768]{1,0:T(8,128)(2,1)S(1)} %constant_dynamic-slice_fusion.5), channel_id=1, source_target_pairs={{0,4},{1,5},{2,6},{3,7},{4,0},{5,1},{6,2},{7,3},{8,76},{9,77},{10,... | collective-permute-start | bytes 589832 | tf_op jit(solution)/shard_map/ppermute | solution.py:402
  98.6 5.7 %collective-permute-start.12 = (bf16[128,768]{1,0:T(8,128)(2,1)S(1)}, bf16[128,768]{1,0:T(8,128)(2,1)S(1)}, u32[]{:S(2)}, u32[]{:S(2)}) collective-permute-start(bf16[128,768]{1,0:T(8,128)(2,1)S(1)} %constant_dynamic-slice_fusion.8), channel_id=1, source_target_pairs={{0,16},{1,17},{2,18},{3,19},{4,20},{5,21},{6,22},{7,23},{8,56},{9,... | collective-permute-start | bytes 589832 | tf_op jit(solution)/shard_map/ppermute | solution.py:402
  100.8 5.6 %collective-permute-start.19 = (bf16[64,768]{1,0:T(8,128)(2,1)S(1)}, bf16[64,768]{1,0:T(8,128)(2,1)S(1)}, u32[]{:S(2)}, u32[]{:S(2)}) collective-permute-start(bf16[64,768]{1,0:T(8,128)(2,1)S(1)} %constant_dynamic-slice_fusion.1), channel_id=1, source_target_pairs={{0,16},{1,17},{2,18},{3,19},{4,20},{5,21},{6,22},{7,23},{8,56},{9,... | collective-permute-start | bytes 294920 | tf_op jit(solution)/shard_map/ppermute | solution.py:402
  109.9 6.7 %collective-permute-start.20 = (bf16[96,768]{1,0:T(8,128)(2,1)}, bf16[96,768]{1,0:T(8,128)(2,1)}, u32[]{:S(2)}, u32[]{:S(2)}) collective-permute-start(bf16[96,768]{1,0:T(8,128)(2,1)} %constant_dynamic-slice_fusion), channel_id=1, source_target_pairs={{0,3},{1,2},{2,1},{3,0},{4,7},{5,6},{6,5},{7,4},{8,9},{9,8},{10,11... | collective-permute-start | bytes 442376 | tf_op jit(solution)/shard_map/ppermute | solution.py:402
  117.5 9.5 %collective-permute-start.21 = (bf16[96,768]{1,0:T(8,128)(2,1)S(1)}, bf16[96,768]{1,0:T(8,128)(2,1)S(1)}, u32[]{:S(2)}, u32[]{:S(2)}) collective-permute-start(bf16[96,768]{1,0:T(8,128)(2,1)S(1)} %add_convert_fusion.8), channel_id=1, source_target_pairs={{0,48},{1,49},{2,50},{3,51},{4,52},{5,53},{6,54},{7,55},{8,24},{9,... | collective-permute-start | bytes 442376 | tf_op jit(solution)/shard_map/ppermute | solution.py:402
  127.0 6.4 %collective-permute-start.22 = (bf16[96,768]{1,0:T(8,128)(2,1)S(1)}, bf16[96,768]{1,0:T(8,128)(2,1)S(1)}, u32[]{:S(2)}, u32[]{:S(2)}) collective-permute-start(bf16[96,768]{1,0:T(8,128)(2,1)S(1)} %add_convert_fusion.7), channel_id=1, source_target_pairs={{0,68},{1,69},{2,70},{3,71},{4,64},{5,65},{6,66},{7,67},{8,12},{9,... | collective-permute-start | bytes 442376 | tf_op jit(solution)/shard_map/ppermute | solution.py:402
  133.5 7.5 %collective-permute-start.23 = (bf16[96,768]{1,0:T(8,128)(2,1)S(1)}, bf16[96,768]{1,0:T(8,128)(2,1)S(1)}, u32[]{:S(2)}, u32[]{:S(2)}) collective-permute-start(bf16[96,768]{1,0:T(8,128)(2,1)S(1)} %add_convert_fusion.6), channel_id=1, source_target_pairs={{0,3},{1,2},{2,1},{3,0},{4,7},{5,6},{6,5},{7,4},{8,9},{9,8},{10,11... | collective-permute-start | bytes 442376 | tf_op jit(solution)/shard_map/ppermute | solution.py:402
  141.8 6.2 %collective-permute-start.30 = (bf16[64,768]{1,0:T(8,128)(2,1)S(1)}, bf16[64,768]{1,0:T(8,128)(2,1)S(1)}, u32[]{:S(2)}, u32[]{:S(2)}) collective-permute-start(bf16[64,768]{1,0:T(8,128)(2,1)S(1)} %get-tuple-element.57), channel_id=1, source_target_pairs={{0,16},{1,17},{2,18},{3,19},{4,20},{5,21},{6,22},{7,23},{8,56},{9,... | collective-permute-start | bytes 294920 | tf_op jit(solution)/shard_map/ppermute | solution.py:402
  145.8 5.7 %collective-permute-start.25 = (bf16[128,768]{1,0:T(8,128)(2,1)S(1)}, bf16[128,768]{1,0:T(8,128)(2,1)S(1)}, u32[]{:S(2)}, u32[]{:S(2)}) collective-permute-start(bf16[128,768]{1,0:T(8,128)(2,1)S(1)} %maximum_select_fusion.7), channel_id=1, source_target_pairs={{0,16},{1,17},{2,18},{3,19},{4,20},{5,21},{6,22},{7,23},{8,56},{9,... | collective-permute-start | bytes 589832 | tf_op jit(solution)/shard_map/ppermute | solution.py:402
  146.5 5.8 %collective-permute-start.28 = (bf16[128,768]{1,0:T(8,128)(2,1)S(1)}, bf16[128,768]{1,0:T(8,128)(2,1)S(1)}, u32[]{:S(2)}, u32[]{:S(2)}) collective-permute-start(bf16[128,768]{1,0:T(8,128)(2,1)S(1)} %maximum_select_fusion.8), channel_id=1, source_target_pairs={{0,4},{1,5},{2,6},{3,7},{4,0},{5,1},{6,2},{7,3},{8,76},{9,77},{10,... | collective-permute-start | bytes 589832 | tf_op jit(solution)/shard_map/ppermute | solution.py:402
  148.0 5.9 %collective-permute-start.31 = (bf16[128,768]{1,0:T(8,128)(2,1)S(1)}, bf16[128,768]{1,0:T(8,128)(2,1)S(1)}, u32[]{:S(2)}, u32[]{:S(2)}) collective-permute-start(bf16[128,768]{1,0:T(8,128)(2,1)S(1)} %maximum_select_fusion.9), channel_id=1, source_target_pairs={{0,1},{1,0},{2,3},{3,2},{4,5},{5,4},{6,7},{7,6},{8,11},{9,10},{10,... | collective-permute-start | bytes 589832 | tf_op jit(solution)/shard_map/ppermute | solution.py:402
  151.7 7.9 %collective-permute-start.26 = (bf16[256,768]{1,0:T(8,128)(2,1)S(1)}, bf16[256,768]{1,0:T(8,128)(2,1)S(1)}, u32[]{:S(2)}, u32[]{:S(2)}) collective-permute-start(bf16[256,768]{1,0:T(8,128)(2,1)S(1)} %maximum_select_fusion.3), channel_id=1, source_target_pairs={{0,1},{1,0},{2,3},{3,2},{4,5},{5,4},{6,7},{7,6},{8,11},{9,10},{10,... | collective-permute-start | bytes 1179656 | tf_op jit(solution)/shard_map/ppermute | solution.py:402
  152.3 7.9 %collective-permute-start.29 = (bf16[256,768]{1,0:T(8,128)(2,1)S(1)}, bf16[256,768]{1,0:T(8,128)(2,1)S(1)}, u32[]{:S(2)}, u32[]{:S(2)}) collective-permute-start(bf16[256,768]{1,0:T(8,128)(2,1)S(1)} %maximum_select_fusion.4), channel_id=1, source_target_pairs={{0,16},{1,17},{2,18},{3,19},{4,20},{5,21},{6,22},{7,23},{8,56},{9,... | collective-permute-start | bytes 1179656 | tf_op jit(solution)/shard_map/ppermute | solution.py:402
  154.0 7.9 %collective-permute-start.32 = (bf16[256,768]{1,0:T(8,128)(2,1)S(1)}, bf16[256,768]{1,0:T(8,128)(2,1)S(1)}, u32[]{:S(2)}, u32[]{:S(2)}) collective-permute-start(bf16[256,768]{1,0:T(8,128)(2,1)S(1)} %maximum_select_fusion.5), channel_id=1, source_target_pairs={{0,4},{1,5},{2,6},{3,7},{4,0},{5,1},{6,2},{7,3},{8,76},{9,77},{10,... | collective-permute-start | bytes 1179656 | tf_op jit(solution)/shard_map/ppermute | solution.py:402
  159.8 26.0 %collective-permute-start.33 = (bf16[512,768]{1,0:T(8,128)(2,1)S(1)}, bf16[512,768]{1,0:T(8,128)(2,1)S(1)}, u32[]{:S(2)}, u32[]{:S(2)}) collective-permute-start(bf16[512,768]{1,0:T(8,128)(2,1)S(1)} %maximum_select_fusion.refs_0_), channel_id=1, source_target_pairs={{0,8},{1,9},{2,10},{3,11},{4,12},{5,13},{6,14},{7,15},{8,0},{9,1},... | collective-permute-start | bytes 2359304 | tf_op jit(solution)/shard_map/ppermute | solution.py:402
  160.5 25.3 %collective-permute-start.34 = (bf16[512,768]{1,0:T(8,128)(2,1)S(1)}, bf16[512,768]{1,0:T(8,128)(2,1)S(1)}, u32[]{:S(2)}, u32[]{:S(2)}) collective-permute-start(bf16[512,768]{1,0:T(8,128)(2,1)S(1)} %maximum_select_fusion.1.refs_1_), channel_id=1, source_target_pairs={{0,8},{1,9},{2,10},{3,11},{4,12},{5,13},{6,14},{7,15},{8,0},{9,1},... | collective-permute-start | bytes 2359304 | tf_op jit(solution)/shard_map/ppermute | solution.py:402
  162.2 23.6 %collective-permute-start.35 = (bf16[512,768]{1,0:T(8,128)(2,1)S(1)}, bf16[512,768]{1,0:T(8,128)(2,1)S(1)}, u32[]{:S(2)}, u32[]{:S(2)}) collective-permute-start(bf16[512,768]{1,0:T(8,128)(2,1)S(1)} %maximum_select_fusion.2.refs_2_), channel_id=1, source_target_pairs={{0,8},{1,9},{2,10},{3,11},{4,12},{5,13},{6,14},{7,15},{8,0},{9,1},... | collective-permute-start | bytes 2359304 | tf_op jit(solution)/shard_map/ppermute | solution.py:402
  162.4 10.9 %collective-permute-start.9 = (bf16[12,8,1536]{2,1,0:T(8,128)(2,1)S(1)}, bf16[12,8,1536]{2,1,0:T(8,128)(2,1)S(1)}, u32[]{:S(2)}, u32[]{:S(2)}) collective-permute-start(bf16[12,8,1536]{2,1,0:T(8,128)(2,1)S(1)} %get-tuple-element.45), channel_id=1, source_target_pairs={{0,8},{1,9},{2,10},{3,11},{4,12},{5,13},{6,14},{7,15},{8,16},{9,17... | collective-permute-start | bytes 884744 | tf_op jit(solution)/shard_map/ppermute | solution.py:457
  162.9 9.3 %collective-permute-start.10 = (bf16[4,8,1536]{2,1,0:T(8,128)(2,1)S(1)}, bf16[4,8,1536]{2,1,0:T(8,128)(2,1)S(1)}, u32[]{:S(2)}, u32[]{:S(2)}) collective-permute-start(bf16[4,8,1536]{2,1,0:T(8,128)(2,1)S(1)} %get-tuple-element.46), channel_id=1, source_target_pairs={{0,15},{1,8},{2,9},{3,10},{4,11},{5,12},{6,13},{7,14},{8,23},{9,16... | collective-permute-start | bytes 294920 | tf_op jit(solution)/shard_map/ppermute | solution.py:457
  172.2 7.8 %collective-permute-start.7 = (bf16[4,32,1536]{2,1,0:T(8,128)(2,1)S(1)}, bf16[4,32,1536]{2,1,0:T(8,128)(2,1)S(1)}, u32[]{:S(2)}, u32[]{:S(2)}) collective-permute-start(bf16[4,32,1536]{2,1,0:T(8,128)(2,1)S(1)} %get-tuple-element.43), channel_id=1, source_target_pairs={{0,7},{1,0},{2,1},{3,2},{4,3},{5,4},{6,5},{7,6},{8,15},{9,8},{10,9... | collective-permute-start | bytes 1179656 | tf_op jit(solution)/shard_map/ppermute | solution.py:457
  173.2 10.3 %collective-permute-start.8 = (bf16[4,32,1536]{2,1,0:T(8,128)(2,1)S(1)}, bf16[4,32,1536]{2,1,0:T(8,128)(2,1)S(1)}, u32[]{:S(2)}, u32[]{:S(2)}) collective-permute-start(bf16[4,32,1536]{2,1,0:T(8,128)(2,1)S(1)} %get-tuple-element.44), channel_id=1, source_target_pairs={{0,1},{1,2},{2,3},{3,4},{4,5},{5,6},{6,7},{7,0},{8,9},{9,10},{10,1... | collective-permute-start | bytes 1179656 | tf_op jit(solution)/shard_map/ppermute | solution.py:457
  (28 other events, 148.6 us)

commit v3 on v2

--- a/solution.py
+++ b/solution.py
@@ -65,7 +65,7 @@
         for j in range(3):
             down[:, 8 * j : 8 * j + 8, lanes] = seam(tile_of(bottom, j + 4), tile_of(bottom, j + 5))
         down[:, 24:32, lanes] = tile_of(bottom, 7)
-        left[:, :, lanes] = strip[...]
+        left[:, :, lanes] = strip[0:12]
         corner[:, :, lanes] = tile_of(bottom, 0)
 
 
@@ -78,14 +78,14 @@
             pl.BlockSpec((4, 64, w), lambda i: (3, 0, 0)),
             pl.BlockSpec((16, 8, w), lambda i: (0, 0, 0)),
         ]
-    shapes = [(4, 32, F), (4, 32, F), (16, 8, F), (4, 8, F)]
+    shapes = [(4, 32, F), (4, 32, F), (12, 8, F), (4, 8, F)]
     return pl.pallas_call(
         pack_body,
         grid=(1,),
         in_specs=specs,
         out_specs=[pl.BlockSpec(sh, lambda i: (0, 0, 0)) for sh in shapes],
         out_shape=[jax.ShapeDtypeStruct(sh, BF16) for sh in shapes],
-        compiler_params=pltpu.CompilerParams(vmem_limit_bytes=16 << 20),
+        compiler_params=pltpu.CompilerParams(vmem_limit_bytes=60 << 20),
         cost_estimate=pl.CostEstimate(flops=0, bytes_accessed=4_000_000, transcendentals=0),
         name="pack",
     )(x, x, x, g, g, g, kb, kb, kb)
@@ -109,8 +109,8 @@
     return out
 
 
-def attn_body(x_ref, g_ref, kb_ref, below, above, right, corner, wq_ref, wk_ref, wv_ref, wo_ref,
-              mixed_ref, dq_ref, dk_ref, dv_ref, xw, part_ref,
+def attn_body(core_ref, x_ref, g_ref, kb_ref, below, above, right, corner, wq_ref, wk_ref, wv_ref, wo_ref,
+              mixed_ref, dq_ref, dk_ref, dv_ref, xw, keep_ref, send_ref,
               gw, bias, hid, hid_t, qs, ks, vs, gm, mix_t):
 
     @pl.when(pl.program_id(0) == 0)
@@ -191,42 +191,44 @@
         rows = pl.ds(pl.multiple_of(i * 128, 128), 128)
         mix_t[:, rows] = jnp.transpose(mixed_ref[rows, :].astype(F32)).astype(BF16)
 
-    @pl.loop(0, 1)
-    def _(i):
-        rows = pl.ds(0, 768)
-        h = hid_t[rows, :]
-        part_ref[0, rows, 0:256] = mm(h, dq_ref[...]).astype(BF16)
-        part_ref[0, rows, 256:512] = mm(h, dk_ref[...]).astype(BF16)
-        part_ref[0, rows, 512:768] = mm(h, dv_ref[...]).astype(BF16)
-
-    for j in range(3):
-        cols = slice(256 * j, 256 * j + 256)
-        part_ref[0, 768:1024, cols] = mm(mix_t[...], gw[:, cols]).astype(BF16)
-
-
-def attn_call(x, g, kb, halo, w_qkv, w_out):
-    fixed = lambda t: pl.BlockSpec(t.shape, lambda i: (0,) * t.ndim, pipeline_mode=pl.Buffered(1))
-    cols = pl.BlockSpec((TOKENS, GD), lambda i: (0, i))
-    wblock = lambda p: pl.BlockSpec((D, GD), lambda i: (0, 3 * p + i))
+    core = core_ref[0]
+    for out, half in ((keep_ref, core), (send_ref, 1 - core)):
+        h = hid_t[pl.ds(pl.multiple_of(half * 384, 128), 384), :]
+        out[0:384, 0:256] = mm(h, dq_ref[...]).astype(BF16)
+        out[0:384, 256:512] = mm(h, dk_ref[...]).astype(BF16)
+        out[0:384, 512:768] = mm(h, dv_ref[...]).astype(BF16)
+        m = mix_t[pl.ds(pl.multiple_of(half * 128, 128), 128), :]
+        out[384:512, :] = mm(m, gw[...]).astype(BF16)
+
+
+def attn_call(core, x, g, kb, halo, w_qkv, w_out):
+    fixed = lambda t: pl.BlockSpec(t.shape, lambda i, c: (0,) * t.ndim, pipeline_mode=pl.Buffered(1))
+    cols = pl.BlockSpec((TOKENS, GD), lambda i, c: (0, i))
+    wblock = lambda p: pl.BlockSpec((D, GD), lambda i, c: (0, 3 * p + i))
+    half = pl.BlockSpec((512, D), lambda i, c: (i, 0))
     tok = jax.ShapeDtypeStruct((TOKENS, D), BF16)
+    halves = jax.ShapeDtypeStruct((1536, D), BF16)
     return pl.pallas_call(
         attn_body,
-        grid=(3,),
-        in_specs=[fixed(t) for t in (x, g, kb, *halo)]
-        + [wblock(0), wblock(1), wblock(2), pl.BlockSpec((GD, D), lambda i: (i, 0))],
-        out_specs=[cols, cols, cols, cols, fixed(tok), pl.BlockSpec((1, 1024, D), lambda i: (i, 0, 0))],
-        out_shape=[tok, tok, tok, tok, tok, jax.ShapeDtypeStruct((3, 1024, D), BF16)],
-        scratch_shapes=[
-            pltpu.VMEM((TOKENS, D), BF16),
-            pltpu.VMEM((TOKENS, 128), F32),
-            pltpu.VMEM((TOKENS, D), BF16),
-            pltpu.VMEM((D, TOKENS), BF16),
-            pltpu.VMEM((TOKENS, GD), BF16),
-            pltpu.VMEM((TOKENS, GD), BF16),
-            pltpu.VMEM((TOKENS, GD), BF16),
-            pltpu.VMEM((TOKENS, GD), BF16),
-            pltpu.VMEM((GD, TOKENS), BF16),
-        ],
+        grid_spec=pltpu.PrefetchScalarGridSpec(
+            num_scalar_prefetch=1,
+            grid=(3,),
+            in_specs=[fixed(t) for t in (x, g, kb, *halo)]
+            + [wblock(0), wblock(1), wblock(2), pl.BlockSpec((GD, D), lambda i, c: (i, 0))],
+            out_specs=[cols, cols, cols, cols, fixed(tok), half, half],
+            scratch_shapes=[
+                pltpu.VMEM((TOKENS, D), BF16),
+                pltpu.VMEM((TOKENS, 128), F32),
+                pltpu.VMEM((TOKENS, D), BF16),
+                pltpu.VMEM((D, TOKENS), BF16),
+                pltpu.VMEM((TOKENS, GD), BF16),
+                pltpu.VMEM((TOKENS, GD), BF16),
+                pltpu.VMEM((TOKENS, GD), BF16),
+                pltpu.VMEM((TOKENS, GD), BF16),
+                pltpu.VMEM((GD, TOKENS), BF16),
+            ],
+        ),
+        out_shape=[tok, tok, tok, tok, tok, halves, halves],
         compiler_params=pltpu.CompilerParams(
             dimension_semantics=("arbitrary",), vmem_limit_bytes=48 << 20
         ),
@@ -234,7 +236,7 @@
             flops=14_000_000_000, bytes_accessed=20_000_000, transcendentals=1_600_000
         ),
         name="attention",
-    )(x, g, kb, *halo, w_qkv, w_qkv, w_qkv, w_out)
+    )(core, x, g, kb, *halo, w_qkv, w_qkv, w_qkv, w_out)
 
 
 def finish_body(x_ref, mixed_ref, dq_ref, dk_ref, dv_ref, wqkv_ref, wo_ref, attn_ref, gs_ref):
@@ -264,7 +266,7 @@
         out_specs=[t, t],
         out_shape=[tok, tok],
         compiler_params=pltpu.CompilerParams(
-            dimension_semantics=("arbitrary",), vmem_limit_bytes=32 << 20
+            dimension_semantics=("arbitrary",), vmem_limit_bytes=60 << 20
         ),
         cost_estimate=pl.CostEstimate(
             flops=4_800_000_000, bytes_accessed=16_000_000, transcendentals=0
@@ -324,44 +326,64 @@
     )(attn, grad)
 
 
-def widen_body(core_ref, *refs):
-    own, other, (wqkv, wout) = refs[0:3], refs[3:6], refs[6:8]
+def combine_body(bits, keep, recv, *outs):
+    for k in range(3):
+        for out, half in ((outs[k], bits[k]), (outs[3 + k], 1 - bits[k])):
+            rows = pl.ds(pl.multiple_of(512 * k + half * 256, 256), 256)
+            out[...] = (keep[rows, :].astype(F32) + recv[rows, :].astype(F32)).astype(BF16)
+
+
+def combine_call(bits, keep, recv):
+    whole = pl.BlockSpec((1536, D), lambda i, c: (0, 0), pipeline_mode=pl.Buffered(1))
+    half = pl.BlockSpec((256, D), lambda i, c: (0, 0), pipeline_mode=pl.Buffered(1))
+    return pl.pallas_call(
+        combine_body,
+        grid_spec=pltpu.PrefetchScalarGridSpec(
+            num_scalar_prefetch=1, grid=(1,), in_specs=[whole] * 2, out_specs=[half] * 6
+        ),
+        out_shape=[jax.ShapeDtypeStruct((256, D), BF16)] * 6,
+        compiler_params=pltpu.CompilerParams(vmem_limit_bytes=16 << 20),
+        cost_estimate=pl.CostEstimate(flops=1_200_000, bytes_accessed=7_000_000, transcendentals=0),
+        name="combine",
+    )(bits, keep, recv)
+
+
+def widen_body(core_ref, own, other, wqkv, wout):
     j = pl.program_id(0)
-    here = core_ref[0]
-
-    def put(srcs):
-        rows = pl.ds(pl.multiple_of(j % 2 * 256, 256), 256)
-
-        @pl.when(j < 3)
-        def _():
-            for k in range(3):
-                for p in range(3):
-                    wqkv[:, D * p + GD * k : D * p + GD * k + GD] = srcs[k][rows, GD * p : GD * p + GD].astype(F32)
-
-        @pl.when(j == 3)
-        def _():
-            for k in range(3):
-                wout[GD * k : GD * k + GD, :] = srcs[k][256:512, :].astype(F32)
-
-    @pl.when(j // 2 == here)
+    core = core_ref[0]
+
+    def put(src):
+        for k in range(3):
+            rows = pl.ds(pl.multiple_of(512 * k + j % 3 * 128, 128), 128)
+            for p in range(3):
+                wqkv[:, D * p + GD * k : D * p + GD * k + GD] = src[rows, GD * p : GD * p + GD].astype(F32)
+
+    @pl.when((j < 6) & (j // 3 == core))
     def _():
         put(own)
 
-    @pl.when(j // 2 != here)
+    @pl.when((j < 6) & (j // 3 != core))
     def _():
         put(other)
 
+    @pl.when(j == 6)
+    def _():
+        for src, half in ((own, core), (other, 1 - core)):
+            for k in range(3):
+                rows = pl.ds(pl.multiple_of(GD * k + half * 128, 128), 128)
+                wout[rows, :] = src[512 * k + 384 : 512 * k + 512, :].astype(F32)
+
 
 def widen_call(core, own, other):
-    half = pl.BlockSpec((512, D), lambda j, c: (0, 0), pipeline_mode=pl.Buffered(1))
+    half = pl.BlockSpec((1536, D), lambda j, c: (0, 0), pipeline_mode=pl.Buffered(1))
     return pl.pallas_call(
         widen_body,
         grid_spec=pltpu.PrefetchScalarGridSpec(
             num_scalar_prefetch=1,
-            grid=(4,),
-            in_specs=[half] * 6,
+            grid=(7,),
+            in_specs=[half] * 2,
             out_specs=[
-                pl.BlockSpec((256, 3 * D), lambda j, c: (jnp.minimum(j, 2), 0)),
+                pl.BlockSpec((128, 3 * D), lambda j, c: (jnp.minimum(j, 5), 0)),
                 pl.BlockSpec((D, D), lambda j, c: (0, 0)),
             ],
         ),
@@ -371,7 +393,8 @@
         ),
         cost_estimate=pl.CostEstimate(flops=0, bytes_accessed=14_000_000, transcendentals=0),
         name="widen",
-    )(core, *own, *other)
+    )(core, own, other)
+
 
 AXES = ("gx", "gy")
 
@@ -431,22 +454,19 @@
     return jnp.where(b == 0, jnp.concatenate([v, o], 0), jnp.concatenate([o, v], 0))
 
 
-def total(parts, gate):
-    order = [["core"] + ["xyz"[(k + s) % 3] for s in range(3)] for k in range(3)]
-    parts = [scatter_half(p, "core") for p in parts]
-    parts, gate = lax.optimization_barrier((parts, gate))
-    for s in range(1, 4):
-        parts = [scatter_half(p, o[s]) for p, o in zip(parts, order)]
-    n = parts[0].shape[0]
-    v = jnp.concatenate(parts, 0)
-    v = scatter_half(v, "x", False)
-    for axis in "yz":
-        v = add(v, exchange(v, axis, False))
-    v = gather_half(v, "x", False)
-    parts = [v[n * k : n * k + n] for k in range(3)]
-    for s in (3, 2, 1):
-        parts = [gather_half(p, o[s]) for p, o in zip(parts, order)]
-    return gate, parts, [exchange(p, "core", True) for p in parts]
+def total(keep, send, gate):
+    axes = [["xyz"[(k + s) % 3] for s in range(3)] for k in range(3)]
+    recv = exchange(send, "core", True)
+    keep, recv, gate = lax.optimization_barrier((keep, recv, gate))
+    bits = jnp.stack([half_of(a[0], True) for a in axes]).astype(jnp.int32)
+    halves = combine_call(bits, keep, recv)
+    parts = [add(halves[k], exchange(halves[3 + k], a[0], True)) for k, a in enumerate(axes)]
+    parts = [scatter_half(p, a[1]) for p, a in zip(parts, axes)]
+    for axis, first in ((2, True), (0, False), (1, False), (2, False)):
+        parts = [add(p, exchange(p, a[axis], first)) for p, a in zip(parts, axes)]
+    for s in (1, 0):
+        parts = [gather_half(p, a[s]) for p, a in zip(parts, axes)]
+    return jnp.concatenate(parts, 0), gate
 
 
 def shift(v, d_gy, d_gx):
@@ -459,19 +479,24 @@
 
 def local(slide_tokens, tissue, grad_tokens, w_qkv, w_out):
     kb = jnp.broadcast_to(tissue.astype(BF16)[..., None], tissue.shape + (128,))
+    core = (lax.axis_index("gx") % 2).astype(jnp.int32).reshape(1)
     up, down, left, corner = pack_call(slide_tokens, grad_tokens, kb)
-    halo = (shift(up, -1, 0), shift(down, 1, 0), shift(left, 0, -1), shift(corner, 1, -1))
-    mixed, dq, dk, dv, x, part = attn_call(slide_tokens, grad_tokens, kb, halo, w_qkv, w_out)
+    corner = shift(corner, 1, -1)
+    left = shift(left, 0, -1)
+    halo = (shift(up, -1, 0), shift(down, 1, 0), left, corner)
+    mixed, dq, dk, dv, x, keep, send = attn_call(core, slide_tokens, grad_tokens, kb, halo, w_qkv, w_out)
     attn, grad = finish_call(x, mixed, dq, dk, dv, w_qkv, w_out)
-    (attn, grad), own, other = total([part[k] for k in range(3)], (attn, grad))
-
-    up, down, side, corner = split_call(attn, grad)
-    halo = (shift(up, -1, 0), shift(down, 1, 0), shift(side, 0, 1), shift(corner, -1, 1))
+    own, (attn, grad) = total(keep, send, (attn, grad))
+
+    own, borders = lax.optimization_barrier((own, tuple(split_call(attn, grad))))
+    up, down, side, corner = borders
+    corner = shift(corner, -1, 1)
+    side = shift(side, 0, 1)
+    halo = (shift(up, -1, 0), shift(down, 1, 0), side, corner)
+    grads = widen_call(core, own, exchange(own, "core", True))
+    halo, grads = lax.optimization_barrier((halo, tuple(grads)))
     block_out, grad_in = merge_call(slide_tokens, grad_tokens, attn, grad, halo)
-
-    core = lax.axis_index("gx") % 2
-    grad_wqkv, grad_wout = widen_call(core.astype(jnp.int32).reshape(1), own, other)
-    return block_out, grad_in, grad_wqkv, grad_wout
+    return block_out, grad_in, *grads
 
 
 def solution(mesh):

time: 192 us -> 162 us (0.84)
  waiting for transfers between devices: 71.5 us -> 43.6 us
  local copies, waits for them, and re-layouts: 23.3 us -> 3.4 us
  Pallas kernels: 46.8 us -> 57.7 us
  starting transfers between devices: 40.7 us -> 46.2 us
  other arithmetic: 7.19 us -> 9.94 us
    ppermute x28 -> x26, waiting for transfers between devices: 43.3 us -> 26.6 us  [exchange(): return lax.ppermute(v, AXES, pairs)]
    unnamed x48 -> x18, local copies, waits for them, and re-layouts: 14.1 us -> 2.43 us
    ppermute x8, waiting for transfers between devices: 28.2 us -> 17 us  [shift(): return lax.ppermute(v, AXES, pairs)]
    select_n x10 -> x6, other arithmetic: 1.32 us -> 6.63 us  [gather_half(): jnp.where(b == 0, jnp.concatenate([v, o], 0), jnp.concatenate([o, v], 0))]
    dynamic_slice x13 -> x3, local copies, waits for them, and re-layouts: 5.2 us -> 0.07 us  [scatter_half(): send = lax.dynamic_slice_in_dim(v, (1 - b) * n, n, 0)]
    pallas_call x1, Pallas kernels: 5.93 us -> 11 us  [finish_call(): pl.pallas_call(finish_body, grid=(tokens // tile,), in_specs=[t, t, t, t,...]
    slice x2 -> x0, local copies, waits for them, and re-layouts: 3.82 us -> none  [the longest x1 3.8 us: local(): (attn, grad), own, other = total([part[k] for k in range(3)], (attn, grad))]
    pallas_call x1 -> x2, Pallas kernels: 32.8 us -> 36.4 us  [the longest x1 32.9 us: attn_call(): pl.pallas_call(attn_body, grid_spec=pltpu.PrefetchScalarGridSpec(num_scal...]
  transfers between devices with their start and end apart: 36 -> 34, of which waited for: 23 -> 19; matrix products, arithmetic and copies ran while one was open for 4% -> 5% of each run, Pallas kernels for 4% -> 10%
where the time goes in v3:
time: 162 us
  Pallas kernels  57.7 us (36%)
  starting transfers between devices  46.2 us (29%)
  waiting for transfers between devices  43.6 us (27%)
  other arithmetic  9.94 us (6%)
  local copies, waits for them, and re-layouts  3.4 us (2%)
    pallas_call x1, Pallas kernels, attn_call(): pl.pallas_call(attn_body, grid_spec=pltpu.PrefetchScalarGridSpec(num_scal...  32.9 us
    ppermute x26, starting transfers between devices, exchange(): return lax.ppermute(v, AXES, pairs)  31.7 us
    ppermute x26, waiting for transfers between devices, exchange(): return lax.ppermute(v, AXES, pairs)  26.6 us
    ppermute x8, waiting for transfers between devices, shift(): return lax.ppermute(v, AXES, pairs)  17 us
    ppermute x8, starting transfers between devices, shift(): return lax.ppermute(v, AXES, pairs)  14.5 us
    pallas_call x1, Pallas kernels, finish_call(): pl.pallas_call(finish_body, grid=(tokens // tile,), in_specs=[t, t, t, t,...  11 us
    select_n x6, other arithmetic, gather_half(): jnp.where(b == 0, jnp.concatenate([v, o], 0), jnp.concatenate([o, v], 0))  6.63 us
    pallas_call x1, Pallas kernels, widen_call(): pl.pallas_call(widen_body, grid_spec=pltpu.PrefetchScalarGridSpec(num_sca...  5.24 us
  transfers between devices with their start and end apart: 34, of which 19 were waited for; matrix products, arithmetic and copies ran while one was open for 5% of the time, Pallas kernels for 10%

profile of v3, /device:TPU:0, one launch (start us, length us, event | category | flops | bytes accessed | tf_op | source)
XLA Modules:
  0.0 161.7 jit_solution(4774534942920621227)
XLA Ops:
  2.2 2.7 %pack.1 = (bf16[4,32,1664]{2,1,0:T(8,128)(2,1)}, bf16[4,32,1664]{2,1,0:T(8,128)(2,1)}, bf16[12,8,1664]{2,1,0:T(8,128)(2,1)}, bf16[4,8,1664]{2,1,0:T(8,128)(2,1)}) custom-call(bf16[16,64,768]{2,1,0:T(8,128)(2,1)} %x_ref.3, bf16[16,64,768]{2,1,0:T(8,128)(2,1)} %x_ref.3, bf16[16,64,768]{2,1,0:T(8,128)(2,1)} %x_ref.3, bf16[16,64,768]{2,1,0:T(8,128)(2,1)} %g_ref.3, ...), custom_call_target="tpu_custom_call" | custom-call | bytes 4000000 | tf_op jit(solution)/shard_map/pack/pallas_call | solution.py:82
  4.9 4.2 %collective-permute-start = (bf16[4,32,1664]{2,1,0:T(8,128)(2,1)}, bf16[4,32,1664]{2,1,0:T(8,128)(2,1)S(1)}, u32[]{:S(2)}, u32[]{:S(2)}) collective-permute-start(bf16[4,32,1664]{2,1,0:T(8,128)(2,1)} %get-tuple-element.46), channel_id=1, source_target_pairs={{0,7},{1,0},{2,1},{3,2},{4,3},{5,4},{6,5},{7,6},{8,15},{9,8},{10,9... | collective-permute-start | bytes 1277960 | tf_op jit(solution)/shard_map/ppermute | solution.py:477
  9.1 5.2 %collective-permute-start.2 = (bf16[12,8,1664]{2,1,0:T(8,128)(2,1)}, bf16[12,8,1664]{2,1,0:T(8,128)(2,1)S(1)}, u32[]{:S(2)}, u32[]{:S(2)}) collective-permute-start(bf16[12,8,1664]{2,1,0:T(8,128)(2,1)} %get-tuple-element.48), channel_id=1, source_target_pairs={{0,120},{1,121},{2,122},{3,123},{4,124},{5,125},{6,126},{7,127},{8... | collective-permute-start | bytes 958472 | tf_op jit(solution)/shard_map/ppermute | solution.py:477
  14.4 9.1 %collective-permute-done.3.corner = bf16[4,8,1664]{2,1,0:T(8,128)(2,1)S(1)} collective-permute-done((bf16[4,8,1664]{2,1,0:T(8,128)(2,1)}, bf16[4,8,1664]{2,1,0:T(8,128)(2,1)S(1)}, u32[]{:S(2)}, u32[]{:S(2)}) %collective-permute-start.3) | collective-permute-done | bytes 106528 | tf_op jit(solution)/shard_map/ppermute | solution.py:477
  23.9 32.9 %attention.1 = (bf16[1024,768]{1,0:T(8,128)(2,1)S(1)}, bf16[1024,768]{1,0:T(8,128)(2,1)S(1)}, bf16[1024,768]{1,0:T(8,128)(2,1)}, bf16[1024,768]{1,0:T(8,128)(2,1...) custom-call(s32[1]{0:T(128)} %bitcast.core_ref, bf16[16,64,768]{2,1,0:T(8,128)(2,1)} %x_ref.3, ...), custom_call_target="tpu_custom_call" | custom-call | flops 14000000000 | bytes 20000000 | tf_op jit(solution)/shard_map/attention/pallas_call | solution.py:211
  59.1 2.0 %collective-permute-start.4 = (bf16[1536,768]{1,0:T(8,128)(2,1)}, bf16[1536,768]{1,0:T(8,128)(2,1)}, u32[]{:S(2)}, u32[]{:S(2)}) collective-permute-start(bf16[1536,768]{1,0:T(8,128)(2,1)} %get-tuple-element.51), channel_id=1, source_target_pairs={{0,8},{1,9},{2,10},{3,11},{4,12},{5,13},{6,14},{7,15},{8,0},{9,1},... | collective-permute-start | bytes 7077896 | tf_op jit(solution)/shard_map/ppermute | solution.py:425
  61.2 11.0 %finish.1 = (bf16[1024,768]{1,0:T(8,128)(2,1)}, bf16[1024,768]{1,0:T(8,128)(2,1)}) custom-call(bf16[1024,768]{1,0:T(8,128)(2,1)} %get-tuple-element.52.x_ref, bf16[1024,768]{1,0:T(8,128)(2,1)} %copy-done.7, bf16[1024,768]{1,0:T(8,128)(2,1)} %copy-done.8, bf16[1024,768]{1,0:T(8,128)(2,1)} %get-tuple-element.55.dk_ref, ...), custom_call_target="tpu_custom_call" | custom-call | flops 4800000000 | bytes 16000000 | tf_op jit(solution)/shard_map/finish/pallas_call | solution.py:260
  72.2 3.5 %combine.1 = (bf16[256,768]{1,0:T(8,128)(2,1)S(1)}, bf16[256,768]{1,0:T(8,128)(2,1)S(1)}, bf16[256,768]{1,0:T(8,128)(2,1)S(1)}, bf16[256,768]{1,0:T(8,128)(2,1)}...) custom-call(s32[3]{0:T(128)S(1)} %pad_add_fusion.bits, bf16[1536,768]{1,0:T(8,128)(2,1)S(1)} %copy-done.5, ...), custom_call_target="tpu_custom_call" | custom-call | flops 1200000 | bytes 7000000 | tf_op jit(solution)/shard_map/combine/pallas_call | solution.py:339
  75.8 1.6 collective-permute-start.13
  77.5 6.3 %collective-permute-done.5 = bf16[256,768]{1,0:T(8,128)(2,1)S(1)} collective-permute-done((bf16[256,768]{1,0:T(8,128)(2,1)}, bf16[256,768]{1,0:T(8,128)(2,1)S(1)}, u32[]{:S(2)}, u32[]{:S(2)}) %collective-permute-start.5) | collective-permute-done | bytes 393248 | tf_op jit(solution)/shard_map/ppermute | solution.py:425
  83.9 1.7 %collective-permute-start.6 = (bf16[128,768]{1,0:T(8,128)(2,1)S(1)}, bf16[128,768]{1,0:T(8,128)(2,1)S(1)}, u32[]{:S(2)}, u32[]{:S(2)}) collective-permute-start(bf16[128,768]{1,0:T(8,128)(2,1)S(1)} %constant_dynamic-slice_fusion.2), channel_id=1, source_target_pairs={{0,16},{1,17},{2,18},{3,19},{4,20},{5,21},{6,22},{7,23},{8,56},{9,... | collective-permute-start | bytes 589832 | tf_op jit(solution)/shard_map/ppermute | solution.py:425
  87.4 2.3 %collective-permute-done.6 = bf16[128,768]{1,0:T(8,128)(2,1)S(1)} collective-permute-done((bf16[128,768]{1,0:T(8,128)(2,1)S(1)}, bf16[128,768]{1,0:T(8,128)(2,1)S(1)}, u32[]{:S(2)}, u32[]{:S(2)}) %collective-permute-start.6) | collective-permute-done | bytes 196640 | tf_op jit(solution)/shard_map/ppermute | solution.py:425
  91.9 1.7 %collective-permute-start.23 = (bf16[128,768]{1,0:T(8,128)(2,1)S(1)}, bf16[128,768]{1,0:T(8,128)(2,1)S(1)}, u32[]{:S(2)}, u32[]{:S(2)}) collective-permute-start(bf16[128,768]{1,0:T(8,128)(2,1)S(1)} %add_convert_fusion.7), channel_id=1, source_target_pairs={{0,16},{1,17},{2,18},{3,19},{4,20},{5,21},{6,22},{7,23},{8,56},{9,... | collective-permute-start | bytes 589832 | tf_op jit(solution)/shard_map/ppermute | solution.py:425
  93.5 2.1 %collective-permute-done.7 = bf16[128,768]{1,0:T(8,128)(2,1)S(1)} collective-permute-done((bf16[128,768]{1,0:T(8,128)(2,1)S(1)}, bf16[128,768]{1,0:T(8,128)(2,1)S(1)}, u32[]{:S(2)}, u32[]{:S(2)}) %collective-permute-start.7) | collective-permute-done | bytes 196640 | tf_op jit(solution)/shard_map/ppermute | solution.py:425
  97.3 5.3 %collective-permute-start.16 = (bf16[128,768]{1,0:T(8,128)(2,1)S(1)}, bf16[128,768]{1,0:T(8,128)(2,1)S(1)}, u32[]{:S(2)}, u32[]{:S(2)}) collective-permute-start(bf16[128,768]{1,0:T(8,128)(2,1)S(1)} %add_convert_fusion.11), channel_id=1, source_target_pairs={{0,48},{1,49},{2,50},{3,51},{4,52},{5,53},{6,54},{7,55},{8,24},{9,... | collective-permute-start | bytes 589832 | tf_op jit(solution)/shard_map/ppermute | solution.py:425
  102.7 2.6 %collective-permute-start.24 = (bf16[128,768]{1,0:T(8,128)(2,1)S(1)}, bf16[128,768]{1,0:T(8,128)(2,1)S(1)}, u32[]{:S(2)}, u32[]{:S(2)}) collective-permute-start(bf16[128,768]{1,0:T(8,128)(2,1)S(1)} %add_convert_fusion.6), channel_id=1, source_target_pairs={{0,68},{1,69},{2,70},{3,71},{4,64},{5,65},{6,66},{7,67},{8,12},{9,... | collective-permute-start | bytes 589832 | tf_op jit(solution)/shard_map/ppermute | solution.py:425
  105.3 2.2 %collective-permute-start.9 = (bf16[128,768]{1,0:T(8,128)(2,1)S(1)}, bf16[128,768]{1,0:T(8,128)(2,1)S(1)}, u32[]{:S(2)}, u32[]{:S(2)}) collective-permute-start(bf16[128,768]{1,0:T(8,128)(2,1)S(1)} %add_convert_fusion.15), channel_id=1, source_target_pairs={{0,48},{1,49},{2,50},{3,51},{4,52},{5,53},{6,54},{7,55},{8,24},{9,... | collective-permute-start | bytes 589832 | tf_op jit(solution)/shard_map/ppermute | solution.py:425
  107.6 2.6 %collective-permute-start.17 = (bf16[128,768]{1,0:T(8,128)(2,1)S(1)}, bf16[128,768]{1,0:T(8,128)(2,1)S(1)}, u32[]{:S(2)}, u32[]{:S(2)}) collective-permute-start(bf16[128,768]{1,0:T(8,128)(2,1)S(1)} %add_convert_fusion.10), channel_id=1, source_target_pairs={{0,68},{1,69},{2,70},{3,71},{4,64},{5,65},{6,66},{7,67},{8,12},{9,... | collective-permute-start | bytes 589832 | tf_op jit(solution)/shard_map/ppermute | solution.py:425
  112.4 1.5 collective-permute-start.10
  117.3 2.0 %collective-permute-start.26 = (bf16[128,768]{1,0:T(8,128)(2,1)S(1)}, bf16[128,768]{1,0:T(8,128)(2,1)S(1)}, u32[]{:S(2)}, u32[]{:S(2)}) collective-permute-start(bf16[128,768]{1,0:T(8,128)(2,1)S(1)} %add_convert_fusion.4), channel_id=1, source_target_pairs={{0,48},{1,49},{2,50},{3,51},{4,52},{5,53},{6,54},{7,55},{8,24},{9,... | collective-permute-start | bytes 589832 | tf_op jit(solution)/shard_map/ppermute | solution.py:425
  119.8 1.8 %collective-permute-done.18 = bf16[128,768]{1,0:T(8,128)(2,1)S(1)} collective-permute-done((bf16[128,768]{1,0:T(8,128)(2,1)S(1)}, bf16[128,768]{1,0:T(8,128)(2,1)S(1)}, u32[]{:S(2)}, u32[]{:S(2)}) %collective-permute-start.18) | collective-permute-done | bytes 196640 | tf_op jit(solution)/shard_map/ppermute | solution.py:425
  122.4 1.9 %collective-permute-done.26 = bf16[128,768]{1,0:T(8,128)(2,1)S(1)} collective-permute-done((bf16[128,768]{1,0:T(8,128)(2,1)S(1)}, bf16[128,768]{1,0:T(8,128)(2,1)S(1)}, u32[]{:S(2)}, u32[]{:S(2)}) %collective-permute-start.26) | collective-permute-done | bytes 196640 | tf_op jit(solution)/shard_map/ppermute | solution.py:425
  125.2 2.0 %collective-permute-start.12 = (bf16[256,768]{1,0:T(8,128)(2,1)S(1)}, bf16[256,768]{1,0:T(8,128)(2,1)}, u32[]{:S(2)}, u32[]{:S(2)}) collective-permute-start(bf16[256,768]{1,0:T(8,128)(2,1)S(1)} %maximum_select_fusion.3), channel_id=1, source_target_pairs={{0,1},{1,0},{2,3},{3,2},{4,5},{5,4},{6,7},{7,6},{8,11},{9,10},{10,... | collective-permute-start | bytes 1179656 | tf_op jit(solution)/shard_map/ppermute | solution.py:425
  128.3 2.1 %maximum_select_fusion.4 = bf16[256,768]{1,0:T(8,128)(2,1)} fusion(bf16[128,768]{1,0:T(8,128)(2,1)} %collective-permute-done.19, bf16[128,768]{1,0:T(8,128)(2,1)} %add_convert_fusion.8, pred[]{:T(512)S(6)} %eq.93), kind=kLoop, calls=%fused_computation.8 | loop fusion | flops 1769472 | bytes 786433 | tf_op jit(solution)/shard_map/jit(_where)/select_n | solution.py:454
  133.3 1.9 %collective-permute-done.12 = bf16[256,768]{1,0:T(8,128)(2,1)} collective-permute-done((bf16[256,768]{1,0:T(8,128)(2,1)S(1)}, bf16[256,768]{1,0:T(8,128)(2,1)}, u32[]{:S(2)}, u32[]{:S(2)}) %collective-permute-start.12) | collective-permute-done | bytes 393248 | tf_op jit(solution)/shard_map/ppermute | solution.py:425
  136.5 2.0 %collective-permute-done.20 = bf16[256,768]{1,0:T(8,128)(2,1)} collective-permute-done((bf16[256,768]{1,0:T(8,128)(2,1)}, bf16[256,768]{1,0:T(8,128)(2,1)}, u32[]{:S(2)}, u32[]{:S(2)}) %collective-permute-start.20) | collective-permute-done | bytes 393248 | tf_op jit(solution)/shard_map/ppermute | solution.py:425
  138.5 1.6 maximum_select_fusion.1
  141.7 2.0 %collective-permute-start.30 = (bf16[4,32,1536]{2,1,0:T(8,128)(2,1)S(1)}, bf16[4,32,1536]{2,1,0:T(8,128)(2,1)S(1)}, u32[]{:S(2)}, u32[]{:S(2)}) collective-permute-start(bf16[4,32,1536]{2,1,0:T(8,128)(2,1)S(1)} %get-tuple-element.74), channel_id=1, source_target_pairs={{0,1},{1,2},{2,3},{3,4},{4,5},{5,6},{6,7},{7,0},{8,9},{9,10},{10,1... | collective-permute-start | bytes 1179656 | tf_op jit(solution)/shard_map/ppermute | solution.py:477
  143.7 2.9 %collective-permute-start.32 = (bf16[4,8,1536]{2,1,0:T(8,128)(2,1)S(1)}, bf16[4,8,1536]{2,1,0:T(8,128)(2,1)S(1)}, u32[]{:S(2)}, u32[]{:S(2)}) collective-permute-start(bf16[4,8,1536]{2,1,0:T(8,128)(2,1)S(1)} %get-tuple-element.76), channel_id=1, source_target_pairs={{0,15},{1,8},{2,9},{3,10},{4,11},{5,12},{6,13},{7,14},{8,23},{9,16... | collective-permute-start | bytes 294920 | tf_op jit(solution)/shard_map/ppermute | solution.py:477
  146.6 5.2 %widen.1 = (f32[768,2304]{1,0:T(8,128)}, f32[768,768]{1,0:T(8,128)}) custom-call(s32[1]{0:T(128)} %bitcast.core_ref, bf16[1536,768]{1,0:T(8,128)(2,1)S(1)} %pad_maximum_fusion.own, bf16[1536,768]{1,0:T(8,128)(2,1)S(1)} %collective-permute-done.33.other), custom_call_target="tpu_custom_call" | custom-call | bytes 14000000 | tf_op jit(solution)/shard_map/widen/pallas_call | solution.py:379
  151.9 7.1 %collective-permute-done.32.corner = bf16[4,8,1536]{2,1,0:T(8,128)(2,1)S(1)} collective-permute-done((bf16[4,8,1536]{2,1,0:T(8,128)(2,1)S(1)}, bf16[4,8,1536]{2,1,0:T(8,128)(2,1)S(1)}, u32[]{:S(2)}, u32[]{:S(2)}) %collective-permute-start.32) | collective-permute-done | bytes 98336 | tf_op jit(solution)/shard_map/ppermute | solution.py:477
  159.4 2.3 %merge.1 = (bf16[16,64,768]{2,1,0:T(8,128)(2,1)}, bf16[16,64,768]{2,1,0:T(8,128)(2,1)}) custom-call(bf16[16,64,768]{2,1,0:T(8,128)(2,1)S(1)} %copy-done, bf16[16,64,768]{2,1,0:T(8,128)(2,1)S(1)} %copy-done.1, bf16[1024,768]{1,0:T(8,128)(2,1)S(1)} %copy-done.2, bf16[1024,768]{1,0:T(8,128)(2,1)S(1)} %copy-done.3, ...), custom_call_target="tpu_custom_call" | custom-call | flops 3000000 | bytes 11000000 | tf_op jit(solution)/shard_map/merge/pallas_call | solution.py:297
  (92 shorter events, 25.5 us)
Async XLA Ops:
  4.9 18.6 %collective-permute-start = (bf16[4,32,1664]{2,1,0:T(8,128)(2,1)}, bf16[4,32,1664]{2,1,0:T(8,128)(2,1)S(1)}, u32[]{:S(2)}, u32[]{:S(2)}) collective-permute-start(bf16[4,32,1664]{2,1,0:T(8,128)(2,1)} %get-tuple-element.46), channel_id=1, source_target_pairs={{0,7},{1,0},{2,1},{3,2},{4,3},{5,4},{6,5},{7,6},{8,15},{9,8},{10,9... | collective-permute-start | bytes 1277960 | tf_op jit(solution)/shard_map/ppermute | solution.py:477
  9.1 14.7 %collective-permute-start.1 = (bf16[4,32,1664]{2,1,0:T(8,128)(2,1)}, bf16[4,32,1664]{2,1,0:T(8,128)(2,1)S(1)}, u32[]{:S(2)}, u32[]{:S(2)}) collective-permute-start(bf16[4,32,1664]{2,1,0:T(8,128)(2,1)} %get-tuple-element.47), channel_id=1, source_target_pairs={{0,1},{1,2},{2,3},{3,4},{4,5},{5,6},{6,7},{7,0},{8,9},{9,10},{10,1... | collective-permute-start | bytes 1277960 | tf_op jit(solution)/shard_map/ppermute | solution.py:477
  9.1 14.4 %collective-permute-start.2 = (bf16[12,8,1664]{2,1,0:T(8,128)(2,1)}, bf16[12,8,1664]{2,1,0:T(8,128)(2,1)S(1)}, u32[]{:S(2)}, u32[]{:S(2)}) collective-permute-start(bf16[12,8,1664]{2,1,0:T(8,128)(2,1)} %get-tuple-element.48), channel_id=1, source_target_pairs={{0,120},{1,121},{2,122},{3,123},{4,124},{5,125},{6,126},{7,127},{8... | collective-permute-start | bytes 958472 | tf_op jit(solution)/shard_map/ppermute | solution.py:477
  14.3 9.2 %collective-permute-start.3 = (bf16[4,8,1664]{2,1,0:T(8,128)(2,1)}, bf16[4,8,1664]{2,1,0:T(8,128)(2,1)S(1)}, u32[]{:S(2)}, u32[]{:S(2)}) collective-permute-start(bf16[4,8,1664]{2,1,0:T(8,128)(2,1)} %get-tuple-element.49), channel_id=1, source_target_pairs={{0,121},{1,122},{2,123},{3,124},{4,125},{5,126},{6,127},{7,120},{8... | collective-permute-start | bytes 319496 | tf_op jit(solution)/shard_map/ppermute | solution.py:477
  59.1 13.1 %collective-permute-start.4 = (bf16[1536,768]{1,0:T(8,128)(2,1)}, bf16[1536,768]{1,0:T(8,128)(2,1)}, u32[]{:S(2)}, u32[]{:S(2)}) collective-permute-start(bf16[1536,768]{1,0:T(8,128)(2,1)} %get-tuple-element.51), channel_id=1, source_target_pairs={{0,8},{1,9},{2,10},{3,11},{4,12},{5,13},{6,14},{7,15},{8,0},{9,1},... | collective-permute-start | bytes 7077896 | tf_op jit(solution)/shard_map/ppermute | solution.py:425
  75.8 8.0 %collective-permute-start.5 = (bf16[256,768]{1,0:T(8,128)(2,1)}, bf16[256,768]{1,0:T(8,128)(2,1)S(1)}, u32[]{:S(2)}, u32[]{:S(2)}) collective-permute-start(bf16[256,768]{1,0:T(8,128)(2,1)} %get-tuple-element.64), channel_id=1, source_target_pairs={{0,1},{1,0},{2,3},{3,2},{4,5},{5,4},{6,7},{7,6},{8,11},{9,10},{10,... | collective-permute-start | bytes 1179656 | tf_op jit(solution)/shard_map/ppermute | solution.py:425
  75.8 9.8 %collective-permute-start.13 = (bf16[256,768]{1,0:T(8,128)(2,1)}, bf16[256,768]{1,0:T(8,128)(2,1)S(1)}, u32[]{:S(2)}, u32[]{:S(2)}) collective-permute-start(bf16[256,768]{1,0:T(8,128)(2,1)} %get-tuple-element.66), channel_id=1, source_target_pairs={{0,16},{1,17},{2,18},{3,19},{4,20},{5,21},{6,22},{7,23},{8,56},{9,... | collective-permute-start | bytes 1179656 | tf_op jit(solution)/shard_map/ppermute | solution.py:425
  77.4 8.5 %collective-permute-start.21 = (bf16[256,768]{1,0:T(8,128)(2,1)S(1)}, bf16[256,768]{1,0:T(8,128)(2,1)S(1)}, u32[]{:S(2)}, u32[]{:S(2)}) collective-permute-start(bf16[256,768]{1,0:T(8,128)(2,1)S(1)} %get-tuple-element.68), channel_id=1, source_target_pairs={{0,4},{1,5},{2,6},{3,7},{4,0},{5,1},{6,2},{7,3},{8,76},{9,77},{10,... | collective-permute-start | bytes 1179656 | tf_op jit(solution)/shard_map/ppermute | solution.py:425
  85.7 5.8 %collective-permute-start.14 = (bf16[128,768]{1,0:T(8,128)(2,1)S(1)}, bf16[128,768]{1,0:T(8,128)(2,1)S(1)}, u32[]{:S(2)}, u32[]{:S(2)}) collective-permute-start(bf16[128,768]{1,0:T(8,128)(2,1)S(1)} %constant_dynamic-slice_fusion.1), channel_id=1, source_target_pairs={{0,4},{1,5},{2,6},{3,7},{4,0},{5,1},{6,2},{7,3},{8,76},{9,77},{10,... | collective-permute-start | bytes 589832 | tf_op jit(solution)/shard_map/ppermute | solution.py:425
  86.0 5.8 %collective-permute-start.22 = (bf16[128,768]{1,0:T(8,128)(2,1)S(1)}, bf16[128,768]{1,0:T(8,128)(2,1)S(1)}, u32[]{:S(2)}, u32[]{:S(2)}) collective-permute-start(bf16[128,768]{1,0:T(8,128)(2,1)S(1)} %constant_dynamic-slice_fusion), channel_id=1, source_target_pairs={{0,1},{1,0},{2,3},{3,2},{4,5},{5,4},{6,7},{7,6},{8,11},{9,10},{10,... | collective-permute-start | bytes 589832 | tf_op jit(solution)/shard_map/ppermute | solution.py:425
  89.7 5.9 %collective-permute-start.7 = (bf16[128,768]{1,0:T(8,128)(2,1)S(1)}, bf16[128,768]{1,0:T(8,128)(2,1)S(1)}, u32[]{:S(2)}, u32[]{:S(2)}) collective-permute-start(bf16[128,768]{1,0:T(8,128)(2,1)S(1)} %add_convert_fusion.17), channel_id=1, source_target_pairs={{0,4},{1,5},{2,6},{3,7},{4,0},{5,1},{6,2},{7,3},{8,76},{9,77},{10,... | collective-permute-start | bytes 589832 | tf_op jit(solution)/shard_map/ppermute | solution.py:425
  91.5 5.7 %collective-permute-start.15 = (bf16[128,768]{1,0:T(8,128)(2,1)S(1)}, bf16[128,768]{1,0:T(8,128)(2,1)S(1)}, u32[]{:S(2)}, u32[]{:S(2)}) collective-permute-start(bf16[128,768]{1,0:T(8,128)(2,1)S(1)} %add_convert_fusion.12), channel_id=1, source_target_pairs={{0,1},{1,0},{2,3},{3,2},{4,5},{5,4},{6,7},{7,6},{8,11},{9,10},{10,... | collective-permute-start | bytes 589832 | tf_op jit(solution)/shard_map/ppermute | solution.py:425
  91.9 10.8 %collective-permute-start.23 = (bf16[128,768]{1,0:T(8,128)(2,1)S(1)}, bf16[128,768]{1,0:T(8,128)(2,1)S(1)}, u32[]{:S(2)}, u32[]{:S(2)}) collective-permute-start(bf16[128,768]{1,0:T(8,128)(2,1)S(1)} %add_convert_fusion.7), channel_id=1, source_target_pairs={{0,16},{1,17},{2,18},{3,19},{4,20},{5,21},{6,22},{7,23},{8,56},{9,... | collective-permute-start | bytes 589832 | tf_op jit(solution)/shard_map/ppermute | solution.py:425
  95.7 9.6 %collective-permute-start.8 = (bf16[128,768]{1,0:T(8,128)(2,1)S(1)}, bf16[128,768]{1,0:T(8,128)(2,1)S(1)}, u32[]{:S(2)}, u32[]{:S(2)}) collective-permute-start(bf16[128,768]{1,0:T(8,128)(2,1)S(1)} %add_convert_fusion.16), channel_id=1, source_target_pairs={{0,3},{1,2},{2,1},{3,0},{4,7},{5,6},{6,5},{7,4},{8,9},{9,8},{10,11... | collective-permute-start | bytes 589832 | tf_op jit(solution)/shard_map/ppermute | solution.py:425
  97.3 10.3 %collective-permute-start.16 = (bf16[128,768]{1,0:T(8,128)(2,1)S(1)}, bf16[128,768]{1,0:T(8,128)(2,1)S(1)}, u32[]{:S(2)}, u32[]{:S(2)}) collective-permute-start(bf16[128,768]{1,0:T(8,128)(2,1)S(1)} %add_convert_fusion.11), channel_id=1, source_target_pairs={{0,48},{1,49},{2,50},{3,51},{4,52},{5,53},{6,54},{7,55},{8,24},{9,... | collective-permute-start | bytes 589832 | tf_op jit(solution)/shard_map/ppermute | solution.py:425
  102.7 7.6 %collective-permute-start.24 = (bf16[128,768]{1,0:T(8,128)(2,1)S(1)}, bf16[128,768]{1,0:T(8,128)(2,1)S(1)}, u32[]{:S(2)}, u32[]{:S(2)}) collective-permute-start(bf16[128,768]{1,0:T(8,128)(2,1)S(1)} %add_convert_fusion.6), channel_id=1, source_target_pairs={{0,68},{1,69},{2,70},{3,71},{4,64},{5,65},{6,66},{7,67},{8,12},{9,... | collective-permute-start | bytes 589832 | tf_op jit(solution)/shard_map/ppermute | solution.py:425
  105.3 7.0 %collective-permute-start.9 = (bf16[128,768]{1,0:T(8,128)(2,1)S(1)}, bf16[128,768]{1,0:T(8,128)(2,1)S(1)}, u32[]{:S(2)}, u32[]{:S(2)}) collective-permute-start(bf16[128,768]{1,0:T(8,128)(2,1)S(1)} %add_convert_fusion.15), channel_id=1, source_target_pairs={{0,48},{1,49},{2,50},{3,51},{4,52},{5,53},{6,54},{7,55},{8,24},{9,... | collective-permute-start | bytes 589832 | tf_op jit(solution)/shard_map/ppermute | solution.py:425
  107.6 7.0 %collective-permute-start.17 = (bf16[128,768]{1,0:T(8,128)(2,1)S(1)}, bf16[128,768]{1,0:T(8,128)(2,1)S(1)}, u32[]{:S(2)}, u32[]{:S(2)}) collective-permute-start(bf16[128,768]{1,0:T(8,128)(2,1)S(1)} %add_convert_fusion.10), channel_id=1, source_target_pairs={{0,68},{1,69},{2,70},{3,71},{4,64},{5,65},{6,66},{7,67},{8,12},{9,... | collective-permute-start | bytes 589832 | tf_op jit(solution)/shard_map/ppermute | solution.py:425
  110.3 7.0 %collective-permute-start.25 = (bf16[128,768]{1,0:T(8,128)(2,1)S(1)}, bf16[128,768]{1,0:T(8,128)(2,1)S(1)}, u32[]{:S(2)}, u32[]{:S(2)}) collective-permute-start(bf16[128,768]{1,0:T(8,128)(2,1)S(1)} %add_convert_fusion.5), channel_id=1, source_target_pairs={{0,3},{1,2},{2,1},{3,0},{4,7},{5,6},{6,5},{7,4},{8,9},{9,8},{10,11... | collective-permute-start | bytes 589832 | tf_op jit(solution)/shard_map/ppermute | solution.py:425
  112.4 7.0 %collective-permute-start.10 = (bf16[128,768]{1,0:T(8,128)(2,1)S(1)}, bf16[128,768]{1,0:T(8,128)(2,1)S(1)}, u32[]{:S(2)}, u32[]{:S(2)}) collective-permute-start(bf16[128,768]{1,0:T(8,128)(2,1)S(1)} %add_convert_fusion.14), channel_id=1, source_target_pairs={{0,68},{1,69},{2,70},{3,71},{4,64},{5,65},{6,66},{7,67},{8,12},{9,... | collective-permute-start | bytes 589832 | tf_op jit(solution)/shard_map/ppermute | solution.py:425
  114.7 7.0 %collective-permute-start.18 = (bf16[128,768]{1,0:T(8,128)(2,1)S(1)}, bf16[128,768]{1,0:T(8,128)(2,1)S(1)}, u32[]{:S(2)}, u32[]{:S(2)}) collective-permute-start(bf16[128,768]{1,0:T(8,128)(2,1)S(1)} %add_convert_fusion.9), channel_id=1, source_target_pairs={{0,3},{1,2},{2,1},{3,0},{4,7},{5,6},{6,5},{7,4},{8,9},{9,8},{10,11... | collective-permute-start | bytes 589832 | tf_op jit(solution)/shard_map/ppermute | solution.py:425
  117.3 7.0 %collective-permute-start.26 = (bf16[128,768]{1,0:T(8,128)(2,1)S(1)}, bf16[128,768]{1,0:T(8,128)(2,1)S(1)}, u32[]{:S(2)}, u32[]{:S(2)}) collective-permute-start(bf16[128,768]{1,0:T(8,128)(2,1)S(1)} %add_convert_fusion.4), channel_id=1, source_target_pairs={{0,48},{1,49},{2,50},{3,51},{4,52},{5,53},{6,54},{7,55},{8,24},{9,... | collective-permute-start | bytes 589832 | tf_op jit(solution)/shard_map/ppermute | solution.py:425
  119.4 5.7 %collective-permute-start.11 = (bf16[128,768]{1,0:T(8,128)(2,1)S(1)}, bf16[128,768]{1,0:T(8,128)(2,1)S(1)}, u32[]{:S(2)}, u32[]{:S(2)}) collective-permute-start(bf16[128,768]{1,0:T(8,128)(2,1)S(1)} %add_convert_fusion.13), channel_id=1, source_target_pairs={{0,16},{1,17},{2,18},{3,19},{4,20},{5,21},{6,22},{7,23},{8,56},{9,... | collective-permute-start | bytes 589832 | tf_op jit(solution)/shard_map/ppermute | solution.py:425
  122.3 6.0 %collective-permute-start.19 = (bf16[128,768]{1,0:T(8,128)(2,1)}, bf16[128,768]{1,0:T(8,128)(2,1)}, u32[]{:S(2)}, u32[]{:S(2)}) collective-permute-start(bf16[128,768]{1,0:T(8,128)(2,1)} %add_convert_fusion.8), channel_id=1, source_target_pairs={{0,4},{1,5},{2,6},{3,7},{4,0},{5,1},{6,2},{7,3},{8,76},{9,77},{10,... | collective-permute-start | bytes 589832 | tf_op jit(solution)/shard_map/ppermute | solution.py:425
  125.0 6.8 %collective-permute-start.27 = (bf16[128,768]{1,0:T(8,128)(2,1)}, bf16[128,768]{1,0:T(8,128)(2,1)}, u32[]{:S(2)}, u32[]{:S(2)}) collective-permute-start(bf16[128,768]{1,0:T(8,128)(2,1)} %add_convert_fusion.3), channel_id=1, source_target_pairs={{0,1},{1,0},{2,3},{3,2},{4,5},{5,4},{6,7},{7,6},{8,11},{9,10},{10,... | collective-permute-start | bytes 589832 | tf_op jit(solution)/shard_map/ppermute | solution.py:425
  125.2 10.0 %collective-permute-start.12 = (bf16[256,768]{1,0:T(8,128)(2,1)S(1)}, bf16[256,768]{1,0:T(8,128)(2,1)}, u32[]{:S(2)}, u32[]{:S(2)}) collective-permute-start(bf16[256,768]{1,0:T(8,128)(2,1)S(1)} %maximum_select_fusion.3), channel_id=1, source_target_pairs={{0,1},{1,0},{2,3},{3,2},{4,5},{5,4},{6,7},{7,6},{8,11},{9,10},{10,... | collective-permute-start | bytes 1179656 | tf_op jit(solution)/shard_map/ppermute | solution.py:425
  130.4 8.1 %collective-permute-start.20 = (bf16[256,768]{1,0:T(8,128)(2,1)}, bf16[256,768]{1,0:T(8,128)(2,1)}, u32[]{:S(2)}, u32[]{:S(2)}) collective-permute-start(bf16[256,768]{1,0:T(8,128)(2,1)} %maximum_select_fusion.4), channel_id=1, source_target_pairs={{0,16},{1,17},{2,18},{3,19},{4,20},{5,21},{6,22},{7,23},{8,56},{9,... | collective-permute-start | bytes 1179656 | tf_op jit(solution)/shard_map/ppermute | solution.py:425
  133.1 7.9 %collective-permute-start.28 = (bf16[256,768]{1,0:T(8,128)(2,1)S(1)}, bf16[256,768]{1,0:T(8,128)(2,1)S(1)}, u32[]{:S(2)}, u32[]{:S(2)}) collective-permute-start(bf16[256,768]{1,0:T(8,128)(2,1)S(1)} %maximum_select_fusion.5), channel_id=1, source_target_pairs={{0,4},{1,5},{2,6},{3,7},{4,0},{5,1},{6,2},{7,3},{8,76},{9,77},{10,... | collective-permute-start | bytes 1179656 | tf_op jit(solution)/shard_map/ppermute | solution.py:425
  141.6 17.4 %collective-permute-start.29 = (bf16[4,32,1536]{2,1,0:T(8,128)(2,1)S(1)}, bf16[4,32,1536]{2,1,0:T(8,128)(2,1)S(1)}, u32[]{:S(2)}, u32[]{:S(2)}) collective-permute-start(bf16[4,32,1536]{2,1,0:T(8,128)(2,1)S(1)} %get-tuple-element.73), channel_id=1, source_target_pairs={{0,7},{1,0},{2,1},{3,2},{4,3},{5,4},{6,5},{7,6},{8,15},{9,8},{10,9... | collective-permute-start | bytes 1179656 | tf_op jit(solution)/shard_map/ppermute | solution.py:477
  141.7 17.7 %collective-permute-start.30 = (bf16[4,32,1536]{2,1,0:T(8,128)(2,1)S(1)}, bf16[4,32,1536]{2,1,0:T(8,128)(2,1)S(1)}, u32[]{:S(2)}, u32[]{:S(2)}) collective-permute-start(bf16[4,32,1536]{2,1,0:T(8,128)(2,1)S(1)} %get-tuple-element.74), channel_id=1, source_target_pairs={{0,1},{1,2},{2,3},{3,4},{4,5},{5,6},{6,7},{7,0},{8,9},{9,10},{10,1... | collective-permute-start | bytes 1179656 | tf_op jit(solution)/shard_map/ppermute | solution.py:477
  143.7 15.3 %collective-permute-start.31 = (bf16[12,8,1536]{2,1,0:T(8,128)(2,1)S(1)}, bf16[12,8,1536]{2,1,0:T(8,128)(2,1)S(1)}, u32[]{:S(2)}, u32[]{:S(2)}) collective-permute-start(bf16[12,8,1536]{2,1,0:T(8,128)(2,1)S(1)} %get-tuple-element.75), channel_id=1, source_target_pairs={{0,8},{1,9},{2,10},{3,11},{4,12},{5,13},{6,14},{7,15},{8,16},{9,17... | collective-permute-start | bytes 884744 | tf_op jit(solution)/shard_map/ppermute | solution.py:477
  143.7 15.3 %collective-permute-start.32 = (bf16[4,8,1536]{2,1,0:T(8,128)(2,1)S(1)}, bf16[4,8,1536]{2,1,0:T(8,128)(2,1)S(1)}, u32[]{:S(2)}, u32[]{:S(2)}) collective-permute-start(bf16[4,8,1536]{2,1,0:T(8,128)(2,1)S(1)} %get-tuple-element.76), channel_id=1, source_target_pairs={{0,15},{1,8},{2,9},{3,10},{4,11},{5,12},{6,13},{7,14},{8,23},{9,16... | collective-permute-start | bytes 294920 | tf_op jit(solution)/shard_map/ppermute | solution.py:477
  (11 other events, 125.8 us)

commit v4 on v3

--- a/solution.py
+++ b/solution.py
@@ -38,6 +38,7 @@
 
 
 TOKENS = 1024
+HERE = pl.BlockSpec(memory_space=pltpu.VMEM)
 F = 2 * D + 128
 
 
@@ -109,12 +110,19 @@
     return out
 
 
-def attn_body(core_ref, x_ref, g_ref, kb_ref, below, above, right, corner, wq_ref, wk_ref, wv_ref, wo_ref,
-              mixed_ref, dq_ref, dk_ref, dv_ref, xw, keep_ref, send_ref,
-              gw, bias, hid, hid_t, qs, ks, vs, gm, mix_t):
+def attn_body(core_ref, x_ref, g_ref, kb_ref, corner, right, below, above, wq_ref, wk_ref, wv_ref, wg_ref, wqkv_hbm, wo_hbm,
+              attn_ref, gs_ref, up, down, side, edge, keep_ref, send_ref,
+              mixed_ref, dq_ref, dk_ref, dv_ref, xw, wqkv, wo, sems, gw, bias, hid, hid_t, qs, ks, vs, gm, mix_t):
+
+    loads = [
+        pltpu.make_async_copy(wqkv_hbm, wqkv, sems.at[0]),
+        pltpu.make_async_copy(wo_hbm, wo, sems.at[1]),
+    ]
 
     @pl.when(pl.program_id(0) == 0)
     def _():
+        for load in loads:
+            load.start()
         halo = (below, above, right, corner)
         for w, t in enumerate(window_pieces(x_ref, *halo, slice(0, D))):
             xw[64 * w : 64 * w + 64, :] = t.astype(F32).reshape(64, D).astype(BF16)
@@ -136,14 +144,13 @@
             hid[rows, :] = n.astype(BF16)
             hid_t[:, rows] = jnp.transpose(n).astype(BF16)
 
-    @pl.loop(0, 1)
-    def _(i):
-        rows = pl.ds(0, TOKENS)
-        h = hid[rows, :]
-        qs[rows, :] = mm(h, wq_ref[...]).astype(BF16)
-        ks[rows, :] = mm(h, wk_ref[...]).astype(BF16)
-        vs[rows, :] = mm(h, wv_ref[...]).astype(BF16)
-        gm[rows, :] = mm(gw[rows, :], wo_ref[...], NT).astype(BF16)
+    group = pl.program_id(0)
+    base = pl.multiple_of(group * GD, GD)
+    cols = pl.ds(base, GD)
+    h = hid[...]
+    for w, out in ((wq_ref, qs), (wk_ref, ks), (wv_ref, vs)):
+        out[...] = mm(h, w[...]).astype(BF16)
+    gm[...] = mm(gw[...], wg_ref[...], NT).astype(BF16)
 
     head_lane = lax.broadcasted_iota(jnp.int32, (64, 128), 1) // 32
 
@@ -180,7 +187,8 @@
         mx = [mm(p, c[2], TN) for p, c in zip(pbs, ch)]
         dk = [mm(d, b) for d, b in zip(dbs, qb)]
         dq = [mm(d, c[1], TN) for d, c in zip(dbs, ch)]
-        for i, c in enumerate(keys):
+        for i, (rows, lanes) in enumerate(keys):
+            c = rows, pl.ds(pl.multiple_of(base + lanes.start, 128), 128)
             dv_ref[c] = dv[i].astype(BF16)
             mixed_ref[c] = gather_diag(mx[i], head_lane).astype(BF16)
             dk_ref[c] = dk[i].astype(BF16)
@@ -189,34 +197,67 @@
     @pl.loop(0, TOKENS // 128)
     def _(i):
         rows = pl.ds(pl.multiple_of(i * 128, 128), 128)
-        mix_t[:, rows] = jnp.transpose(mixed_ref[rows, :].astype(F32)).astype(BF16)
+        mix_t[:, rows] = jnp.transpose(mixed_ref[rows, cols].astype(F32)).astype(BF16)
 
     core = core_ref[0]
     for out, half in ((keep_ref, core), (send_ref, 1 - core)):
         h = hid_t[pl.ds(pl.multiple_of(half * 384, 128), 384), :]
-        out[0:384, 0:256] = mm(h, dq_ref[...]).astype(BF16)
-        out[0:384, 256:512] = mm(h, dk_ref[...]).astype(BF16)
-        out[0:384, 512:768] = mm(h, dv_ref[...]).astype(BF16)
+        for p, t in enumerate((dq_ref, dk_ref, dv_ref)):
+            out[0:384, GD * p : GD * p + GD] = mm(h, t[:, cols]).astype(BF16)
         m = mix_t[pl.ds(pl.multiple_of(half * 128, 128), 128), :]
         out[384:512, :] = mm(m, gw[...]).astype(BF16)
 
+    @pl.when(group == 2)
+    def _():
+        for load in loads:
+            load.wait()
+
+        @pl.loop(0, 2)
+        def _(i):
+            rows = pl.ds(pl.multiple_of(i * 512, 512), 512)
+            attn_ref[rows, :] = mm(mixed_ref[rows, :], wo[...]).astype(BF16)
+            dh = mm(dq_ref[rows, :], wqkv[:, 0:768], NT)
+            dh += mm(dk_ref[rows, :], wqkv[:, 768:1536], NT)
+            dh += mm(dv_ref[rows, :], wqkv[:, 1536:2304], NT)
+            x = xw[rows, :].astype(F32)
+            c = x - jnp.mean(x, -1, keepdims=True)
+            inv = lax.rsqrt(jnp.mean(c * c, -1, keepdims=True) + EPS)
+            n = c * inv
+            back = dh - jnp.mean(dh, -1, keepdims=True) - n * jnp.mean(dh * n, -1, keepdims=True)
+            gs_ref[rows, :] = (inv * back).astype(BF16)
+
+        for win, lanes in ((attn_ref, slice(0, D)), (gs_ref, slice(D, 2 * D))):
+            piece = lambda w: win[64 * w : 64 * w + 64, :].astype(F32).reshape(8, 8, D).astype(BF16)
+            for j in range(4):
+                at = slice(8 * j, 8 * j + 8)
+                up[:, at, lanes] = piece(12 + j)[0:4]
+                down[:, at, lanes] = piece(8 + j)[4:8]
+            side[0:4, :, lanes] = piece(15)[4:8]
+            side[4:12, :, lanes] = piece(7)
+            edge[:, :, lanes] = piece(15)[0:4]
+
 
 def attn_call(core, x, g, kb, halo, w_qkv, w_out):
-    fixed = lambda t: pl.BlockSpec(t.shape, lambda i, c: (0,) * t.ndim, pipeline_mode=pl.Buffered(1))
-    cols = pl.BlockSpec((TOKENS, GD), lambda i, c: (0, i))
+    fixed = lambda t: pl.BlockSpec(t.shape, lambda i, c: (0,) * len(t.shape), pipeline_mode=pl.Buffered(1))
     wblock = lambda p: pl.BlockSpec((D, GD), lambda i, c: (0, 3 * p + i))
     half = pl.BlockSpec((512, D), lambda i, c: (i, 0))
+    far = pl.BlockSpec(memory_space=pl.ANY)
     tok = jax.ShapeDtypeStruct((TOKENS, D), BF16)
     halves = jax.ShapeDtypeStruct((1536, D), BF16)
+    borders = [jax.ShapeDtypeStruct((r, c, 2 * D), BF16) for r, c in ((4, 32), (4, 32), (12, 8), (4, 8))]
     return pl.pallas_call(
         attn_body,
         grid_spec=pltpu.PrefetchScalarGridSpec(
             num_scalar_prefetch=1,
             grid=(3,),
             in_specs=[fixed(t) for t in (x, g, kb, *halo)]
-            + [wblock(0), wblock(1), wblock(2), pl.BlockSpec((GD, D), lambda i, c: (i, 0))],
-            out_specs=[cols, cols, cols, cols, fixed(tok), half, half],
-            scratch_shapes=[
+            + [wblock(0), wblock(1), wblock(2), pl.BlockSpec((GD, D), lambda i, c: (i, 0)), far, far],
+            out_specs=[fixed(t) for t in (tok, tok, *borders)] + [half, half],
+            scratch_shapes=[pltpu.VMEM((TOKENS, D), BF16)] * 5
+            + [
+                pltpu.VMEM((D, 3 * D), BF16),
+                pltpu.VMEM((D, D), BF16),
+                pltpu.SemaphoreType.DMA((2,)),
                 pltpu.VMEM((TOKENS, D), BF16),
                 pltpu.VMEM((TOKENS, 128), F32),
                 pltpu.VMEM((TOKENS, D), BF16),
@@ -228,54 +269,18 @@
                 pltpu.VMEM((GD, TOKENS), BF16),
             ],
         ),
-        out_shape=[tok, tok, tok, tok, tok, halves, halves],
+        out_shape=[tok, tok, *borders, halves, halves],
         compiler_params=pltpu.CompilerParams(
-            dimension_semantics=("arbitrary",), vmem_limit_bytes=48 << 20
+            dimension_semantics=("arbitrary",), vmem_limit_bytes=56 << 20
         ),
         cost_estimate=pl.CostEstimate(
-            flops=14_000_000_000, bytes_accessed=20_000_000, transcendentals=1_600_000
+            flops=16_000_000_000, bytes_accessed=25_000_000, transcendentals=1_600_000
         ),
         name="attention",
-    )(core, x, g, kb, *halo, w_qkv, w_qkv, w_qkv, w_out)
-
-
-def finish_body(x_ref, mixed_ref, dq_ref, dk_ref, dv_ref, wqkv_ref, wo_ref, attn_ref, gs_ref):
-    attn_ref[...] = mm(mixed_ref[...], wo_ref[...]).astype(BF16)
-    dh = mm(dq_ref[...], wqkv_ref[:, 0:768], NT)
-    dh += mm(dk_ref[...], wqkv_ref[:, 768:1536], NT)
-    dh += mm(dv_ref[...], wqkv_ref[:, 1536:2304], NT)
-    x = x_ref[...].astype(F32)
-    c = x - jnp.mean(x, -1, keepdims=True)
-    inv = lax.rsqrt(jnp.mean(c * c, -1, keepdims=True) + EPS)
-    n = c * inv
-    back = dh - jnp.mean(dh, -1, keepdims=True) - n * jnp.mean(dh * n, -1, keepdims=True)
-    gs_ref[...] = (inv * back).astype(BF16)
-
-
-def finish_call(x, mixed, dq, dk, dv, w_qkv, w_out):
-    tokens = x.shape[0]
-    tile = 512
-    t = pl.BlockSpec((tile, D), lambda i: (i, 0))
-    tok = jax.ShapeDtypeStruct((tokens, D), BF16)
-    return pl.pallas_call(
-        finish_body,
-        grid=(tokens // tile,),
-        in_specs=[t, t, t, t, t,
-                  pl.BlockSpec((D, 3 * D), lambda i: (0, 0), pipeline_mode=pl.Buffered(1)),
-                  pl.BlockSpec((D, D), lambda i: (0, 0), pipeline_mode=pl.Buffered(1))],
-        out_specs=[t, t],
-        out_shape=[tok, tok],
-        compiler_params=pltpu.CompilerParams(
-            dimension_semantics=("arbitrary",), vmem_limit_bytes=60 << 20
-        ),
-        cost_estimate=pl.CostEstimate(
-            flops=4_800_000_000, bytes_accessed=16_000_000, transcendentals=0
-        ),
-        name="finish",
-    )(x, mixed, dq, dk, dv, w_qkv, w_out)
-
-
-def merge_body(x_ref, g_ref, attn_ref, grad_ref, below, above, left, corner, out_ref, gin_ref):
+    )(core, x, g, kb, *halo, w_qkv, w_qkv, w_qkv, w_out, w_qkv, w_out)
+
+
+def merge_body(x_ref, g_ref, attn_ref, grad_ref, corner, left, below, above, out_ref, gin_ref):
     for src, win, dst, lanes in (
         (x_ref, attn_ref, out_ref, slice(0, D)),
         (g_ref, grad_ref, gin_ref, slice(D, 2 * D)),
@@ -303,49 +308,53 @@
     )(x, g, attn, grad, *halo)
 
 
-def split_body(attn_ref, grad_ref, up, down, side, corner):
-    for win, lanes in ((attn_ref, slice(0, D)), (grad_ref, slice(D, 2 * D))):
-        piece = lambda w: win[64 * w : 64 * w + 64, :].astype(F32).reshape(8, 8, D).astype(BF16)
-        for j in range(4):
-            cols = slice(8 * j, 8 * j + 8)
-            up[:, cols, lanes] = piece(12 + j)[0:4]
-            down[:, cols, lanes] = piece(8 + j)[4:8]
-        side[0:4, :, lanes] = piece(15)[4:8]
-        side[4:12, :, lanes] = piece(7)
-        corner[:, :, lanes] = piece(15)[0:4]
-
-
-def split_call(attn, grad):
-    shapes = [(4, 32, 2 * D), (4, 32, 2 * D), (12, 8, 2 * D), (4, 8, 2 * D)]
-    return pl.pallas_call(
-        split_body,
-        out_shape=[jax.ShapeDtypeStruct(sh, BF16) for sh in shapes],
-        compiler_params=pltpu.CompilerParams(vmem_limit_bytes=16 << 20),
-        cost_estimate=pl.CostEstimate(flops=0, bytes_accessed=5_000_000, transcendentals=0),
-        name="split",
-    )(attn, grad)
-
-
 def combine_body(bits, keep, recv, *outs):
     for k in range(3):
-        for out, half in ((outs[k], bits[k]), (outs[3 + k], 1 - bits[k])):
-            rows = pl.ds(pl.multiple_of(512 * k + half * 256, 256), 256)
-            out[...] = (keep[rows, :].astype(F32) + recv[rows, :].astype(F32)).astype(BF16)
+
+        @pl.when(pl.program_id(0) == k)
+        def _():
+            for out, half in ((outs[k], bits[k]), (outs[3 + k], 1 - bits[k])):
+                rows = pl.ds(pl.multiple_of(half * 256, 256), 256)
+                out[...] = (keep[rows, :].astype(F32) + recv[rows, :].astype(F32)).astype(BF16)
 
 
 def combine_call(bits, keep, recv):
-    whole = pl.BlockSpec((1536, D), lambda i, c: (0, 0), pipeline_mode=pl.Buffered(1))
+    part = pl.BlockSpec((512, D), lambda i, c: (i, 0))
     half = pl.BlockSpec((256, D), lambda i, c: (0, 0), pipeline_mode=pl.Buffered(1))
     return pl.pallas_call(
         combine_body,
         grid_spec=pltpu.PrefetchScalarGridSpec(
-            num_scalar_prefetch=1, grid=(1,), in_specs=[whole] * 2, out_specs=[half] * 6
+            num_scalar_prefetch=1, grid=(3,), in_specs=[part] * 2, out_specs=[half] * 6
         ),
         out_shape=[jax.ShapeDtypeStruct((256, D), BF16)] * 6,
-        compiler_params=pltpu.CompilerParams(vmem_limit_bytes=16 << 20),
+        compiler_params=pltpu.CompilerParams(
+            dimension_semantics=("arbitrary",), vmem_limit_bytes=16 << 20
+        ),
         cost_estimate=pl.CostEstimate(flops=1_200_000, bytes_accessed=7_000_000, transcendentals=0),
         name="combine",
     )(bits, keep, recv)
+
+
+def join_body(bits, *refs):
+    out = refs[-1]
+    n = refs[0].shape[0]
+    for k in range(len(refs) // 2):
+        out[pl.ds(pl.multiple_of(n * (2 * k + bits[k]), n), n), :] = refs[2 * k][...]
+        out[pl.ds(pl.multiple_of(n * (2 * k + 1 - bits[k]), n), n), :] = refs[2 * k + 1][...]
+
+
+def join_call(bits, *halves):
+    rows = len(halves) * halves[0].shape[0]
+    return pl.pallas_call(
+        join_body,
+        grid_spec=pltpu.PrefetchScalarGridSpec(
+            num_scalar_prefetch=1, grid=(1,), in_specs=[HERE] * len(halves), out_specs=HERE
+        ),
+        out_shape=jax.ShapeDtypeStruct((rows, D), BF16),
+        compiler_params=pltpu.CompilerParams(vmem_limit_bytes=16 << 20),
+        cost_estimate=pl.CostEstimate(flops=0, bytes_accessed=3072 * rows, transcendentals=0),
+        name="join",
+    )(bits, *halves)
 
 
 def widen_body(core_ref, own, other, wqkv, wout):
@@ -375,13 +384,12 @@
 
 
 def widen_call(core, own, other):
-    half = pl.BlockSpec((1536, D), lambda j, c: (0, 0), pipeline_mode=pl.Buffered(1))
     return pl.pallas_call(
         widen_body,
         grid_spec=pltpu.PrefetchScalarGridSpec(
             num_scalar_prefetch=1,
             grid=(7,),
-            in_specs=[half] * 2,
+            in_specs=[HERE] * 2,
             out_specs=[
                 pl.BlockSpec((128, 3 * D), lambda j, c: (jnp.minimum(j, 5), 0)),
                 pl.BlockSpec((D, D), lambda j, c: (0, 0)),
@@ -448,25 +456,21 @@
     return add(keep, exchange(send, axis, first))
 
 
-def gather_half(v, axis, first=True):
-    b = half_of(axis, first)
-    o = exchange(v, axis, first)
-    return jnp.where(b == 0, jnp.concatenate([v, o], 0), jnp.concatenate([o, v], 0))
-
-
-def total(keep, send, gate):
+def total(keep, send):
     axes = [["xyz"[(k + s) % 3] for s in range(3)] for k in range(3)]
     recv = exchange(send, "core", True)
-    keep, recv, gate = lax.optimization_barrier((keep, recv, gate))
     bits = jnp.stack([half_of(a[0], True) for a in axes]).astype(jnp.int32)
     halves = combine_call(bits, keep, recv)
     parts = [add(halves[k], exchange(halves[3 + k], a[0], True)) for k, a in enumerate(axes)]
     parts = [scatter_half(p, a[1]) for p, a in zip(parts, axes)]
     for axis, first in ((2, True), (0, False), (1, False), (2, False)):
         parts = [add(p, exchange(p, a[axis], first)) for p, a in zip(parts, axes)]
-    for s in (1, 0):
-        parts = [gather_half(p, a[s]) for p, a in zip(parts, axes)]
-    return jnp.concatenate(parts, 0), gate
+    second = [half_of(a[1], True).astype(jnp.int32).reshape(1) for a in axes]
+    parts = [join_call(b, p, exchange(p, a[1], True)) for b, p, a in zip(second, parts, axes)]
+    halves = []
+    for p, a in zip(parts, axes):
+        halves += [p, exchange(p, a[0], True)]
+    return join_call(bits, *halves)
 
 
 def shift(v, d_gy, d_gx):
@@ -481,18 +485,14 @@
     kb = jnp.broadcast_to(tissue.astype(BF16)[..., None], tissue.shape + (128,))
     core = (lax.axis_index("gx") % 2).astype(jnp.int32).reshape(1)
     up, down, left, corner = pack_call(slide_tokens, grad_tokens, kb)
-    corner = shift(corner, 1, -1)
-    left = shift(left, 0, -1)
-    halo = (shift(up, -1, 0), shift(down, 1, 0), left, corner)
-    mixed, dq, dk, dv, x, keep, send = attn_call(core, slide_tokens, grad_tokens, kb, halo, w_qkv, w_out)
-    attn, grad = finish_call(x, mixed, dq, dk, dv, w_qkv, w_out)
-    own, (attn, grad) = total(keep, send, (attn, grad))
-
-    own, borders = lax.optimization_barrier((own, tuple(split_call(attn, grad))))
-    up, down, side, corner = borders
-    corner = shift(corner, -1, 1)
-    side = shift(side, 0, 1)
-    halo = (shift(up, -1, 0), shift(down, 1, 0), side, corner)
+    halo = (shift(corner, 1, -1), shift(left, 0, -1), shift(up, -1, 0), shift(down, 1, 0))
+    attn, grad, up, down, side, edge, keep, send = attn_call(
+        core, slide_tokens, grad_tokens, kb, halo, w_qkv, w_out
+    )
+    own = total(keep, send)
+
+    own, (up, down, side, edge) = lax.optimization_barrier((own, (up, down, side, edge)))
+    halo = (shift(edge, -1, 1), shift(side, 0, 1), shift(up, -1, 0), shift(down, 1, 0))
     grads = widen_call(core, own, exchange(own, "core", True))
     halo, grads = lax.optimization_barrier((halo, tuple(grads)))
     block_out, grad_in = merge_call(slide_tokens, grad_tokens, attn, grad, halo)

time: 162 us -> 159 us (0.981)
  waiting for transfers between devices: 43.6 us -> 53.5 us
  other arithmetic: 9.94 us -> 1.87 us
  Pallas kernels: 57.7 us -> 52.7 us
    pallas_call x2 -> x4, Pallas kernels: 11.1 us -> 0.78 us  [join_call(): pl.pallas_call(join_body, grid_spec=pltpu.PrefetchScalarGridSpec(num_scal...]
    ppermute x26, waiting for transfers between devices: 26.6 us -> 35.7 us  [exchange(): return lax.ppermute(v, AXES, pairs)]
    pallas_call x1, Pallas kernels: 32.9 us -> 39.8 us  [attn_call(): pl.pallas_call(attn_body, grid_spec=pltpu.PrefetchScalarGridSpec(num_scal...]
    select_n x6 -> x0, other arithmetic: 6.63 us -> none  [gather_half(): jnp.where(b == 0, jnp.concatenate([v, o], 0), jnp.concatenate([o, v], 0))]
    unnamed x18 -> x28, local copies, waits for them, and re-layouts: 2.43 us -> 3.24 us
  transfers between devices with their start and end apart: 34 -> 34, of which waited for: 19 -> 21; matrix products, arithmetic and copies ran while one was open for 5% -> 1% of each run, Pallas kernels for 10% -> 3%
where the time goes in v4:
time: 159 us
  waiting for transfers between devices  53.5 us (34%)
  Pallas kernels  52.7 us (33%)
  starting transfers between devices  45.8 us (29%)
  local copies, waits for them, and re-layouts  4.24 us (3%)
  other arithmetic  1.87 us (1%)
    pallas_call x1, Pallas kernels, attn_call(): pl.pallas_call(attn_body, grid_spec=pltpu.PrefetchScalarGridSpec(num_scal...  39.8 us
    ppermute x26, waiting for transfers between devices, exchange(): return lax.ppermute(v, AXES, pairs)  35.7 us
    ppermute x26, starting transfers between devices, exchange(): return lax.ppermute(v, AXES, pairs)  32 us
    ppermute x8, waiting for transfers between devices, shift(): return lax.ppermute(v, AXES, pairs)  17.7 us
    ppermute x8, starting transfers between devices, shift(): return lax.ppermute(v, AXES, pairs)  13.8 us
    pallas_call x1, Pallas kernels, widen_call(): pl.pallas_call(widen_body, grid_spec=pltpu.PrefetchScalarGridSpec(num_sca...  5.24 us
    unnamed x28, local copies, waits for them, and re-layouts  3.24 us
  transfers between devices with their start and end apart: 34, of which 21 were waited for; matrix products, arithmetic and copies ran while one was open for 1% of the time, Pallas kernels for 3%

profile of v4, /device:TPU:0, one launch (start us, length us, event | category | flops | bytes accessed | tf_op | source)
XLA Modules:
  0.0 159.0 jit_solution(8836128808151992304)
XLA Ops:
  2.3 2.6 %pack.1 = (bf16[4,32,1664]{2,1,0:T(8,128)(2,1)}, bf16[4,32,1664]{2,1,0:T(8,128)(2,1)}, bf16[12,8,1664]{2,1,0:T(8,128)(2,1)}, bf16[4,8,1664]{2,1,0:T(8,128)(2,1)}) custom-call(bf16[16,64,768]{2,1,0:T(8,128)(2,1)} %x_ref.3, bf16[16,64,768]{2,1,0:T(8,128)(2,1)} %x_ref.3, bf16[16,64,768]{2,1,0:T(8,128)(2,1)} %x_ref.3, bf16[16,64,768]{2,1,0:T(8,128)(2,1)} %g_ref.3, ...), custom_call_target="tpu_custom_call" | custom-call | bytes 4000000 | tf_op jit(solution)/shard_map/pack/pallas_call | solution.py:83
  4.8 4.2 %collective-permute-start.2 = (bf16[4,32,1664]{2,1,0:T(8,128)(2,1)}, bf16[4,32,1664]{2,1,0:T(8,128)(2,1)S(1)}, u32[]{:S(2)}, u32[]{:S(2)}) collective-permute-start(bf16[4,32,1664]{2,1,0:T(8,128)(2,1)} %get-tuple-element.39), channel_id=1, source_target_pairs={{0,7},{1,0},{2,1},{3,2},{4,3},{5,4},{6,5},{7,6},{8,15},{9,8},{10,9... | collective-permute-start | bytes 1277960 | tf_op jit(solution)/shard_map/ppermute | solution.py:481
  9.0 5.2 %collective-permute-start.1 = (bf16[12,8,1664]{2,1,0:T(8,128)(2,1)}, bf16[12,8,1664]{2,1,0:T(8,128)(2,1)S(1)}, u32[]{:S(2)}, u32[]{:S(2)}) collective-permute-start(bf16[12,8,1664]{2,1,0:T(8,128)(2,1)} %get-tuple-element.38), channel_id=1, source_target_pairs={{0,120},{1,121},{2,122},{3,123},{4,124},{5,125},{6,126},{7,127},{8... | collective-permute-start | bytes 958472 | tf_op jit(solution)/shard_map/ppermute | solution.py:481
  14.3 9.1 %collective-permute-done.corner = bf16[4,8,1664]{2,1,0:T(8,128)(2,1)S(1)} collective-permute-done((bf16[4,8,1664]{2,1,0:T(8,128)(2,1)}, bf16[4,8,1664]{2,1,0:T(8,128)(2,1)S(1)}, u32[]{:S(2)}, u32[]{:S(2)}) %collective-permute-start) | collective-permute-done | bytes 106528 | tf_op jit(solution)/shard_map/ppermute | solution.py:481
  24.5 39.8 %attention.1 = (bf16[1024,768]{1,0:T(8,128)(2,1)}, bf16[1024,768]{1,0:T(8,128)(2,1)}, bf16[4,32,1536]{2,1,0:T(8,128)(2,1)}, bf16[4,32,1536]{2,1,0:T(8,128)(2,1)}...) custom-call(s32[1]{0:T(128)} %bitcast.core_ref, ...), custom_call_target="tpu_custom_call" | custom-call | flops 16000000000 | bytes 25000000 | tf_op jit(solution)/shard_map/attention/pallas_call | solution.py:248
  64.3 2.3 %collective-permute-start.4 = (bf16[1536,768]{1,0:T(8,128)(2,1)}, bf16[1536,768]{1,0:T(8,128)(2,1)S(1)}, u32[]{:S(2)}, u32[]{:S(2)}) collective-permute-start(bf16[1536,768]{1,0:T(8,128)(2,1)} %get-tuple-element.44), channel_id=1, source_target_pairs={{0,8},{1,9},{2,10},{3,11},{4,12},{5,13},{6,14},{7,15},{8,0},{9,1},... | collective-permute-start | bytes 7077896 | tf_op jit(solution)/shard_map/ppermute | solution.py:433
  66.8 4.3 %collective-permute-done.4.recv = bf16[1536,768]{1,0:T(8,128)(2,1)S(1)} collective-permute-done((bf16[1536,768]{1,0:T(8,128)(2,1)}, bf16[1536,768]{1,0:T(8,128)(2,1)S(1)}, u32[]{:S(2)}, u32[]{:S(2)}) %collective-permute-start.4) | collective-permute-done | bytes 2359328 | tf_op jit(solution)/shard_map/ppermute | solution.py:433
  71.1 1.7 %copy-done.2 = bf16[1536,768]{1,0:T(8,128)(2,1)S(1)} copy-done((bf16[1536,768]{1,0:T(8,128)(2,1)S(1)}, bf16[1536,768]{1,0:T(8,128)(2,1)}, u32[]{:S(2)}) %copy-start.2) | copy-done | bytes 2359320
  72.7 2.0 %combine.1 = (bf16[256,768]{1,0:T(8,128)(2,1)S(1)}, bf16[256,768]{1,0:T(8,128)(2,1)S(1)}, bf16[256,768]{1,0:T(8,128)(2,1)S(1)}, bf16[256,768]{1,0:T(8,128)(2,1)}...) custom-call(s32[3]{0:T(128)S(1)} %pad_add_fusion.bits, bf16[1536,768]{1,0:T(8,128)(2,1)S(1)} %copy-done.2, ...), custom_call_target="tpu_custom_call" | custom-call | flops 1200000 | bytes 7000000 | tf_op jit(solution)/shard_map/combine/pallas_call | solution.py:324
  75.5 1.6 collective-permute-start.13
  77.2 6.3 %collective-permute-done.5 = bf16[256,768]{1,0:T(8,128)(2,1)S(1)} collective-permute-done((bf16[256,768]{1,0:T(8,128)(2,1)}, bf16[256,768]{1,0:T(8,128)(2,1)S(1)}, u32[]{:S(2)}, u32[]{:S(2)}) %collective-permute-start.5) | collective-permute-done | bytes 393248 | tf_op jit(solution)/shard_map/ppermute | solution.py:433
  83.6 1.7 %collective-permute-start.6 = (bf16[128,768]{1,0:T(8,128)(2,1)S(1)}, bf16[128,768]{1,0:T(8,128)(2,1)S(1)}, u32[]{:S(2)}, u32[]{:S(2)}) collective-permute-start(bf16[128,768]{1,0:T(8,128)(2,1)S(1)} %constant_dynamic-slice_fusion.2), channel_id=1, source_target_pairs={{0,16},{1,17},{2,18},{3,19},{4,20},{5,21},{6,22},{7,23},{8,56},{9,... | collective-permute-start | bytes 589832 | tf_op jit(solution)/shard_map/ppermute | solution.py:433
  85.8 1.6 collective-permute-start.22
  87.3 2.1 %collective-permute-done.6 = bf16[128,768]{1,0:T(8,128)(2,1)S(1)} collective-permute-done((bf16[128,768]{1,0:T(8,128)(2,1)S(1)}, bf16[128,768]{1,0:T(8,128)(2,1)S(1)}, u32[]{:S(2)}, u32[]{:S(2)}) %collective-permute-start.6) | collective-permute-done | bytes 196640 | tf_op jit(solution)/shard_map/ppermute | solution.py:433
  91.6 1.7 %collective-permute-start.23 = (bf16[128,768]{1,0:T(8,128)(2,1)S(1)}, bf16[128,768]{1,0:T(8,128)(2,1)S(1)}, u32[]{:S(2)}, u32[]{:S(2)}) collective-permute-start(bf16[128,768]{1,0:T(8,128)(2,1)S(1)} %add_convert_fusion.7), channel_id=1, source_target_pairs={{0,16},{1,17},{2,18},{3,19},{4,20},{5,21},{6,22},{7,23},{8,56},{9,... | collective-permute-start | bytes 589832 | tf_op jit(solution)/shard_map/ppermute | solution.py:433
  93.3 2.1 %collective-permute-done.7 = bf16[128,768]{1,0:T(8,128)(2,1)S(1)} collective-permute-done((bf16[128,768]{1,0:T(8,128)(2,1)S(1)}, bf16[128,768]{1,0:T(8,128)(2,1)S(1)}, u32[]{:S(2)}, u32[]{:S(2)}) %collective-permute-start.7) | collective-permute-done | bytes 196640 | tf_op jit(solution)/shard_map/ppermute | solution.py:433
  97.0 5.3 %collective-permute-start.16 = (bf16[128,768]{1,0:T(8,128)(2,1)S(1)}, bf16[128,768]{1,0:T(8,128)(2,1)S(1)}, u32[]{:S(2)}, u32[]{:S(2)}) collective-permute-start(bf16[128,768]{1,0:T(8,128)(2,1)S(1)} %add_convert_fusion.11), channel_id=1, source_target_pairs={{0,48},{1,49},{2,50},{3,51},{4,52},{5,53},{6,54},{7,55},{8,24},{9,... | collective-permute-start | bytes 589832 | tf_op jit(solution)/shard_map/ppermute | solution.py:433
  102.4 2.6 %collective-permute-start.24 = (bf16[128,768]{1,0:T(8,128)(2,1)S(1)}, bf16[128,768]{1,0:T(8,128)(2,1)S(1)}, u32[]{:S(2)}, u32[]{:S(2)}) collective-permute-start(bf16[128,768]{1,0:T(8,128)(2,1)S(1)} %add_convert_fusion.6), channel_id=1, source_target_pairs={{0,68},{1,69},{2,70},{3,71},{4,64},{5,65},{6,66},{7,67},{8,12},{9,... | collective-permute-start | bytes 589832 | tf_op jit(solution)/shard_map/ppermute | solution.py:433
  105.1 2.3 %collective-permute-start.9 = (bf16[128,768]{1,0:T(8,128)(2,1)S(1)}, bf16[128,768]{1,0:T(8,128)(2,1)S(1)}, u32[]{:S(2)}, u32[]{:S(2)}) collective-permute-start(bf16[128,768]{1,0:T(8,128)(2,1)S(1)} %add_convert_fusion.15), channel_id=1, source_target_pairs={{0,48},{1,49},{2,50},{3,51},{4,52},{5,53},{6,54},{7,55},{8,24},{9,... | collective-permute-start | bytes 589832 | tf_op jit(solution)/shard_map/ppermute | solution.py:433
  107.4 2.6 %collective-permute-start.17 = (bf16[128,768]{1,0:T(8,128)(2,1)S(1)}, bf16[128,768]{1,0:T(8,128)(2,1)S(1)}, u32[]{:S(2)}, u32[]{:S(2)}) collective-permute-start(bf16[128,768]{1,0:T(8,128)(2,1)S(1)} %add_convert_fusion.10), channel_id=1, source_target_pairs={{0,68},{1,69},{2,70},{3,71},{4,64},{5,65},{6,66},{7,67},{8,12},{9,... | collective-permute-start | bytes 589832 | tf_op jit(solution)/shard_map/ppermute | solution.py:433
  112.1 1.5 collective-permute-start.10
  117.1 2.0 %collective-permute-start.26 = (bf16[128,768]{1,0:T(8,128)(2,1)S(1)}, bf16[128,768]{1,0:T(8,128)(2,1)S(1)}, u32[]{:S(2)}, u32[]{:S(2)}) collective-permute-start(bf16[128,768]{1,0:T(8,128)(2,1)S(1)} %add_convert_fusion.4), channel_id=1, source_target_pairs={{0,48},{1,49},{2,50},{3,51},{4,52},{5,53},{6,54},{7,55},{8,24},{9,... | collective-permute-start | bytes 589832 | tf_op jit(solution)/shard_map/ppermute | solution.py:433
  119.6 1.8 %collective-permute-done.18 = bf16[128,768]{1,0:T(8,128)(2,1)S(1)} collective-permute-done((bf16[128,768]{1,0:T(8,128)(2,1)S(1)}, bf16[128,768]{1,0:T(8,128)(2,1)S(1)}, u32[]{:S(2)}, u32[]{:S(2)}) %collective-permute-start.18) | collective-permute-done | bytes 196640 | tf_op jit(solution)/shard_map/ppermute | solution.py:433
  121.5 2.5 %collective-permute-done.26 = bf16[128,768]{1,0:T(8,128)(2,1)S(1)} collective-permute-done((bf16[128,768]{1,0:T(8,128)(2,1)S(1)}, bf16[128,768]{1,0:T(8,128)(2,1)S(1)}, u32[]{:S(2)}, u32[]{:S(2)}) %collective-permute-start.26) | collective-permute-done | bytes 196640 | tf_op jit(solution)/shard_map/ppermute | solution.py:433
  127.2 1.5 collective-permute-start.20
  130.3 3.8 %collective-permute-done.12.refs_1_ = bf16[256,768]{1,0:T(8,128)(2,1)S(1)} collective-permute-done((bf16[256,768]{1,0:T(8,128)(2,1)S(1)}, bf16[256,768]{1,0:T(8,128)(2,1)S(1)}, u32[]{:S(2)}, u32[]{:S(2)}) %collective-permute-start.12) | collective-permute-done | bytes 393248 | tf_op jit(solution)/shard_map/ppermute | solution.py:433
  135.1 2.7 %collective-permute-done.28.refs_5_ = bf16[256,768]{1,0:T(8,128)(2,1)S(1)} collective-permute-done((bf16[256,768]{1,0:T(8,128)(2,1)S(1)}, bf16[256,768]{1,0:T(8,128)(2,1)S(1)}, u32[]{:S(2)}, u32[]{:S(2)}) %collective-permute-start.28) | collective-permute-done | bytes 393248 | tf_op jit(solution)/shard_map/ppermute | solution.py:433
  138.9 1.9 %collective-permute-start.32 = (bf16[4,32,1536]{2,1,0:T(8,128)(2,1)S(1)}, bf16[4,32,1536]{2,1,0:T(8,128)(2,1)S(1)}, u32[]{:S(2)}, u32[]{:S(2)}) collective-permute-start(bf16[4,32,1536]{2,1,0:T(8,128)(2,1)S(1)} %copy-done.8), channel_id=1, source_target_pairs={{0,1},{1,2},{2,3},{3,4},{4,5},{5,6},{6,7},{7,0},{8,9},{9,10},{10,1... | collective-permute-start | bytes 1179656 | tf_op jit(solution)/shard_map/ppermute | solution.py:481
  140.8 2.2 %collective-permute-start.29 = (bf16[4,8,1536]{2,1,0:T(8,128)(2,1)S(1)}, bf16[4,8,1536]{2,1,0:T(8,128)(2,1)S(1)}, u32[]{:S(2)}, u32[]{:S(2)}) collective-permute-start(bf16[4,8,1536]{2,1,0:T(8,128)(2,1)S(1)} %copy-done.13), channel_id=1, source_target_pairs={{0,15},{1,8},{2,9},{3,10},{4,11},{5,12},{6,13},{7,14},{8,23},{9,16... | collective-permute-start | bytes 294920 | tf_op jit(solution)/shard_map/ppermute | solution.py:481
  143.2 5.2 %widen.1 = (f32[768,2304]{1,0:T(8,128)}, f32[768,768]{1,0:T(8,128)}) custom-call(s32[1]{0:T(128)} %bitcast.core_ref, bf16[1536,768]{1,0:T(8,128)(2,1)S(1)} %join.7.own, bf16[1536,768]{1,0:T(8,128)(2,1)S(1)} %collective-permute-done.33.other), custom_call_target="tpu_custom_call" | custom-call | bytes 14000000 | tf_op jit(solution)/shard_map/widen/pallas_call | solution.py:387
  148.4 8.3 %collective-permute-done.29.corner = bf16[4,8,1536]{2,1,0:T(8,128)(2,1)S(1)} collective-permute-done((bf16[4,8,1536]{2,1,0:T(8,128)(2,1)S(1)}, bf16[4,8,1536]{2,1,0:T(8,128)(2,1)S(1)}, u32[]{:S(2)}, u32[]{:S(2)}) %collective-permute-start.29) | collective-permute-done | bytes 98336 | tf_op jit(solution)/shard_map/ppermute | solution.py:481
  156.7 2.3 %merge.1 = (bf16[16,64,768]{2,1,0:T(8,128)(2,1)}, bf16[16,64,768]{2,1,0:T(8,128)(2,1)}) custom-call(bf16[16,64,768]{2,1,0:T(8,128)(2,1)S(1)} %copy-done, bf16[16,64,768]{2,1,0:T(8,128)(2,1)S(1)} %copy-done.1, bf16[1024,768]{1,0:T(8,128)(2,1)S(1)} %copy-done.3, bf16[1024,768]{1,0:T(8,128)(2,1)S(1)} %copy-done.4, ...), custom_call_target="tpu_custom_call" | custom-call | flops 3000000 | bytes 11000000 | tf_op jit(solution)/shard_map/merge/pallas_call | solution.py:302
  (97 shorter events, 21.4 us)
Async XLA Ops:
  4.8 18.6 %collective-permute-start.2 = (bf16[4,32,1664]{2,1,0:T(8,128)(2,1)}, bf16[4,32,1664]{2,1,0:T(8,128)(2,1)S(1)}, u32[]{:S(2)}, u32[]{:S(2)}) collective-permute-start(bf16[4,32,1664]{2,1,0:T(8,128)(2,1)} %get-tuple-element.39), channel_id=1, source_target_pairs={{0,7},{1,0},{2,1},{3,2},{4,3},{5,4},{6,5},{7,6},{8,15},{9,8},{10,9... | collective-permute-start | bytes 1277960 | tf_op jit(solution)/shard_map/ppermute | solution.py:481
  9.0 14.7 %collective-permute-start.3 = (bf16[4,32,1664]{2,1,0:T(8,128)(2,1)}, bf16[4,32,1664]{2,1,0:T(8,128)(2,1)S(1)}, u32[]{:S(2)}, u32[]{:S(2)}) collective-permute-start(bf16[4,32,1664]{2,1,0:T(8,128)(2,1)} %get-tuple-element.40), channel_id=1, source_target_pairs={{0,1},{1,2},{2,3},{3,4},{4,5},{5,6},{6,7},{7,0},{8,9},{9,10},{10,1... | collective-permute-start | bytes 1277960 | tf_op jit(solution)/shard_map/ppermute | solution.py:481
  9.0 14.4 %collective-permute-start.1 = (bf16[12,8,1664]{2,1,0:T(8,128)(2,1)}, bf16[12,8,1664]{2,1,0:T(8,128)(2,1)S(1)}, u32[]{:S(2)}, u32[]{:S(2)}) collective-permute-start(bf16[12,8,1664]{2,1,0:T(8,128)(2,1)} %get-tuple-element.38), channel_id=1, source_target_pairs={{0,120},{1,121},{2,122},{3,123},{4,124},{5,125},{6,126},{7,127},{8... | collective-permute-start | bytes 958472 | tf_op jit(solution)/shard_map/ppermute | solution.py:481
  14.2 9.2 %collective-permute-start = (bf16[4,8,1664]{2,1,0:T(8,128)(2,1)}, bf16[4,8,1664]{2,1,0:T(8,128)(2,1)S(1)}, u32[]{:S(2)}, u32[]{:S(2)}) collective-permute-start(bf16[4,8,1664]{2,1,0:T(8,128)(2,1)} %get-tuple-element.37), channel_id=1, source_target_pairs={{0,121},{1,122},{2,123},{3,124},{4,125},{5,126},{6,127},{7,120},{8... | collective-permute-start | bytes 319496 | tf_op jit(solution)/shard_map/ppermute | solution.py:481
  64.3 6.7 %collective-permute-start.4 = (bf16[1536,768]{1,0:T(8,128)(2,1)}, bf16[1536,768]{1,0:T(8,128)(2,1)S(1)}, u32[]{:S(2)}, u32[]{:S(2)}) collective-permute-start(bf16[1536,768]{1,0:T(8,128)(2,1)} %get-tuple-element.44), channel_id=1, source_target_pairs={{0,8},{1,9},{2,10},{3,11},{4,12},{5,13},{6,14},{7,15},{8,0},{9,1},... | collective-permute-start | bytes 7077896 | tf_op jit(solution)/shard_map/ppermute | solution.py:433
  75.5 8.0 %collective-permute-start.5 = (bf16[256,768]{1,0:T(8,128)(2,1)}, bf16[256,768]{1,0:T(8,128)(2,1)S(1)}, u32[]{:S(2)}, u32[]{:S(2)}) collective-permute-start(bf16[256,768]{1,0:T(8,128)(2,1)} %get-tuple-element.46), channel_id=1, source_target_pairs={{0,1},{1,0},{2,3},{3,2},{4,5},{5,4},{6,7},{7,6},{8,11},{9,10},{10,... | collective-permute-start | bytes 1179656 | tf_op jit(solution)/shard_map/ppermute | solution.py:433
  75.5 9.8 %collective-permute-start.13 = (bf16[256,768]{1,0:T(8,128)(2,1)}, bf16[256,768]{1,0:T(8,128)(2,1)S(1)}, u32[]{:S(2)}, u32[]{:S(2)}) collective-permute-start(bf16[256,768]{1,0:T(8,128)(2,1)} %get-tuple-element.48), channel_id=1, source_target_pairs={{0,16},{1,17},{2,18},{3,19},{4,20},{5,21},{6,22},{7,23},{8,56},{9,... | collective-permute-start | bytes 1179656 | tf_op jit(solution)/shard_map/ppermute | solution.py:433
  77.1 8.5 %collective-permute-start.21 = (bf16[256,768]{1,0:T(8,128)(2,1)}, bf16[256,768]{1,0:T(8,128)(2,1)S(1)}, u32[]{:S(2)}, u32[]{:S(2)}) collective-permute-start(bf16[256,768]{1,0:T(8,128)(2,1)} %copy-done.5), channel_id=1, source_target_pairs={{0,4},{1,5},{2,6},{3,7},{4,0},{5,1},{6,2},{7,3},{8,76},{9,77},{10,... | collective-permute-start | bytes 1179656 | tf_op jit(solution)/shard_map/ppermute | solution.py:433
  83.6 5.7 %collective-permute-start.6 = (bf16[128,768]{1,0:T(8,128)(2,1)S(1)}, bf16[128,768]{1,0:T(8,128)(2,1)S(1)}, u32[]{:S(2)}, u32[]{:S(2)}) collective-permute-start(bf16[128,768]{1,0:T(8,128)(2,1)S(1)} %constant_dynamic-slice_fusion.2), channel_id=1, source_target_pairs={{0,16},{1,17},{2,18},{3,19},{4,20},{5,21},{6,22},{7,23},{8,56},{9,... | collective-permute-start | bytes 589832 | tf_op jit(solution)/shard_map/ppermute | solution.py:433
  85.4 5.8 %collective-permute-start.14 = (bf16[128,768]{1,0:T(8,128)(2,1)S(1)}, bf16[128,768]{1,0:T(8,128)(2,1)S(1)}, u32[]{:S(2)}, u32[]{:S(2)}) collective-permute-start(bf16[128,768]{1,0:T(8,128)(2,1)S(1)} %constant_dynamic-slice_fusion.1), channel_id=1, source_target_pairs={{0,4},{1,5},{2,6},{3,7},{4,0},{5,1},{6,2},{7,3},{8,76},{9,77},{10,... | collective-permute-start | bytes 589832 | tf_op jit(solution)/shard_map/ppermute | solution.py:433
  85.8 5.8 %collective-permute-start.22 = (bf16[128,768]{1,0:T(8,128)(2,1)S(1)}, bf16[128,768]{1,0:T(8,128)(2,1)S(1)}, u32[]{:S(2)}, u32[]{:S(2)}) collective-permute-start(bf16[128,768]{1,0:T(8,128)(2,1)S(1)} %constant_dynamic-slice_fusion), channel_id=1, source_target_pairs={{0,1},{1,0},{2,3},{3,2},{4,5},{5,4},{6,7},{7,6},{8,11},{9,10},{10,... | collective-permute-start | bytes 589832 | tf_op jit(solution)/shard_map/ppermute | solution.py:433
  89.5 5.9 %collective-permute-start.7 = (bf16[128,768]{1,0:T(8,128)(2,1)S(1)}, bf16[128,768]{1,0:T(8,128)(2,1)S(1)}, u32[]{:S(2)}, u32[]{:S(2)}) collective-permute-start(bf16[128,768]{1,0:T(8,128)(2,1)S(1)} %add_convert_fusion.17), channel_id=1, source_target_pairs={{0,4},{1,5},{2,6},{3,7},{4,0},{5,1},{6,2},{7,3},{8,76},{9,77},{10,... | collective-permute-start | bytes 589832 | tf_op jit(solution)/shard_map/ppermute | solution.py:433
  91.2 5.7 %collective-permute-start.15 = (bf16[128,768]{1,0:T(8,128)(2,1)S(1)}, bf16[128,768]{1,0:T(8,128)(2,1)S(1)}, u32[]{:S(2)}, u32[]{:S(2)}) collective-permute-start(bf16[128,768]{1,0:T(8,128)(2,1)S(1)} %add_convert_fusion.12), channel_id=1, source_target_pairs={{0,1},{1,0},{2,3},{3,2},{4,5},{5,4},{6,7},{7,6},{8,11},{9,10},{10,... | collective-permute-start | bytes 589832 | tf_op jit(solution)/shard_map/ppermute | solution.py:433
  91.6 10.8 %collective-permute-start.23 = (bf16[128,768]{1,0:T(8,128)(2,1)S(1)}, bf16[128,768]{1,0:T(8,128)(2,1)S(1)}, u32[]{:S(2)}, u32[]{:S(2)}) collective-permute-start(bf16[128,768]{1,0:T(8,128)(2,1)S(1)} %add_convert_fusion.7), channel_id=1, source_target_pairs={{0,16},{1,17},{2,18},{3,19},{4,20},{5,21},{6,22},{7,23},{8,56},{9,... | collective-permute-start | bytes 589832 | tf_op jit(solution)/shard_map/ppermute | solution.py:433
  95.4 9.6 %collective-permute-start.8 = (bf16[128,768]{1,0:T(8,128)(2,1)S(1)}, bf16[128,768]{1,0:T(8,128)(2,1)S(1)}, u32[]{:S(2)}, u32[]{:S(2)}) collective-permute-start(bf16[128,768]{1,0:T(8,128)(2,1)S(1)} %add_convert_fusion.16), channel_id=1, source_target_pairs={{0,3},{1,2},{2,1},{3,0},{4,7},{5,6},{6,5},{7,4},{8,9},{9,8},{10,11... | collective-permute-start | bytes 589832 | tf_op jit(solution)/shard_map/ppermute | solution.py:433
  97.0 10.3 %collective-permute-start.16 = (bf16[128,768]{1,0:T(8,128)(2,1)S(1)}, bf16[128,768]{1,0:T(8,128)(2,1)S(1)}, u32[]{:S(2)}, u32[]{:S(2)}) collective-permute-start(bf16[128,768]{1,0:T(8,128)(2,1)S(1)} %add_convert_fusion.11), channel_id=1, source_target_pairs={{0,48},{1,49},{2,50},{3,51},{4,52},{5,53},{6,54},{7,55},{8,24},{9,... | collective-permute-start | bytes 589832 | tf_op jit(solution)/shard_map/ppermute | solution.py:433
  102.4 7.6 %collective-permute-start.24 = (bf16[128,768]{1,0:T(8,128)(2,1)S(1)}, bf16[128,768]{1,0:T(8,128)(2,1)S(1)}, u32[]{:S(2)}, u32[]{:S(2)}) collective-permute-start(bf16[128,768]{1,0:T(8,128)(2,1)S(1)} %add_convert_fusion.6), channel_id=1, source_target_pairs={{0,68},{1,69},{2,70},{3,71},{4,64},{5,65},{6,66},{7,67},{8,12},{9,... | collective-permute-start | bytes 589832 | tf_op jit(solution)/shard_map/ppermute | solution.py:433
  105.1 7.0 %collective-permute-start.9 = (bf16[128,768]{1,0:T(8,128)(2,1)S(1)}, bf16[128,768]{1,0:T(8,128)(2,1)S(1)}, u32[]{:S(2)}, u32[]{:S(2)}) collective-permute-start(bf16[128,768]{1,0:T(8,128)(2,1)S(1)} %add_convert_fusion.15), channel_id=1, source_target_pairs={{0,48},{1,49},{2,50},{3,51},{4,52},{5,53},{6,54},{7,55},{8,24},{9,... | collective-permute-start | bytes 589832 | tf_op jit(solution)/shard_map/ppermute | solution.py:433
  107.4 7.0 %collective-permute-start.17 = (bf16[128,768]{1,0:T(8,128)(2,1)S(1)}, bf16[128,768]{1,0:T(8,128)(2,1)S(1)}, u32[]{:S(2)}, u32[]{:S(2)}) collective-permute-start(bf16[128,768]{1,0:T(8,128)(2,1)S(1)} %add_convert_fusion.10), channel_id=1, source_target_pairs={{0,68},{1,69},{2,70},{3,71},{4,64},{5,65},{6,66},{7,67},{8,12},{9,... | collective-permute-start | bytes 589832 | tf_op jit(solution)/shard_map/ppermute | solution.py:433
  110.1 7.0 %collective-permute-start.25 = (bf16[128,768]{1,0:T(8,128)(2,1)S(1)}, bf16[128,768]{1,0:T(8,128)(2,1)S(1)}, u32[]{:S(2)}, u32[]{:S(2)}) collective-permute-start(bf16[128,768]{1,0:T(8,128)(2,1)S(1)} %add_convert_fusion.5), channel_id=1, source_target_pairs={{0,3},{1,2},{2,1},{3,0},{4,7},{5,6},{6,5},{7,4},{8,9},{9,8},{10,11... | collective-permute-start | bytes 589832 | tf_op jit(solution)/shard_map/ppermute | solution.py:433
  112.1 7.0 %collective-permute-start.10 = (bf16[128,768]{1,0:T(8,128)(2,1)S(1)}, bf16[128,768]{1,0:T(8,128)(2,1)S(1)}, u32[]{:S(2)}, u32[]{:S(2)}) collective-permute-start(bf16[128,768]{1,0:T(8,128)(2,1)S(1)} %add_convert_fusion.14), channel_id=1, source_target_pairs={{0,68},{1,69},{2,70},{3,71},{4,64},{5,65},{6,66},{7,67},{8,12},{9,... | collective-permute-start | bytes 589832 | tf_op jit(solution)/shard_map/ppermute | solution.py:433
  114.4 7.0 %collective-permute-start.18 = (bf16[128,768]{1,0:T(8,128)(2,1)S(1)}, bf16[128,768]{1,0:T(8,128)(2,1)S(1)}, u32[]{:S(2)}, u32[]{:S(2)}) collective-permute-start(bf16[128,768]{1,0:T(8,128)(2,1)S(1)} %add_convert_fusion.9), channel_id=1, source_target_pairs={{0,3},{1,2},{2,1},{3,0},{4,7},{5,6},{6,5},{7,4},{8,9},{9,8},{10,11... | collective-permute-start | bytes 589832 | tf_op jit(solution)/shard_map/ppermute | solution.py:433
  117.1 7.0 %collective-permute-start.26 = (bf16[128,768]{1,0:T(8,128)(2,1)S(1)}, bf16[128,768]{1,0:T(8,128)(2,1)S(1)}, u32[]{:S(2)}, u32[]{:S(2)}) collective-permute-start(bf16[128,768]{1,0:T(8,128)(2,1)S(1)} %add_convert_fusion.4), channel_id=1, source_target_pairs={{0,48},{1,49},{2,50},{3,51},{4,52},{5,53},{6,54},{7,55},{8,24},{9,... | collective-permute-start | bytes 589832 | tf_op jit(solution)/shard_map/ppermute | solution.py:433
  119.2 5.7 %collective-permute-start.11 = (bf16[128,768]{1,0:T(8,128)(2,1)S(1)}, bf16[128,768]{1,0:T(8,128)(2,1)S(1)}, u32[]{:S(2)}, u32[]{:S(2)}) collective-permute-start(bf16[128,768]{1,0:T(8,128)(2,1)S(1)} %add_convert_fusion.13.refs_0_), channel_id=1, source_target_pairs={{0,16},{1,17},{2,18},{3,19},{4,20},{5,21},{6,22},{7,23},{8,56},{9,... | collective-permute-start | bytes 589832 | tf_op jit(solution)/shard_map/ppermute | solution.py:433
  121.5 5.8 %collective-permute-start.19 = (bf16[128,768]{1,0:T(8,128)(2,1)S(1)}, bf16[128,768]{1,0:T(8,128)(2,1)S(1)}, u32[]{:S(2)}, u32[]{:S(2)}) collective-permute-start(bf16[128,768]{1,0:T(8,128)(2,1)S(1)} %add_convert_fusion.8.refs_0_), channel_id=1, source_target_pairs={{0,4},{1,5},{2,6},{3,7},{4,0},{5,1},{6,2},{7,3},{8,76},{9,77},{10,... | collective-permute-start | bytes 589832 | tf_op jit(solution)/shard_map/ppermute | solution.py:433
  124.9 9.1 %collective-permute-start.12 = (bf16[256,768]{1,0:T(8,128)(2,1)S(1)}, bf16[256,768]{1,0:T(8,128)(2,1)S(1)}, u32[]{:S(2)}, u32[]{:S(2)}) collective-permute-start(bf16[256,768]{1,0:T(8,128)(2,1)S(1)} %join.4.refs_0_), channel_id=1, source_target_pairs={{0,1},{1,0},{2,3},{3,2},{4,5},{5,4},{6,7},{7,6},{8,11},{9,10},{10,... | collective-permute-start | bytes 1179656 | tf_op jit(solution)/shard_map/ppermute | solution.py:433
  127.2 7.9 %collective-permute-start.20 = (bf16[256,768]{1,0:T(8,128)(2,1)S(1)}, bf16[256,768]{1,0:T(8,128)(2,1)S(1)}, u32[]{:S(2)}, u32[]{:S(2)}) collective-permute-start(bf16[256,768]{1,0:T(8,128)(2,1)S(1)} %join.5.refs_2_), channel_id=1, source_target_pairs={{0,16},{1,17},{2,18},{3,19},{4,20},{5,21},{6,22},{7,23},{8,56},{9,... | collective-permute-start | bytes 1179656 | tf_op jit(solution)/shard_map/ppermute | solution.py:433
  129.9 7.9 %collective-permute-start.28 = (bf16[256,768]{1,0:T(8,128)(2,1)S(1)}, bf16[256,768]{1,0:T(8,128)(2,1)S(1)}, u32[]{:S(2)}, u32[]{:S(2)}) collective-permute-start(bf16[256,768]{1,0:T(8,128)(2,1)S(1)} %join.6.refs_4_), channel_id=1, source_target_pairs={{0,4},{1,5},{2,6},{3,7},{4,0},{5,1},{6,2},{7,3},{8,76},{9,77},{10,... | collective-permute-start | bytes 1179656 | tf_op jit(solution)/shard_map/ppermute | solution.py:433
  138.6 18.0 %collective-permute-start.31 = (bf16[4,32,1536]{2,1,0:T(8,128)(2,1)S(1)}, bf16[4,32,1536]{2,1,0:T(8,128)(2,1)S(1)}, u32[]{:S(2)}, u32[]{:S(2)}) collective-permute-start(bf16[4,32,1536]{2,1,0:T(8,128)(2,1)S(1)} %copy-done.9), channel_id=1, source_target_pairs={{0,7},{1,0},{2,1},{3,2},{4,3},{5,4},{6,5},{7,6},{8,15},{9,8},{10,9... | collective-permute-start | bytes 1179656 | tf_op jit(solution)/shard_map/ppermute | solution.py:481
  138.9 17.8 %collective-permute-start.32 = (bf16[4,32,1536]{2,1,0:T(8,128)(2,1)S(1)}, bf16[4,32,1536]{2,1,0:T(8,128)(2,1)S(1)}, u32[]{:S(2)}, u32[]{:S(2)}) collective-permute-start(bf16[4,32,1536]{2,1,0:T(8,128)(2,1)S(1)} %copy-done.8), channel_id=1, source_target_pairs={{0,1},{1,2},{2,3},{3,4},{4,5},{5,6},{6,7},{7,0},{8,9},{9,10},{10,1... | collective-permute-start | bytes 1179656 | tf_op jit(solution)/shard_map/ppermute | solution.py:481
  140.7 15.9 %collective-permute-start.30 = (bf16[12,8,1536]{2,1,0:T(8,128)(2,1)S(1)}, bf16[12,8,1536]{2,1,0:T(8,128)(2,1)S(1)}, u32[]{:S(2)}, u32[]{:S(2)}) collective-permute-start(bf16[12,8,1536]{2,1,0:T(8,128)(2,1)S(1)} %copy-done.11), channel_id=1, source_target_pairs={{0,8},{1,9},{2,10},{3,11},{4,12},{5,13},{6,14},{7,15},{8,16},{9,17... | collective-permute-start | bytes 884744 | tf_op jit(solution)/shard_map/ppermute | solution.py:481
  140.8 15.9 %collective-permute-start.29 = (bf16[4,8,1536]{2,1,0:T(8,128)(2,1)S(1)}, bf16[4,8,1536]{2,1,0:T(8,128)(2,1)S(1)}, u32[]{:S(2)}, u32[]{:S(2)}) collective-permute-start(bf16[4,8,1536]{2,1,0:T(8,128)(2,1)S(1)} %copy-done.13), channel_id=1, source_target_pairs={{0,15},{1,8},{2,9},{3,10},{4,11},{5,12},{6,13},{7,14},{8,23},{9,16... | collective-permute-start | bytes 294920 | tf_op jit(solution)/shard_map/ppermute | solution.py:481
  (16 other events, 128.7 us)

commit v5 on v4

--- a/solution.py
+++ b/solution.py
@@ -54,6 +54,16 @@
     return t[:, 8 * j : 8 * j + 8, :]
 
 
+def fold(t):
+    t = t.astype(F32)
+    return seam(pltpu.roll(t[6:12], 4, 1), t[0:6]).astype(BF16)
+
+
+def unfold(t):
+    t = t.astype(F32)
+    return jnp.concatenate([t, pltpu.roll(t, 4, 1)], 0)
+
+
 def pack_body(*refs):
     ins, (up, down, left, corner) = refs[:9], refs[9:]
     lane = 0
@@ -66,7 +76,7 @@
         for j in range(3):
             down[:, 8 * j : 8 * j + 8, lanes] = seam(tile_of(bottom, j + 4), tile_of(bottom, j + 5))
         down[:, 24:32, lanes] = tile_of(bottom, 7)
-        left[:, :, lanes] = strip[0:12]
+        left[:, :, lanes] = fold(strip[0:12])
         corner[:, :, lanes] = tile_of(bottom, 0)
 
 
@@ -79,7 +89,7 @@
             pl.BlockSpec((4, 64, w), lambda i: (3, 0, 0)),
             pl.BlockSpec((16, 8, w), lambda i: (0, 0, 0)),
         ]
-    shapes = [(4, 32, F), (4, 32, F), (12, 8, F), (4, 8, F)]
+    shapes = [(4, 32, F), (4, 32, F), (6, 8, F), (4, 8, F)]
     return pl.pallas_call(
         pack_body,
         grid=(1,),
@@ -94,14 +104,15 @@
 
 def window_pieces(src, below, above, right, corner, lanes):
     out = []
+    right = unfold(right[:, :, lanes]).astype(BF16)
     for j in range(8):
-        nxt = tile_of(src[4:12], j + 1) if j < 7 else right[4:12, :, lanes]
+        nxt = tile_of(src[4:12], j + 1) if j < 7 else right[4:12]
         out.append(seam(tile_of(src[4:12], j), nxt))
     for j in range(4):
         own = seam(tile_of(src[12:16], j), tile_of(src[12:16], j + 1))
         out.append(jnp.concatenate([own, tile_of(below, j)[:, :, lanes]], 0))
     for j in range(4):
-        nxt = tile_of(src[0:4], j + 5) if j < 3 else right[0:4, :, lanes]
+        nxt = tile_of(src[0:4], j + 5) if j < 3 else right[0:4]
         own = seam(tile_of(src[0:4], j + 4), nxt)
         top = tile_of(above, j)[:, :, lanes]
         if j == 3:
@@ -232,8 +243,7 @@
                 at = slice(8 * j, 8 * j + 8)
                 up[:, at, lanes] = piece(12 + j)[0:4]
                 down[:, at, lanes] = piece(8 + j)[4:8]
-            side[0:4, :, lanes] = piece(15)[4:8]
-            side[4:12, :, lanes] = piece(7)
+            side[:, :, lanes] = fold(jnp.concatenate([piece(15)[4:8], piece(7)], 0))
             edge[:, :, lanes] = piece(15)[0:4]
 
 
@@ -244,7 +254,7 @@
     far = pl.BlockSpec(memory_space=pl.ANY)
     tok = jax.ShapeDtypeStruct((TOKENS, D), BF16)
     halves = jax.ShapeDtypeStruct((1536, D), BF16)
-    borders = [jax.ShapeDtypeStruct((r, c, 2 * D), BF16) for r, c in ((4, 32), (4, 32), (12, 8), (4, 8))]
+    borders = [jax.ShapeDtypeStruct((r, c, 2 * D), BF16) for r, c in ((4, 32), (4, 32), (6, 8), (4, 8))]
     return pl.pallas_call(
         attn_body,
         grid_spec=pltpu.PrefetchScalarGridSpec(
@@ -287,9 +297,10 @@
     ):
         piece = lambda w: win[64 * w : 64 * w + 64, :].astype(F32).reshape(8, 8, D)
         far = lambda t, j: tile_of(t, j)[:, :, lanes].astype(F32)
-        mids = [left[4:12, :, lanes].astype(F32)] + [piece(j) for j in range(8)]
+        first = unfold(left[:, :, lanes])
+        mids = [first[4:12]] + [piece(j) for j in range(8)]
         lows = [corner[:, :, lanes].astype(F32)] + [piece(8 + j)[0:4] for j in range(4)] + [far(below, j) for j in range(4)]
-        tops = [left[0:4, :, lanes].astype(F32)] + [far(above, j) for j in range(4)] + [piece(12 + j)[4:8] for j in range(4)]
+        tops = [first[0:4]] + [far(above, j) for j in range(4)] + [piece(12 + j)[4:8] for j in range(4)]
         for j in range(8):
             cols = slice(8 * j, 8 * j + 8)
             for rows, t in ((slice(4, 12), mids), (slice(12, 16), lows), (slice(0, 4), tops)):

time: 159 us -> 157 us (0.987)
  starting transfers between devices: 45.8 us -> 43.9 us
    ppermute x26, starting transfers between devices: 32 us -> 29.6 us  [exchange(): return lax.ppermute(v, AXES, pairs)]
  transfers between devices with their start and end apart: 34 -> 34, of which waited for: 21 -> 20; matrix products, arithmetic and copies ran while one was open for 1% -> 1% of each run, Pallas kernels for 3% -> 3%
where the time goes in v5:
time: 157 us
  waiting for transfers between devices  53.6 us (34%)
  Pallas kernels  52.6 us (34%)
  starting transfers between devices  43.9 us (28%)
  local copies, waits for them, and re-layouts  4.22 us (3%)
  other arithmetic  1.87 us (1%)
    pallas_call x1, Pallas kernels, attn_call(): pl.pallas_call(attn_body, grid_spec=pltpu.PrefetchScalarGridSpec(num_scal...  39.7 us
    ppermute x26, waiting for transfers between devices, exchange(): return lax.ppermute(v, AXES, pairs)  36.1 us
    ppermute x26, starting transfers between devices, exchange(): return lax.ppermute(v, AXES, pairs)  29.6 us
    ppermute x8, waiting for transfers between devices, shift(): return lax.ppermute(v, AXES, pairs)  17.4 us
    ppermute x8, starting transfers between devices, shift(): return lax.ppermute(v, AXES, pairs)  14.3 us
    pallas_call x1, Pallas kernels, widen_call(): pl.pallas_call(widen_body, grid_spec=pltpu.PrefetchScalarGridSpec(num_sca...  5.24 us
    unnamed x28, local copies, waits for them, and re-layouts  3.24 us
  transfers between devices with their start and end apart: 34, of which 20 were waited for; matrix products, arithmetic and copies ran while one was open for 1% of the time, Pallas kernels for 3%

profile of v5, /device:TPU:0, one launch (start us, length us, event | category | flops | bytes accessed | tf_op | source)
XLA Modules:
  0.0 157.2 jit_solution(12899387758752591568)
XLA Ops:
  2.2 2.5 %pack.1 = (bf16[4,32,1664]{2,1,0:T(8,128)(2,1)}, bf16[4,32,1664]{2,1,0:T(8,128)(2,1)}, bf16[6,8,1664]{2,1,0:T(8,128)(2,1)}, bf16[4,8,1664]{2,1,0:T(8,128)(2,1)}) custom-call(bf16[16,64,768]{2,1,0:T(8,128)(2,1)} %x_ref.3, bf16[16,64,768]{2,1,0:T(8,128)(2,1)} %x_ref.3, bf16[16,64,768]{2,1,0:T(8,128)(2,1)} %x_ref.3, bf16[16,64,768]{2,1,0:T(8,128)(2,1)} %g_ref.3, ...), custom_call_target="tpu_custom_call" | custom-call | bytes 4000000 | tf_op jit(solution)/shard_map/pack/pallas_call | solution.py:93
  4.7 4.2 %collective-permute-start.2 = (bf16[4,32,1664]{2,1,0:T(8,128)(2,1)}, bf16[4,32,1664]{2,1,0:T(8,128)(2,1)S(1)}, u32[]{:S(2)}, u32[]{:S(2)}) collective-permute-start(bf16[4,32,1664]{2,1,0:T(8,128)(2,1)} %get-tuple-element.39), channel_id=1, source_target_pairs={{0,7},{1,0},{2,1},{3,2},{4,3},{5,4},{6,5},{7,6},{8,15},{9,8},{10,9... | collective-permute-start | bytes 1277960 | tf_op jit(solution)/shard_map/ppermute | solution.py:492
  8.9 5.2 %collective-permute-start.1 = (bf16[6,8,1664]{2,1,0:T(8,128)(2,1)}, bf16[6,8,1664]{2,1,0:T(8,128)(2,1)S(1)}, u32[]{:S(2)}, u32[]{:S(2)}) collective-permute-start(bf16[6,8,1664]{2,1,0:T(8,128)(2,1)} %get-tuple-element.38), channel_id=1, source_target_pairs={{0,120},{1,121},{2,122},{3,123},{4,124},{5,125},{6,126},{7,127},{8... | collective-permute-start | bytes 479240 | tf_op jit(solution)/shard_map/ppermute | solution.py:492
  14.2 9.1 %collective-permute-done.corner = bf16[4,8,1664]{2,1,0:T(8,128)(2,1)S(1)} collective-permute-done((bf16[4,8,1664]{2,1,0:T(8,128)(2,1)}, bf16[4,8,1664]{2,1,0:T(8,128)(2,1)S(1)}, u32[]{:S(2)}, u32[]{:S(2)}) %collective-permute-start) | collective-permute-done | bytes 106528 | tf_op jit(solution)/shard_map/ppermute | solution.py:492
  24.5 39.7 %attention.1 = (bf16[1024,768]{1,0:T(8,128)(2,1)}, bf16[1024,768]{1,0:T(8,128)(2,1)}, bf16[4,32,1536]{2,1,0:T(8,128)(2,1)}, bf16[4,32,1536]{2,1,0:T(8,128)(2,1)}...) custom-call(s32[1]{0:T(128)} %bitcast.core_ref, ...), custom_call_target="tpu_custom_call" | custom-call | flops 16000000000 | bytes 25000000 | tf_op jit(solution)/shard_map/attention/pallas_call | solution.py:258
  64.2 2.3 %collective-permute-start.4 = (bf16[1536,768]{1,0:T(8,128)(2,1)}, bf16[1536,768]{1,0:T(8,128)(2,1)S(1)}, u32[]{:S(2)}, u32[]{:S(2)}) collective-permute-start(bf16[1536,768]{1,0:T(8,128)(2,1)} %get-tuple-element.44), channel_id=1, source_target_pairs={{0,8},{1,9},{2,10},{3,11},{4,12},{5,13},{6,14},{7,15},{8,0},{9,1},... | collective-permute-start | bytes 7077896 | tf_op jit(solution)/shard_map/ppermute | solution.py:444
  66.6 4.3 %collective-permute-done.4.recv = bf16[1536,768]{1,0:T(8,128)(2,1)S(1)} collective-permute-done((bf16[1536,768]{1,0:T(8,128)(2,1)}, bf16[1536,768]{1,0:T(8,128)(2,1)S(1)}, u32[]{:S(2)}, u32[]{:S(2)}) %collective-permute-start.4) | collective-permute-done | bytes 2359328 | tf_op jit(solution)/shard_map/ppermute | solution.py:444
  70.9 1.7 %copy-done.2 = bf16[1536,768]{1,0:T(8,128)(2,1)S(1)} copy-done((bf16[1536,768]{1,0:T(8,128)(2,1)S(1)}, bf16[1536,768]{1,0:T(8,128)(2,1)}, u32[]{:S(2)}) %copy-start.2) | copy-done | bytes 2359320
  72.5 2.0 %combine.1 = (bf16[256,768]{1,0:T(8,128)(2,1)S(1)}, bf16[256,768]{1,0:T(8,128)(2,1)S(1)}, bf16[256,768]{1,0:T(8,128)(2,1)S(1)}, bf16[256,768]{1,0:T(8,128)(2,1)}...) custom-call(s32[3]{0:T(128)S(1)} %pad_add_fusion.bits, bf16[1536,768]{1,0:T(8,128)(2,1)S(1)} %copy-done.2, ...), custom_call_target="tpu_custom_call" | custom-call | flops 1200000 | bytes 7000000 | tf_op jit(solution)/shard_map/combine/pallas_call | solution.py:335
  75.3 1.6 %collective-permute-start.13 = (bf16[256,768]{1,0:T(8,128)(2,1)}, bf16[256,768]{1,0:T(8,128)(2,1)S(1)}, u32[]{:S(2)}, u32[]{:S(2)}) collective-permute-start(bf16[256,768]{1,0:T(8,128)(2,1)} %get-tuple-element.48), channel_id=1, source_target_pairs={{0,16},{1,17},{2,18},{3,19},{4,20},{5,21},{6,22},{7,23},{8,56},{9,... | collective-permute-start | bytes 1179656 | tf_op jit(solution)/shard_map/ppermute | solution.py:444
  77.0 6.3 %collective-permute-done.5 = bf16[256,768]{1,0:T(8,128)(2,1)S(1)} collective-permute-done((bf16[256,768]{1,0:T(8,128)(2,1)}, bf16[256,768]{1,0:T(8,128)(2,1)S(1)}, u32[]{:S(2)}, u32[]{:S(2)}) %collective-permute-start.5) | collective-permute-done | bytes 393248 | tf_op jit(solution)/shard_map/ppermute | solution.py:444
  83.4 1.7 %collective-permute-start.6 = (bf16[128,768]{1,0:T(8,128)(2,1)S(1)}, bf16[128,768]{1,0:T(8,128)(2,1)S(1)}, u32[]{:S(2)}, u32[]{:S(2)}) collective-permute-start(bf16[128,768]{1,0:T(8,128)(2,1)S(1)} %constant_dynamic-slice_fusion.2), channel_id=1, source_target_pairs={{0,16},{1,17},{2,18},{3,19},{4,20},{5,21},{6,22},{7,23},{8,56},{9,... | collective-permute-start | bytes 589832 | tf_op jit(solution)/shard_map/ppermute | solution.py:444
  85.6 1.6 %collective-permute-start.22 = (bf16[128,768]{1,0:T(8,128)(2,1)S(1)}, bf16[128,768]{1,0:T(8,128)(2,1)S(1)}, u32[]{:S(2)}, u32[]{:S(2)}) collective-permute-start(bf16[128,768]{1,0:T(8,128)(2,1)S(1)} %constant_dynamic-slice_fusion), channel_id=1, source_target_pairs={{0,1},{1,0},{2,3},{3,2},{4,5},{5,4},{6,7},{7,6},{8,11},{9,10},{10,... | collective-permute-start | bytes 589832 | tf_op jit(solution)/shard_map/ppermute | solution.py:444
  87.1 2.1 %collective-permute-done.6 = bf16[128,768]{1,0:T(8,128)(2,1)S(1)} collective-permute-done((bf16[128,768]{1,0:T(8,128)(2,1)S(1)}, bf16[128,768]{1,0:T(8,128)(2,1)S(1)}, u32[]{:S(2)}, u32[]{:S(2)}) %collective-permute-start.6) | collective-permute-done | bytes 196640 | tf_op jit(solution)/shard_map/ppermute | solution.py:444
  91.4 1.7 %collective-permute-start.23 = (bf16[128,768]{1,0:T(8,128)(2,1)S(1)}, bf16[128,768]{1,0:T(8,128)(2,1)S(1)}, u32[]{:S(2)}, u32[]{:S(2)}) collective-permute-start(bf16[128,768]{1,0:T(8,128)(2,1)S(1)} %add_convert_fusion.7), channel_id=1, source_target_pairs={{0,16},{1,17},{2,18},{3,19},{4,20},{5,21},{6,22},{7,23},{8,56},{9,... | collective-permute-start | bytes 589832 | tf_op jit(solution)/shard_map/ppermute | solution.py:444
  93.1 2.1 %collective-permute-done.7 = bf16[128,768]{1,0:T(8,128)(2,1)S(1)} collective-permute-done((bf16[128,768]{1,0:T(8,128)(2,1)S(1)}, bf16[128,768]{1,0:T(8,128)(2,1)S(1)}, u32[]{:S(2)}, u32[]{:S(2)}) %collective-permute-start.7) | collective-permute-done | bytes 196640 | tf_op jit(solution)/shard_map/ppermute | solution.py:444
  96.8 3.6 %collective-permute-start.16 = (bf16[128,768]{1,0:T(8,128)(2,1)S(1)}, bf16[128,768]{1,0:T(8,128)(2,1)S(1)}, u32[]{:S(2)}, u32[]{:S(2)}) collective-permute-start(bf16[128,768]{1,0:T(8,128)(2,1)S(1)} %add_convert_fusion.11), channel_id=1, source_target_pairs={{0,48},{1,49},{2,50},{3,51},{4,52},{5,53},{6,54},{7,55},{8,24},{9,... | collective-permute-start | bytes 589832 | tf_op jit(solution)/shard_map/ppermute | solution.py:444
  100.5 2.6 %collective-permute-start.24 = (bf16[128,768]{1,0:T(8,128)(2,1)S(1)}, bf16[128,768]{1,0:T(8,128)(2,1)S(1)}, u32[]{:S(2)}, u32[]{:S(2)}) collective-permute-start(bf16[128,768]{1,0:T(8,128)(2,1)S(1)} %add_convert_fusion.6), channel_id=1, source_target_pairs={{0,68},{1,69},{2,70},{3,71},{4,64},{5,65},{6,66},{7,67},{8,12},{9,... | collective-permute-start | bytes 589832 | tf_op jit(solution)/shard_map/ppermute | solution.py:444
  103.2 2.9 %collective-permute-start.9 = (bf16[128,768]{1,0:T(8,128)(2,1)S(1)}, bf16[128,768]{1,0:T(8,128)(2,1)S(1)}, u32[]{:S(2)}, u32[]{:S(2)}) collective-permute-start(bf16[128,768]{1,0:T(8,128)(2,1)S(1)} %add_convert_fusion.15), channel_id=1, source_target_pairs={{0,48},{1,49},{2,50},{3,51},{4,52},{5,53},{6,54},{7,55},{8,24},{9,... | collective-permute-start | bytes 589832 | tf_op jit(solution)/shard_map/ppermute | solution.py:444
  106.2 1.9 %collective-permute-start.17 = (bf16[128,768]{1,0:T(8,128)(2,1)S(1)}, bf16[128,768]{1,0:T(8,128)(2,1)S(1)}, u32[]{:S(2)}, u32[]{:S(2)}) collective-permute-start(bf16[128,768]{1,0:T(8,128)(2,1)S(1)} %add_convert_fusion.10), channel_id=1, source_target_pairs={{0,68},{1,69},{2,70},{3,71},{4,64},{5,65},{6,66},{7,67},{8,12},{9,... | collective-permute-start | bytes 589832 | tf_op jit(solution)/shard_map/ppermute | solution.py:444
  108.2 1.5 collective-permute-start.25
  110.2 1.7 %collective-permute-start.10 = (bf16[128,768]{1,0:T(8,128)(2,1)S(1)}, bf16[128,768]{1,0:T(8,128)(2,1)S(1)}, u32[]{:S(2)}, u32[]{:S(2)}) collective-permute-start(bf16[128,768]{1,0:T(8,128)(2,1)S(1)} %add_convert_fusion.14), channel_id=1, source_target_pairs={{0,68},{1,69},{2,70},{3,71},{4,64},{5,65},{6,66},{7,67},{8,12},{9,... | collective-permute-start | bytes 589832 | tf_op jit(solution)/shard_map/ppermute | solution.py:444
  113.7 1.5 collective-permute-done.25
  115.2 2.0 %collective-permute-start.26 = (bf16[128,768]{1,0:T(8,128)(2,1)S(1)}, bf16[128,768]{1,0:T(8,128)(2,1)S(1)}, u32[]{:S(2)}, u32[]{:S(2)}) collective-permute-start(bf16[128,768]{1,0:T(8,128)(2,1)S(1)} %add_convert_fusion.4), channel_id=1, source_target_pairs={{0,48},{1,49},{2,50},{3,51},{4,52},{5,53},{6,54},{7,55},{8,24},{9,... | collective-permute-start | bytes 589832 | tf_op jit(solution)/shard_map/ppermute | solution.py:444
  117.7 3.2 %collective-permute-done.18 = bf16[128,768]{1,0:T(8,128)(2,1)S(1)} collective-permute-done((bf16[128,768]{1,0:T(8,128)(2,1)S(1)}, bf16[128,768]{1,0:T(8,128)(2,1)S(1)}, u32[]{:S(2)}, u32[]{:S(2)}) %collective-permute-start.18) | collective-permute-done | bytes 196640 | tf_op jit(solution)/shard_map/ppermute | solution.py:444
  124.4 2.2 %collective-permute-done.19.refs_1_ = bf16[128,768]{1,0:T(8,128)(2,1)S(1)} collective-permute-done((bf16[128,768]{1,0:T(8,128)(2,1)S(1)}, bf16[128,768]{1,0:T(8,128)(2,1)S(1)}, u32[]{:S(2)}, u32[]{:S(2)}) %collective-permute-start.19) | collective-permute-done | bytes 196640 | tf_op jit(solution)/shard_map/ppermute | solution.py:444
  129.0 3.2 %collective-permute-done.12.refs_1_ = bf16[256,768]{1,0:T(8,128)(2,1)S(1)} collective-permute-done((bf16[256,768]{1,0:T(8,128)(2,1)S(1)}, bf16[256,768]{1,0:T(8,128)(2,1)S(1)}, u32[]{:S(2)}, u32[]{:S(2)}) %collective-permute-start.12) | collective-permute-done | bytes 393248 | tf_op jit(solution)/shard_map/ppermute | solution.py:444
  132.2 2.4 %collective-permute-done.20.refs_3_ = bf16[256,768]{1,0:T(8,128)(2,1)S(1)} collective-permute-done((bf16[256,768]{1,0:T(8,128)(2,1)S(1)}, bf16[256,768]{1,0:T(8,128)(2,1)S(1)}, u32[]{:S(2)}, u32[]{:S(2)}) %collective-permute-start.20) | collective-permute-done | bytes 393248 | tf_op jit(solution)/shard_map/ppermute | solution.py:444
  138.8 2.7 %collective-permute-start.29 = (bf16[4,8,1536]{2,1,0:T(8,128)(2,1)S(1)}, bf16[4,8,1536]{2,1,0:T(8,128)(2,1)S(1)}, u32[]{:S(2)}, u32[]{:S(2)}) collective-permute-start(bf16[4,8,1536]{2,1,0:T(8,128)(2,1)S(1)} %copy-done.13), channel_id=1, source_target_pairs={{0,15},{1,8},{2,9},{3,10},{4,11},{5,12},{6,13},{7,14},{8,23},{9,16... | collective-permute-start | bytes 294920 | tf_op jit(solution)/shard_map/ppermute | solution.py:492
  141.6 5.2 %widen.1 = (f32[768,2304]{1,0:T(8,128)}, f32[768,768]{1,0:T(8,128)}) custom-call(s32[1]{0:T(128)} %bitcast.core_ref, bf16[1536,768]{1,0:T(8,128)(2,1)S(1)} %join.7.own, bf16[1536,768]{1,0:T(8,128)(2,1)S(1)} %collective-permute-done.33.other), custom_call_target="tpu_custom_call" | custom-call | bytes 14000000 | tf_op jit(solution)/shard_map/widen/pallas_call | solution.py:398
  146.8 8.0 %collective-permute-done.29.corner = bf16[4,8,1536]{2,1,0:T(8,128)(2,1)S(1)} collective-permute-done((bf16[4,8,1536]{2,1,0:T(8,128)(2,1)S(1)}, bf16[4,8,1536]{2,1,0:T(8,128)(2,1)S(1)}, u32[]{:S(2)}, u32[]{:S(2)}) %collective-permute-start.29) | collective-permute-done | bytes 98336 | tf_op jit(solution)/shard_map/ppermute | solution.py:492
  154.9 2.3 %merge.1 = (bf16[16,64,768]{2,1,0:T(8,128)(2,1)}, bf16[16,64,768]{2,1,0:T(8,128)(2,1)}) custom-call(bf16[16,64,768]{2,1,0:T(8,128)(2,1)S(1)} %copy-done, bf16[16,64,768]{2,1,0:T(8,128)(2,1)S(1)} %copy-done.1, bf16[1024,768]{1,0:T(8,128)(2,1)S(1)} %copy-done.3, bf16[1024,768]{1,0:T(8,128)(2,1)S(1)} %copy-done.4, ...), custom_call_target="tpu_custom_call" | custom-call | flops 3000000 | bytes 11000000 | tf_op jit(solution)/shard_map/merge/pallas_call | solution.py:313
  (97 shorter events, 21.3 us)
Async XLA Ops:
  4.7 18.6 %collective-permute-start.2 = (bf16[4,32,1664]{2,1,0:T(8,128)(2,1)}, bf16[4,32,1664]{2,1,0:T(8,128)(2,1)S(1)}, u32[]{:S(2)}, u32[]{:S(2)}) collective-permute-start(bf16[4,32,1664]{2,1,0:T(8,128)(2,1)} %get-tuple-element.39), channel_id=1, source_target_pairs={{0,7},{1,0},{2,1},{3,2},{4,3},{5,4},{6,5},{7,6},{8,15},{9,8},{10,9... | collective-permute-start | bytes 1277960 | tf_op jit(solution)/shard_map/ppermute | solution.py:492
  8.9 14.7 %collective-permute-start.3 = (bf16[4,32,1664]{2,1,0:T(8,128)(2,1)}, bf16[4,32,1664]{2,1,0:T(8,128)(2,1)S(1)}, u32[]{:S(2)}, u32[]{:S(2)}) collective-permute-start(bf16[4,32,1664]{2,1,0:T(8,128)(2,1)} %get-tuple-element.40), channel_id=1, source_target_pairs={{0,1},{1,2},{2,3},{3,4},{4,5},{5,6},{6,7},{7,0},{8,9},{9,10},{10,1... | collective-permute-start | bytes 1277960 | tf_op jit(solution)/shard_map/ppermute | solution.py:492
  8.9 14.4 %collective-permute-start.1 = (bf16[6,8,1664]{2,1,0:T(8,128)(2,1)}, bf16[6,8,1664]{2,1,0:T(8,128)(2,1)S(1)}, u32[]{:S(2)}, u32[]{:S(2)}) collective-permute-start(bf16[6,8,1664]{2,1,0:T(8,128)(2,1)} %get-tuple-element.38), channel_id=1, source_target_pairs={{0,120},{1,121},{2,122},{3,123},{4,124},{5,125},{6,126},{7,127},{8... | collective-permute-start | bytes 479240 | tf_op jit(solution)/shard_map/ppermute | solution.py:492
  14.1 9.2 %collective-permute-start = (bf16[4,8,1664]{2,1,0:T(8,128)(2,1)}, bf16[4,8,1664]{2,1,0:T(8,128)(2,1)S(1)}, u32[]{:S(2)}, u32[]{:S(2)}) collective-permute-start(bf16[4,8,1664]{2,1,0:T(8,128)(2,1)} %get-tuple-element.37), channel_id=1, source_target_pairs={{0,121},{1,122},{2,123},{3,124},{4,125},{5,126},{6,127},{7,120},{8... | collective-permute-start | bytes 319496 | tf_op jit(solution)/shard_map/ppermute | solution.py:492
  64.2 6.6 %collective-permute-start.4 = (bf16[1536,768]{1,0:T(8,128)(2,1)}, bf16[1536,768]{1,0:T(8,128)(2,1)S(1)}, u32[]{:S(2)}, u32[]{:S(2)}) collective-permute-start(bf16[1536,768]{1,0:T(8,128)(2,1)} %get-tuple-element.44), channel_id=1, source_target_pairs={{0,8},{1,9},{2,10},{3,11},{4,12},{5,13},{6,14},{7,15},{8,0},{9,1},... | collective-permute-start | bytes 7077896 | tf_op jit(solution)/shard_map/ppermute | solution.py:444
  75.3 8.0 %collective-permute-start.5 = (bf16[256,768]{1,0:T(8,128)(2,1)}, bf16[256,768]{1,0:T(8,128)(2,1)S(1)}, u32[]{:S(2)}, u32[]{:S(2)}) collective-permute-start(bf16[256,768]{1,0:T(8,128)(2,1)} %get-tuple-element.46), channel_id=1, source_target_pairs={{0,1},{1,0},{2,3},{3,2},{4,5},{5,4},{6,7},{7,6},{8,11},{9,10},{10,... | collective-permute-start | bytes 1179656 | tf_op jit(solution)/shard_map/ppermute | solution.py:444
  75.3 9.8 %collective-permute-start.13 = (bf16[256,768]{1,0:T(8,128)(2,1)}, bf16[256,768]{1,0:T(8,128)(2,1)S(1)}, u32[]{:S(2)}, u32[]{:S(2)}) collective-permute-start(bf16[256,768]{1,0:T(8,128)(2,1)} %get-tuple-element.48), channel_id=1, source_target_pairs={{0,16},{1,17},{2,18},{3,19},{4,20},{5,21},{6,22},{7,23},{8,56},{9,... | collective-permute-start | bytes 1179656 | tf_op jit(solution)/shard_map/ppermute | solution.py:444
  76.9 8.5 %collective-permute-start.21 = (bf16[256,768]{1,0:T(8,128)(2,1)}, bf16[256,768]{1,0:T(8,128)(2,1)S(1)}, u32[]{:S(2)}, u32[]{:S(2)}) collective-permute-start(bf16[256,768]{1,0:T(8,128)(2,1)} %copy-done.5), channel_id=1, source_target_pairs={{0,4},{1,5},{2,6},{3,7},{4,0},{5,1},{6,2},{7,3},{8,76},{9,77},{10,... | collective-permute-start | bytes 1179656 | tf_op jit(solution)/shard_map/ppermute | solution.py:444
  85.2 5.8 %collective-permute-start.14 = (bf16[128,768]{1,0:T(8,128)(2,1)S(1)}, bf16[128,768]{1,0:T(8,128)(2,1)S(1)}, u32[]{:S(2)}, u32[]{:S(2)}) collective-permute-start(bf16[128,768]{1,0:T(8,128)(2,1)S(1)} %constant_dynamic-slice_fusion.1), channel_id=1, source_target_pairs={{0,4},{1,5},{2,6},{3,7},{4,0},{5,1},{6,2},{7,3},{8,76},{9,77},{10,... | collective-permute-start | bytes 589832 | tf_op jit(solution)/shard_map/ppermute | solution.py:444
  85.6 5.8 %collective-permute-start.22 = (bf16[128,768]{1,0:T(8,128)(2,1)S(1)}, bf16[128,768]{1,0:T(8,128)(2,1)S(1)}, u32[]{:S(2)}, u32[]{:S(2)}) collective-permute-start(bf16[128,768]{1,0:T(8,128)(2,1)S(1)} %constant_dynamic-slice_fusion), channel_id=1, source_target_pairs={{0,1},{1,0},{2,3},{3,2},{4,5},{5,4},{6,7},{7,6},{8,11},{9,10},{10,... | collective-permute-start | bytes 589832 | tf_op jit(solution)/shard_map/ppermute | solution.py:444
  89.3 5.9 %collective-permute-start.7 = (bf16[128,768]{1,0:T(8,128)(2,1)S(1)}, bf16[128,768]{1,0:T(8,128)(2,1)S(1)}, u32[]{:S(2)}, u32[]{:S(2)}) collective-permute-start(bf16[128,768]{1,0:T(8,128)(2,1)S(1)} %add_convert_fusion.17), channel_id=1, source_target_pairs={{0,4},{1,5},{2,6},{3,7},{4,0},{5,1},{6,2},{7,3},{8,76},{9,77},{10,... | collective-permute-start | bytes 589832 | tf_op jit(solution)/shard_map/ppermute | solution.py:444
  91.0 5.7 %collective-permute-start.15 = (bf16[128,768]{1,0:T(8,128)(2,1)S(1)}, bf16[128,768]{1,0:T(8,128)(2,1)S(1)}, u32[]{:S(2)}, u32[]{:S(2)}) collective-permute-start(bf16[128,768]{1,0:T(8,128)(2,1)S(1)} %add_convert_fusion.12), channel_id=1, source_target_pairs={{0,1},{1,0},{2,3},{3,2},{4,5},{5,4},{6,7},{7,6},{8,11},{9,10},{10,... | collective-permute-start | bytes 589832 | tf_op jit(solution)/shard_map/ppermute | solution.py:444
  91.4 9.1 %collective-permute-start.23 = (bf16[128,768]{1,0:T(8,128)(2,1)S(1)}, bf16[128,768]{1,0:T(8,128)(2,1)S(1)}, u32[]{:S(2)}, u32[]{:S(2)}) collective-permute-start(bf16[128,768]{1,0:T(8,128)(2,1)S(1)} %add_convert_fusion.7), channel_id=1, source_target_pairs={{0,16},{1,17},{2,18},{3,19},{4,20},{5,21},{6,22},{7,23},{8,56},{9,... | collective-permute-start | bytes 589832 | tf_op jit(solution)/shard_map/ppermute | solution.py:444
  95.2 7.9 %collective-permute-start.8 = (bf16[128,768]{1,0:T(8,128)(2,1)S(1)}, bf16[128,768]{1,0:T(8,128)(2,1)S(1)}, u32[]{:S(2)}, u32[]{:S(2)}) collective-permute-start(bf16[128,768]{1,0:T(8,128)(2,1)S(1)} %add_convert_fusion.16), channel_id=1, source_target_pairs={{0,3},{1,2},{2,1},{3,0},{4,7},{5,6},{6,5},{7,4},{8,9},{9,8},{10,11... | collective-permute-start | bytes 589832 | tf_op jit(solution)/shard_map/ppermute | solution.py:444
  96.8 9.3 %collective-permute-start.16 = (bf16[128,768]{1,0:T(8,128)(2,1)S(1)}, bf16[128,768]{1,0:T(8,128)(2,1)S(1)}, u32[]{:S(2)}, u32[]{:S(2)}) collective-permute-start(bf16[128,768]{1,0:T(8,128)(2,1)S(1)} %add_convert_fusion.11), channel_id=1, source_target_pairs={{0,48},{1,49},{2,50},{3,51},{4,52},{5,53},{6,54},{7,55},{8,24},{9,... | collective-permute-start | bytes 589832 | tf_op jit(solution)/shard_map/ppermute | solution.py:444
  100.5 7.6 %collective-permute-start.24 = (bf16[128,768]{1,0:T(8,128)(2,1)S(1)}, bf16[128,768]{1,0:T(8,128)(2,1)S(1)}, u32[]{:S(2)}, u32[]{:S(2)}) collective-permute-start(bf16[128,768]{1,0:T(8,128)(2,1)S(1)} %add_convert_fusion.6), channel_id=1, source_target_pairs={{0,68},{1,69},{2,70},{3,71},{4,64},{5,65},{6,66},{7,67},{8,12},{9,... | collective-permute-start | bytes 589832 | tf_op jit(solution)/shard_map/ppermute | solution.py:444
  103.2 7.0 %collective-permute-start.9 = (bf16[128,768]{1,0:T(8,128)(2,1)S(1)}, bf16[128,768]{1,0:T(8,128)(2,1)S(1)}, u32[]{:S(2)}, u32[]{:S(2)}) collective-permute-start(bf16[128,768]{1,0:T(8,128)(2,1)S(1)} %add_convert_fusion.15), channel_id=1, source_target_pairs={{0,48},{1,49},{2,50},{3,51},{4,52},{5,53},{6,54},{7,55},{8,24},{9,... | collective-permute-start | bytes 589832 | tf_op jit(solution)/shard_map/ppermute | solution.py:444
  106.2 7.0 %collective-permute-start.17 = (bf16[128,768]{1,0:T(8,128)(2,1)S(1)}, bf16[128,768]{1,0:T(8,128)(2,1)S(1)}, u32[]{:S(2)}, u32[]{:S(2)}) collective-permute-start(bf16[128,768]{1,0:T(8,128)(2,1)S(1)} %add_convert_fusion.10), channel_id=1, source_target_pairs={{0,68},{1,69},{2,70},{3,71},{4,64},{5,65},{6,66},{7,67},{8,12},{9,... | collective-permute-start | bytes 589832 | tf_op jit(solution)/shard_map/ppermute | solution.py:444
  108.2 7.0 %collective-permute-start.25 = (bf16[128,768]{1,0:T(8,128)(2,1)S(1)}, bf16[128,768]{1,0:T(8,128)(2,1)S(1)}, u32[]{:S(2)}, u32[]{:S(2)}) collective-permute-start(bf16[128,768]{1,0:T(8,128)(2,1)S(1)} %add_convert_fusion.5), channel_id=1, source_target_pairs={{0,3},{1,2},{2,1},{3,0},{4,7},{5,6},{6,5},{7,4},{8,9},{9,8},{10,11... | collective-permute-start | bytes 589832 | tf_op jit(solution)/shard_map/ppermute | solution.py:444
  110.2 7.0 %collective-permute-start.10 = (bf16[128,768]{1,0:T(8,128)(2,1)S(1)}, bf16[128,768]{1,0:T(8,128)(2,1)S(1)}, u32[]{:S(2)}, u32[]{:S(2)}) collective-permute-start(bf16[128,768]{1,0:T(8,128)(2,1)S(1)} %add_convert_fusion.14), channel_id=1, source_target_pairs={{0,68},{1,69},{2,70},{3,71},{4,64},{5,65},{6,66},{7,67},{8,12},{9,... | collective-permute-start | bytes 589832 | tf_op jit(solution)/shard_map/ppermute | solution.py:444
  113.2 7.6 %collective-permute-start.18 = (bf16[128,768]{1,0:T(8,128)(2,1)S(1)}, bf16[128,768]{1,0:T(8,128)(2,1)S(1)}, u32[]{:S(2)}, u32[]{:S(2)}) collective-permute-start(bf16[128,768]{1,0:T(8,128)(2,1)S(1)} %add_convert_fusion.9), channel_id=1, source_target_pairs={{0,3},{1,2},{2,1},{3,0},{4,7},{5,6},{6,5},{7,4},{8,9},{9,8},{10,11... | collective-permute-start | bytes 589832 | tf_op jit(solution)/shard_map/ppermute | solution.py:444
  115.2 7.0 %collective-permute-start.26 = (bf16[128,768]{1,0:T(8,128)(2,1)S(1)}, bf16[128,768]{1,0:T(8,128)(2,1)S(1)}, u32[]{:S(2)}, u32[]{:S(2)}) collective-permute-start(bf16[128,768]{1,0:T(8,128)(2,1)S(1)} %add_convert_fusion.4), channel_id=1, source_target_pairs={{0,48},{1,49},{2,50},{3,51},{4,52},{5,53},{6,54},{7,55},{8,24},{9,... | collective-permute-start | bytes 589832 | tf_op jit(solution)/shard_map/ppermute | solution.py:444
  117.3 5.7 %collective-permute-start.11 = (bf16[128,768]{1,0:T(8,128)(2,1)S(1)}, bf16[128,768]{1,0:T(8,128)(2,1)S(1)}, u32[]{:S(2)}, u32[]{:S(2)}) collective-permute-start(bf16[128,768]{1,0:T(8,128)(2,1)S(1)} %add_convert_fusion.13.refs_0_), channel_id=1, source_target_pairs={{0,16},{1,17},{2,18},{3,19},{4,20},{5,21},{6,22},{7,23},{8,56},{9,... | collective-permute-start | bytes 589832 | tf_op jit(solution)/shard_map/ppermute | solution.py:444
  120.9 5.8 %collective-permute-start.19 = (bf16[128,768]{1,0:T(8,128)(2,1)S(1)}, bf16[128,768]{1,0:T(8,128)(2,1)S(1)}, u32[]{:S(2)}, u32[]{:S(2)}) collective-permute-start(bf16[128,768]{1,0:T(8,128)(2,1)S(1)} %add_convert_fusion.8.refs_0_), channel_id=1, source_target_pairs={{0,4},{1,5},{2,6},{3,7},{4,0},{5,1},{6,2},{7,3},{8,76},{9,77},{10,... | collective-permute-start | bytes 589832 | tf_op jit(solution)/shard_map/ppermute | solution.py:444
  122.2 5.7 %collective-permute-start.27 = (bf16[128,768]{1,0:T(8,128)(2,1)S(1)}, bf16[128,768]{1,0:T(8,128)(2,1)S(1)}, u32[]{:S(2)}, u32[]{:S(2)}) collective-permute-start(bf16[128,768]{1,0:T(8,128)(2,1)S(1)} %add_convert_fusion.3.refs_0_), channel_id=1, source_target_pairs={{0,1},{1,0},{2,3},{3,2},{4,5},{5,4},{6,7},{7,6},{8,11},{9,10},{10,... | collective-permute-start | bytes 589832 | tf_op jit(solution)/shard_map/ppermute | solution.py:444
  123.0 9.1 %collective-permute-start.12 = (bf16[256,768]{1,0:T(8,128)(2,1)S(1)}, bf16[256,768]{1,0:T(8,128)(2,1)S(1)}, u32[]{:S(2)}, u32[]{:S(2)}) collective-permute-start(bf16[256,768]{1,0:T(8,128)(2,1)S(1)} %join.4.refs_0_), channel_id=1, source_target_pairs={{0,1},{1,0},{2,3},{3,2},{4,5},{5,4},{6,7},{7,6},{8,11},{9,10},{10,... | collective-permute-start | bytes 1179656 | tf_op jit(solution)/shard_map/ppermute | solution.py:444
  126.7 7.9 %collective-permute-start.20 = (bf16[256,768]{1,0:T(8,128)(2,1)S(1)}, bf16[256,768]{1,0:T(8,128)(2,1)S(1)}, u32[]{:S(2)}, u32[]{:S(2)}) collective-permute-start(bf16[256,768]{1,0:T(8,128)(2,1)S(1)} %join.5.refs_2_), channel_id=1, source_target_pairs={{0,16},{1,17},{2,18},{3,19},{4,20},{5,21},{6,22},{7,23},{8,56},{9,... | collective-permute-start | bytes 1179656 | tf_op jit(solution)/shard_map/ppermute | solution.py:444
  128.0 7.9 %collective-permute-start.28 = (bf16[256,768]{1,0:T(8,128)(2,1)S(1)}, bf16[256,768]{1,0:T(8,128)(2,1)S(1)}, u32[]{:S(2)}, u32[]{:S(2)}) collective-permute-start(bf16[256,768]{1,0:T(8,128)(2,1)S(1)} %join.6.refs_4_), channel_id=1, source_target_pairs={{0,4},{1,5},{2,6},{3,7},{4,0},{5,1},{6,2},{7,3},{8,76},{9,77},{10,... | collective-permute-start | bytes 1179656 | tf_op jit(solution)/shard_map/ppermute | solution.py:444
  136.7 18.1 %collective-permute-start.31 = (bf16[4,32,1536]{2,1,0:T(8,128)(2,1)S(1)}, bf16[4,32,1536]{2,1,0:T(8,128)(2,1)S(1)}, u32[]{:S(2)}, u32[]{:S(2)}) collective-permute-start(bf16[4,32,1536]{2,1,0:T(8,128)(2,1)S(1)} %copy-done.9), channel_id=1, source_target_pairs={{0,7},{1,0},{2,1},{3,2},{4,3},{5,4},{6,5},{7,6},{8,15},{9,8},{10,9... | collective-permute-start | bytes 1179656 | tf_op jit(solution)/shard_map/ppermute | solution.py:492
  137.6 17.2 %collective-permute-start.32 = (bf16[4,32,1536]{2,1,0:T(8,128)(2,1)S(1)}, bf16[4,32,1536]{2,1,0:T(8,128)(2,1)S(1)}, u32[]{:S(2)}, u32[]{:S(2)}) collective-permute-start(bf16[4,32,1536]{2,1,0:T(8,128)(2,1)S(1)} %copy-done.8), channel_id=1, source_target_pairs={{0,1},{1,2},{2,3},{3,4},{4,5},{5,6},{6,7},{7,0},{8,9},{9,10},{10,1... | collective-permute-start | bytes 1179656 | tf_op jit(solution)/shard_map/ppermute | solution.py:492
  138.8 16.0 %collective-permute-start.30 = (bf16[6,8,1536]{2,1,0:T(8,128)(2,1)S(1)}, bf16[6,8,1536]{2,1,0:T(8,128)(2,1)S(1)}, u32[]{:S(2)}, u32[]{:S(2)}) collective-permute-start(bf16[6,8,1536]{2,1,0:T(8,128)(2,1)S(1)} %copy-done.11), channel_id=1, source_target_pairs={{0,8},{1,9},{2,10},{3,11},{4,12},{5,13},{6,14},{7,15},{8,16},{9,17... | collective-permute-start | bytes 442376 | tf_op jit(solution)/shard_map/ppermute | solution.py:492
  138.8 16.0 %collective-permute-start.29 = (bf16[4,8,1536]{2,1,0:T(8,128)(2,1)S(1)}, bf16[4,8,1536]{2,1,0:T(8,128)(2,1)S(1)}, u32[]{:S(2)}, u32[]{:S(2)}) collective-permute-start(bf16[4,8,1536]{2,1,0:T(8,128)(2,1)S(1)} %copy-done.13), channel_id=1, source_target_pairs={{0,15},{1,8},{2,9},{3,10},{4,11},{5,12},{6,13},{7,14},{8,23},{9,16... | collective-permute-start | bytes 294920 | tf_op jit(solution)/shard_map/ppermute | solution.py:492
  (16 other events, 129.8 us)

commit v6 on v5

--- a/solution.py
+++ b/solution.py
@@ -223,9 +223,8 @@
         for load in loads:
             load.wait()
 
-        @pl.loop(0, 2)
-        def _(i):
-            rows = pl.ds(pl.multiple_of(i * 512, 512), 512)
+        for i in range(2):
+            rows = slice(512 * i, 512 * i + 512)
             attn_ref[rows, :] = mm(mixed_ref[rows, :], wo[...]).astype(BF16)
             dh = mm(dq_ref[rows, :], wqkv[:, 0:768], NT)
             dh += mm(dk_ref[rows, :], wqkv[:, 768:1536], NT)
@@ -493,7 +492,7 @@
 
 
 def local(slide_tokens, tissue, grad_tokens, w_qkv, w_out):
-    kb = jnp.broadcast_to(tissue.astype(BF16)[..., None], tissue.shape + (128,))
+    kb = jnp.broadcast_to(tissue[..., None], tissue.shape + (128,)).astype(BF16)
     core = (lax.axis_index("gx") % 2).astype(jnp.int32).reshape(1)
     up, down, left, corner = pack_call(slide_tokens, grad_tokens, kb)
     halo = (shift(corner, 1, -1), shift(left, 0, -1), shift(up, -1, 0), shift(down, 1, 0))

time: 157 us -> 157 us (level)
  no operation moved by 1% of the time
where the time goes in v6:
time: 157 us
  waiting for transfers between devices  54.5 us (35%)
  Pallas kernels  52.4 us (33%)
  starting transfers between devices  43.2 us (28%)
  local copies, waits for them, and re-layouts  4.22 us (3%)
  other arithmetic  1.87 us (1%)
    pallas_call x1, Pallas kernels, attn_call(): pl.pallas_call(attn_body, grid_spec=pltpu.PrefetchScalarGridSpec(num_scal...  39.5 us
    ppermute x26, waiting for transfers between devices, exchange(): return lax.ppermute(v, AXES, pairs)  36.5 us
    ppermute x26, starting transfers between devices, exchange(): return lax.ppermute(v, AXES, pairs)  29.1 us
    ppermute x8, waiting for transfers between devices, shift(): return lax.ppermute(v, AXES, pairs)  18 us
    ppermute x8, starting transfers between devices, shift(): return lax.ppermute(v, AXES, pairs)  14.1 us
    pallas_call x1, Pallas kernels, widen_call(): pl.pallas_call(widen_body, grid_spec=pltpu.PrefetchScalarGridSpec(num_sca...  5.24 us
    unnamed x28, local copies, waits for them, and re-layouts  3.24 us
  transfers between devices with their start and end apart: 34, of which 20 were waited for; matrix products, arithmetic and copies ran while one was open for 1% of the time, Pallas kernels for 3%

profile of v6, /device:TPU:0, one launch (start us, length us, event | category | flops | bytes accessed | tf_op | source)
XLA Modules:
  0.0 157.2 jit_solution(10788052350005831434)
XLA Ops:
  2.2 2.5 %pack.1 = (bf16[4,32,1664]{2,1,0:T(8,128)(2,1)}, bf16[4,32,1664]{2,1,0:T(8,128)(2,1)}, bf16[6,8,1664]{2,1,0:T(8,128)(2,1)}, bf16[4,8,1664]{2,1,0:T(8,128)(2,1)}) custom-call(bf16[16,64,768]{2,1,0:T(8,128)(2,1)} %x_ref.3, bf16[16,64,768]{2,1,0:T(8,128)(2,1)} %x_ref.3, bf16[16,64,768]{2,1,0:T(8,128)(2,1)} %x_ref.3, bf16[16,64,768]{2,1,0:T(8,128)(2,1)} %g_ref.3, ...), custom_call_target="tpu_custom_call" | custom-call | bytes 4000000 | tf_op jit(solution)/shard_map/pack/pallas_call | solution.py:93
  4.7 4.2 %collective-permute-start.2 = (bf16[4,32,1664]{2,1,0:T(8,128)(2,1)}, bf16[4,32,1664]{2,1,0:T(8,128)(2,1)S(1)}, u32[]{:S(2)}, u32[]{:S(2)}) collective-permute-start(bf16[4,32,1664]{2,1,0:T(8,128)(2,1)} %get-tuple-element.39), channel_id=1, source_target_pairs={{0,7},{1,0},{2,1},{3,2},{4,3},{5,4},{6,5},{7,6},{8,15},{9,8},{10,9... | collective-permute-start | bytes 1277960 | tf_op jit(solution)/shard_map/ppermute | solution.py:491
  8.9 5.2 %collective-permute-start.1 = (bf16[6,8,1664]{2,1,0:T(8,128)(2,1)}, bf16[6,8,1664]{2,1,0:T(8,128)(2,1)S(1)}, u32[]{:S(2)}, u32[]{:S(2)}) collective-permute-start(bf16[6,8,1664]{2,1,0:T(8,128)(2,1)} %get-tuple-element.38), channel_id=1, source_target_pairs={{0,120},{1,121},{2,122},{3,123},{4,124},{5,125},{6,126},{7,127},{8... | collective-permute-start | bytes 479240 | tf_op jit(solution)/shard_map/ppermute | solution.py:491
  14.2 9.1 %collective-permute-done.corner = bf16[4,8,1664]{2,1,0:T(8,128)(2,1)S(1)} collective-permute-done((bf16[4,8,1664]{2,1,0:T(8,128)(2,1)}, bf16[4,8,1664]{2,1,0:T(8,128)(2,1)S(1)}, u32[]{:S(2)}, u32[]{:S(2)}) %collective-permute-start) | collective-permute-done | bytes 106528 | tf_op jit(solution)/shard_map/ppermute | solution.py:491
  24.5 39.5 %attention.1 = (bf16[1024,768]{1,0:T(8,128)(2,1)}, bf16[1024,768]{1,0:T(8,128)(2,1)}, bf16[4,32,1536]{2,1,0:T(8,128)(2,1)}, bf16[4,32,1536]{2,1,0:T(8,128)(2,1)}...) custom-call(s32[1]{0:T(128)} %bitcast.core_ref, ...), custom_call_target="tpu_custom_call" | custom-call | flops 16000000000 | bytes 25000000 | tf_op jit(solution)/shard_map/attention/pallas_call | solution.py:257
  64.0 2.3 %collective-permute-start.4 = (bf16[1536,768]{1,0:T(8,128)(2,1)}, bf16[1536,768]{1,0:T(8,128)(2,1)S(1)}, u32[]{:S(2)}, u32[]{:S(2)}) collective-permute-start(bf16[1536,768]{1,0:T(8,128)(2,1)} %get-tuple-element.44), channel_id=1, source_target_pairs={{0,8},{1,9},{2,10},{3,11},{4,12},{5,13},{6,14},{7,15},{8,0},{9,1},... | collective-permute-start | bytes 7077896 | tf_op jit(solution)/shard_map/ppermute | solution.py:443
  66.4 4.3 %collective-permute-done.4.recv = bf16[1536,768]{1,0:T(8,128)(2,1)S(1)} collective-permute-done((bf16[1536,768]{1,0:T(8,128)(2,1)}, bf16[1536,768]{1,0:T(8,128)(2,1)S(1)}, u32[]{:S(2)}, u32[]{:S(2)}) %collective-permute-start.4) | collective-permute-done | bytes 2359328 | tf_op jit(solution)/shard_map/ppermute | solution.py:443
  70.7 1.7 %copy-done.2 = bf16[1536,768]{1,0:T(8,128)(2,1)S(1)} copy-done((bf16[1536,768]{1,0:T(8,128)(2,1)S(1)}, bf16[1536,768]{1,0:T(8,128)(2,1)}, u32[]{:S(2)}) %copy-start.2) | copy-done | bytes 2359320
  72.3 2.0 %combine.1 = (bf16[256,768]{1,0:T(8,128)(2,1)S(1)}, bf16[256,768]{1,0:T(8,128)(2,1)S(1)}, bf16[256,768]{1,0:T(8,128)(2,1)S(1)}, bf16[256,768]{1,0:T(8,128)(2,1)}...) custom-call(s32[3]{0:T(128)S(1)} %pad_add_fusion.bits, bf16[1536,768]{1,0:T(8,128)(2,1)S(1)} %copy-done.2, ...), custom_call_target="tpu_custom_call" | custom-call | flops 1200000 | bytes 7000000 | tf_op jit(solution)/shard_map/combine/pallas_call | solution.py:334
  75.1 1.6 %collective-permute-start.13 = (bf16[256,768]{1,0:T(8,128)(2,1)}, bf16[256,768]{1,0:T(8,128)(2,1)S(1)}, u32[]{:S(2)}, u32[]{:S(2)}) collective-permute-start(bf16[256,768]{1,0:T(8,128)(2,1)} %get-tuple-element.48), channel_id=1, source_target_pairs={{0,16},{1,17},{2,18},{3,19},{4,20},{5,21},{6,22},{7,23},{8,56},{9,... | collective-permute-start | bytes 1179656 | tf_op jit(solution)/shard_map/ppermute | solution.py:443
  76.8 6.3 %collective-permute-done.5 = bf16[256,768]{1,0:T(8,128)(2,1)S(1)} collective-permute-done((bf16[256,768]{1,0:T(8,128)(2,1)}, bf16[256,768]{1,0:T(8,128)(2,1)S(1)}, u32[]{:S(2)}, u32[]{:S(2)}) %collective-permute-start.5) | collective-permute-done | bytes 393248 | tf_op jit(solution)/shard_map/ppermute | solution.py:443
  83.2 1.7 %collective-permute-start.6 = (bf16[128,768]{1,0:T(8,128)(2,1)S(1)}, bf16[128,768]{1,0:T(8,128)(2,1)S(1)}, u32[]{:S(2)}, u32[]{:S(2)}) collective-permute-start(bf16[128,768]{1,0:T(8,128)(2,1)S(1)} %constant_dynamic-slice_fusion.2), channel_id=1, source_target_pairs={{0,16},{1,17},{2,18},{3,19},{4,20},{5,21},{6,22},{7,23},{8,56},{9,... | collective-permute-start | bytes 589832 | tf_op jit(solution)/shard_map/ppermute | solution.py:443
  85.3 1.6 %collective-permute-start.22 = (bf16[128,768]{1,0:T(8,128)(2,1)S(1)}, bf16[128,768]{1,0:T(8,128)(2,1)S(1)}, u32[]{:S(2)}, u32[]{:S(2)}) collective-permute-start(bf16[128,768]{1,0:T(8,128)(2,1)S(1)} %constant_dynamic-slice_fusion), channel_id=1, source_target_pairs={{0,1},{1,0},{2,3},{3,2},{4,5},{5,4},{6,7},{7,6},{8,11},{9,10},{10,... | collective-permute-start | bytes 589832 | tf_op jit(solution)/shard_map/ppermute | solution.py:443
  86.9 2.1 %collective-permute-done.6 = bf16[128,768]{1,0:T(8,128)(2,1)S(1)} collective-permute-done((bf16[128,768]{1,0:T(8,128)(2,1)S(1)}, bf16[128,768]{1,0:T(8,128)(2,1)S(1)}, u32[]{:S(2)}, u32[]{:S(2)}) %collective-permute-start.6) | collective-permute-done | bytes 196640 | tf_op jit(solution)/shard_map/ppermute | solution.py:443
  89.2 1.5 collective-permute-done.14
  91.2 1.7 %collective-permute-start.23 = (bf16[128,768]{1,0:T(8,128)(2,1)S(1)}, bf16[128,768]{1,0:T(8,128)(2,1)S(1)}, u32[]{:S(2)}, u32[]{:S(2)}) collective-permute-start(bf16[128,768]{1,0:T(8,128)(2,1)S(1)} %add_convert_fusion.7), channel_id=1, source_target_pairs={{0,16},{1,17},{2,18},{3,19},{4,20},{5,21},{6,22},{7,23},{8,56},{9,... | collective-permute-start | bytes 589832 | tf_op jit(solution)/shard_map/ppermute | solution.py:443
  92.9 1.9 %collective-permute-done.7 = bf16[128,768]{1,0:T(8,128)(2,1)S(1)} collective-permute-done((bf16[128,768]{1,0:T(8,128)(2,1)S(1)}, bf16[128,768]{1,0:T(8,128)(2,1)S(1)}, u32[]{:S(2)}, u32[]{:S(2)}) %collective-permute-start.7) | collective-permute-done | bytes 196640 | tf_op jit(solution)/shard_map/ppermute | solution.py:443
  95.0 1.6 %collective-permute-done.15 = bf16[128,768]{1,0:T(8,128)(2,1)S(1)} collective-permute-done((bf16[128,768]{1,0:T(8,128)(2,1)S(1)}, bf16[128,768]{1,0:T(8,128)(2,1)S(1)}, u32[]{:S(2)}, u32[]{:S(2)}) %collective-permute-start.15) | collective-permute-done | bytes 196640 | tf_op jit(solution)/shard_map/ppermute | solution.py:443
  96.6 3.6 %collective-permute-start.16 = (bf16[128,768]{1,0:T(8,128)(2,1)S(1)}, bf16[128,768]{1,0:T(8,128)(2,1)S(1)}, u32[]{:S(2)}, u32[]{:S(2)}) collective-permute-start(bf16[128,768]{1,0:T(8,128)(2,1)S(1)} %add_convert_fusion.11), channel_id=1, source_target_pairs={{0,48},{1,49},{2,50},{3,51},{4,52},{5,53},{6,54},{7,55},{8,24},{9,... | collective-permute-start | bytes 589832 | tf_op jit(solution)/shard_map/ppermute | solution.py:443
  100.3 2.6 %collective-permute-start.24 = (bf16[128,768]{1,0:T(8,128)(2,1)S(1)}, bf16[128,768]{1,0:T(8,128)(2,1)S(1)}, u32[]{:S(2)}, u32[]{:S(2)}) collective-permute-start(bf16[128,768]{1,0:T(8,128)(2,1)S(1)} %add_convert_fusion.6), channel_id=1, source_target_pairs={{0,68},{1,69},{2,70},{3,71},{4,64},{5,65},{6,66},{7,67},{8,12},{9,... | collective-permute-start | bytes 589832 | tf_op jit(solution)/shard_map/ppermute | solution.py:443
  103.0 2.8 %collective-permute-start.9 = (bf16[128,768]{1,0:T(8,128)(2,1)S(1)}, bf16[128,768]{1,0:T(8,128)(2,1)S(1)}, u32[]{:S(2)}, u32[]{:S(2)}) collective-permute-start(bf16[128,768]{1,0:T(8,128)(2,1)S(1)} %add_convert_fusion.15), channel_id=1, source_target_pairs={{0,48},{1,49},{2,50},{3,51},{4,52},{5,53},{6,54},{7,55},{8,24},{9,... | collective-permute-start | bytes 589832 | tf_op jit(solution)/shard_map/ppermute | solution.py:443
  105.8 1.9 %collective-permute-start.17 = (bf16[128,768]{1,0:T(8,128)(2,1)S(1)}, bf16[128,768]{1,0:T(8,128)(2,1)S(1)}, u32[]{:S(2)}, u32[]{:S(2)}) collective-permute-start(bf16[128,768]{1,0:T(8,128)(2,1)S(1)} %add_convert_fusion.10), channel_id=1, source_target_pairs={{0,68},{1,69},{2,70},{3,71},{4,64},{5,65},{6,66},{7,67},{8,12},{9,... | collective-permute-start | bytes 589832 | tf_op jit(solution)/shard_map/ppermute | solution.py:443
  114.8 2.2 %collective-permute-start.26 = (bf16[128,768]{1,0:T(8,128)(2,1)S(1)}, bf16[128,768]{1,0:T(8,128)(2,1)S(1)}, u32[]{:S(2)}, u32[]{:S(2)}) collective-permute-start(bf16[128,768]{1,0:T(8,128)(2,1)S(1)} %add_convert_fusion.4), channel_id=1, source_target_pairs={{0,48},{1,49},{2,50},{3,51},{4,52},{5,53},{6,54},{7,55},{8,24},{9,... | collective-permute-start | bytes 589832 | tf_op jit(solution)/shard_map/ppermute | solution.py:443
  117.3 3.0 %collective-permute-done.18 = bf16[128,768]{1,0:T(8,128)(2,1)S(1)} collective-permute-done((bf16[128,768]{1,0:T(8,128)(2,1)S(1)}, bf16[128,768]{1,0:T(8,128)(2,1)S(1)}, u32[]{:S(2)}, u32[]{:S(2)}) %collective-permute-start.18) | collective-permute-done | bytes 196640 | tf_op jit(solution)/shard_map/ppermute | solution.py:443
  124.0 2.0 %collective-permute-done.19.refs_1_ = bf16[128,768]{1,0:T(8,128)(2,1)S(1)} collective-permute-done((bf16[128,768]{1,0:T(8,128)(2,1)S(1)}, bf16[128,768]{1,0:T(8,128)(2,1)S(1)}, u32[]{:S(2)}, u32[]{:S(2)}) %collective-permute-start.19) | collective-permute-done | bytes 196640 | tf_op jit(solution)/shard_map/ppermute | solution.py:443
  128.4 3.4 %collective-permute-done.12.refs_1_ = bf16[256,768]{1,0:T(8,128)(2,1)S(1)} collective-permute-done((bf16[256,768]{1,0:T(8,128)(2,1)S(1)}, bf16[256,768]{1,0:T(8,128)(2,1)S(1)}, u32[]{:S(2)}, u32[]{:S(2)}) %collective-permute-start.12) | collective-permute-done | bytes 393248 | tf_op jit(solution)/shard_map/ppermute | solution.py:443
  131.8 2.2 %collective-permute-done.20.refs_3_ = bf16[256,768]{1,0:T(8,128)(2,1)S(1)} collective-permute-done((bf16[256,768]{1,0:T(8,128)(2,1)S(1)}, bf16[256,768]{1,0:T(8,128)(2,1)S(1)}, u32[]{:S(2)}, u32[]{:S(2)}) %collective-permute-start.20) | collective-permute-done | bytes 393248 | tf_op jit(solution)/shard_map/ppermute | solution.py:443
  133.9 1.6 collective-permute-done.28.refs_5_
  138.5 2.5 %collective-permute-start.29 = (bf16[4,8,1536]{2,1,0:T(8,128)(2,1)S(1)}, bf16[4,8,1536]{2,1,0:T(8,128)(2,1)S(1)}, u32[]{:S(2)}, u32[]{:S(2)}) collective-permute-start(bf16[4,8,1536]{2,1,0:T(8,128)(2,1)S(1)} %copy-done.13), channel_id=1, source_target_pairs={{0,15},{1,8},{2,9},{3,10},{4,11},{5,12},{6,13},{7,14},{8,23},{9,16... | collective-permute-start | bytes 294920 | tf_op jit(solution)/shard_map/ppermute | solution.py:491
  141.0 5.2 %widen.1 = (f32[768,2304]{1,0:T(8,128)}, f32[768,768]{1,0:T(8,128)}) custom-call(s32[1]{0:T(128)} %bitcast.core_ref, bf16[1536,768]{1,0:T(8,128)(2,1)S(1)} %join.7.own, bf16[1536,768]{1,0:T(8,128)(2,1)S(1)} %collective-permute-done.33.other), custom_call_target="tpu_custom_call" | custom-call | bytes 14000000 | tf_op jit(solution)/shard_map/widen/pallas_call | solution.py:397
  146.2 8.6 %collective-permute-done.29.corner = bf16[4,8,1536]{2,1,0:T(8,128)(2,1)S(1)} collective-permute-done((bf16[4,8,1536]{2,1,0:T(8,128)(2,1)S(1)}, bf16[4,8,1536]{2,1,0:T(8,128)(2,1)S(1)}, u32[]{:S(2)}, u32[]{:S(2)}) %collective-permute-start.29) | collective-permute-done | bytes 98336 | tf_op jit(solution)/shard_map/ppermute | solution.py:491
  154.9 2.3 %merge.1 = (bf16[16,64,768]{2,1,0:T(8,128)(2,1)}, bf16[16,64,768]{2,1,0:T(8,128)(2,1)}) custom-call(bf16[16,64,768]{2,1,0:T(8,128)(2,1)S(1)} %copy-done, bf16[16,64,768]{2,1,0:T(8,128)(2,1)S(1)} %copy-done.1, bf16[1024,768]{1,0:T(8,128)(2,1)S(1)} %copy-done.3, bf16[1024,768]{1,0:T(8,128)(2,1)S(1)} %copy-done.4, ...), custom_call_target="tpu_custom_call" | custom-call | flops 3000000 | bytes 11000000 | tf_op jit(solution)/shard_map/merge/pallas_call | solution.py:312
  (97 shorter events, 21.6 us)
Async XLA Ops:
  4.7 18.6 %collective-permute-start.2 = (bf16[4,32,1664]{2,1,0:T(8,128)(2,1)}, bf16[4,32,1664]{2,1,0:T(8,128)(2,1)S(1)}, u32[]{:S(2)}, u32[]{:S(2)}) collective-permute-start(bf16[4,32,1664]{2,1,0:T(8,128)(2,1)} %get-tuple-element.39), channel_id=1, source_target_pairs={{0,7},{1,0},{2,1},{3,2},{4,3},{5,4},{6,5},{7,6},{8,15},{9,8},{10,9... | collective-permute-start | bytes 1277960 | tf_op jit(solution)/shard_map/ppermute | solution.py:491
  8.9 14.7 %collective-permute-start.3 = (bf16[4,32,1664]{2,1,0:T(8,128)(2,1)}, bf16[4,32,1664]{2,1,0:T(8,128)(2,1)S(1)}, u32[]{:S(2)}, u32[]{:S(2)}) collective-permute-start(bf16[4,32,1664]{2,1,0:T(8,128)(2,1)} %get-tuple-element.40), channel_id=1, source_target_pairs={{0,1},{1,2},{2,3},{3,4},{4,5},{5,6},{6,7},{7,0},{8,9},{9,10},{10,1... | collective-permute-start | bytes 1277960 | tf_op jit(solution)/shard_map/ppermute | solution.py:491
  8.9 14.4 %collective-permute-start.1 = (bf16[6,8,1664]{2,1,0:T(8,128)(2,1)}, bf16[6,8,1664]{2,1,0:T(8,128)(2,1)S(1)}, u32[]{:S(2)}, u32[]{:S(2)}) collective-permute-start(bf16[6,8,1664]{2,1,0:T(8,128)(2,1)} %get-tuple-element.38), channel_id=1, source_target_pairs={{0,120},{1,121},{2,122},{3,123},{4,124},{5,125},{6,126},{7,127},{8... | collective-permute-start | bytes 479240 | tf_op jit(solution)/shard_map/ppermute | solution.py:491
  14.1 9.2 %collective-permute-start = (bf16[4,8,1664]{2,1,0:T(8,128)(2,1)}, bf16[4,8,1664]{2,1,0:T(8,128)(2,1)S(1)}, u32[]{:S(2)}, u32[]{:S(2)}) collective-permute-start(bf16[4,8,1664]{2,1,0:T(8,128)(2,1)} %get-tuple-element.37), channel_id=1, source_target_pairs={{0,121},{1,122},{2,123},{3,124},{4,125},{5,126},{6,127},{7,120},{8... | collective-permute-start | bytes 319496 | tf_op jit(solution)/shard_map/ppermute | solution.py:491
  64.0 6.6 %collective-permute-start.4 = (bf16[1536,768]{1,0:T(8,128)(2,1)}, bf16[1536,768]{1,0:T(8,128)(2,1)S(1)}, u32[]{:S(2)}, u32[]{:S(2)}) collective-permute-start(bf16[1536,768]{1,0:T(8,128)(2,1)} %get-tuple-element.44), channel_id=1, source_target_pairs={{0,8},{1,9},{2,10},{3,11},{4,12},{5,13},{6,14},{7,15},{8,0},{9,1},... | collective-permute-start | bytes 7077896 | tf_op jit(solution)/shard_map/ppermute | solution.py:443
  75.1 8.0 %collective-permute-start.5 = (bf16[256,768]{1,0:T(8,128)(2,1)}, bf16[256,768]{1,0:T(8,128)(2,1)S(1)}, u32[]{:S(2)}, u32[]{:S(2)}) collective-permute-start(bf16[256,768]{1,0:T(8,128)(2,1)} %get-tuple-element.46), channel_id=1, source_target_pairs={{0,1},{1,0},{2,3},{3,2},{4,5},{5,4},{6,7},{7,6},{8,11},{9,10},{10,... | collective-permute-start | bytes 1179656 | tf_op jit(solution)/shard_map/ppermute | solution.py:443
  75.1 9.8 %collective-permute-start.13 = (bf16[256,768]{1,0:T(8,128)(2,1)}, bf16[256,768]{1,0:T(8,128)(2,1)S(1)}, u32[]{:S(2)}, u32[]{:S(2)}) collective-permute-start(bf16[256,768]{1,0:T(8,128)(2,1)} %get-tuple-element.48), channel_id=1, source_target_pairs={{0,16},{1,17},{2,18},{3,19},{4,20},{5,21},{6,22},{7,23},{8,56},{9,... | collective-permute-start | bytes 1179656 | tf_op jit(solution)/shard_map/ppermute | solution.py:443
  76.7 8.5 %collective-permute-start.21 = (bf16[256,768]{1,0:T(8,128)(2,1)}, bf16[256,768]{1,0:T(8,128)(2,1)S(1)}, u32[]{:S(2)}, u32[]{:S(2)}) collective-permute-start(bf16[256,768]{1,0:T(8,128)(2,1)} %copy-done.5), channel_id=1, source_target_pairs={{0,4},{1,5},{2,6},{3,7},{4,0},{5,1},{6,2},{7,3},{8,76},{9,77},{10,... | collective-permute-start | bytes 1179656 | tf_op jit(solution)/shard_map/ppermute | solution.py:443
  83.2 5.7 %collective-permute-start.6 = (bf16[128,768]{1,0:T(8,128)(2,1)S(1)}, bf16[128,768]{1,0:T(8,128)(2,1)S(1)}, u32[]{:S(2)}, u32[]{:S(2)}) collective-permute-start(bf16[128,768]{1,0:T(8,128)(2,1)S(1)} %constant_dynamic-slice_fusion.2), channel_id=1, source_target_pairs={{0,16},{1,17},{2,18},{3,19},{4,20},{5,21},{6,22},{7,23},{8,56},{9,... | collective-permute-start | bytes 589832 | tf_op jit(solution)/shard_map/ppermute | solution.py:443
  85.0 5.8 %collective-permute-start.14 = (bf16[128,768]{1,0:T(8,128)(2,1)S(1)}, bf16[128,768]{1,0:T(8,128)(2,1)S(1)}, u32[]{:S(2)}, u32[]{:S(2)}) collective-permute-start(bf16[128,768]{1,0:T(8,128)(2,1)S(1)} %constant_dynamic-slice_fusion.1), channel_id=1, source_target_pairs={{0,4},{1,5},{2,6},{3,7},{4,0},{5,1},{6,2},{7,3},{8,76},{9,77},{10,... | collective-permute-start | bytes 589832 | tf_op jit(solution)/shard_map/ppermute | solution.py:443
  85.3 5.8 %collective-permute-start.22 = (bf16[128,768]{1,0:T(8,128)(2,1)S(1)}, bf16[128,768]{1,0:T(8,128)(2,1)S(1)}, u32[]{:S(2)}, u32[]{:S(2)}) collective-permute-start(bf16[128,768]{1,0:T(8,128)(2,1)S(1)} %constant_dynamic-slice_fusion), channel_id=1, source_target_pairs={{0,1},{1,0},{2,3},{3,2},{4,5},{5,4},{6,7},{7,6},{8,11},{9,10},{10,... | collective-permute-start | bytes 589832 | tf_op jit(solution)/shard_map/ppermute | solution.py:443
  89.0 5.8 %collective-permute-start.7 = (bf16[128,768]{1,0:T(8,128)(2,1)S(1)}, bf16[128,768]{1,0:T(8,128)(2,1)S(1)}, u32[]{:S(2)}, u32[]{:S(2)}) collective-permute-start(bf16[128,768]{1,0:T(8,128)(2,1)S(1)} %add_convert_fusion.17), channel_id=1, source_target_pairs={{0,4},{1,5},{2,6},{3,7},{4,0},{5,1},{6,2},{7,3},{8,76},{9,77},{10,... | collective-permute-start | bytes 589832 | tf_op jit(solution)/shard_map/ppermute | solution.py:443
  90.8 5.7 %collective-permute-start.15 = (bf16[128,768]{1,0:T(8,128)(2,1)S(1)}, bf16[128,768]{1,0:T(8,128)(2,1)S(1)}, u32[]{:S(2)}, u32[]{:S(2)}) collective-permute-start(bf16[128,768]{1,0:T(8,128)(2,1)S(1)} %add_convert_fusion.12), channel_id=1, source_target_pairs={{0,1},{1,0},{2,3},{3,2},{4,5},{5,4},{6,7},{7,6},{8,11},{9,10},{10,... | collective-permute-start | bytes 589832 | tf_op jit(solution)/shard_map/ppermute | solution.py:443
  91.2 9.1 %collective-permute-start.23 = (bf16[128,768]{1,0:T(8,128)(2,1)S(1)}, bf16[128,768]{1,0:T(8,128)(2,1)S(1)}, u32[]{:S(2)}, u32[]{:S(2)}) collective-permute-start(bf16[128,768]{1,0:T(8,128)(2,1)S(1)} %add_convert_fusion.7), channel_id=1, source_target_pairs={{0,16},{1,17},{2,18},{3,19},{4,20},{5,21},{6,22},{7,23},{8,56},{9,... | collective-permute-start | bytes 589832 | tf_op jit(solution)/shard_map/ppermute | solution.py:443
  94.9 8.1 %collective-permute-start.8 = (bf16[128,768]{1,0:T(8,128)(2,1)S(1)}, bf16[128,768]{1,0:T(8,128)(2,1)S(1)}, u32[]{:S(2)}, u32[]{:S(2)}) collective-permute-start(bf16[128,768]{1,0:T(8,128)(2,1)S(1)} %add_convert_fusion.16), channel_id=1, source_target_pairs={{0,3},{1,2},{2,1},{3,0},{4,7},{5,6},{6,5},{7,4},{8,9},{9,8},{10,11... | collective-permute-start | bytes 589832 | tf_op jit(solution)/shard_map/ppermute | solution.py:443
  96.6 9.1 %collective-permute-start.16 = (bf16[128,768]{1,0:T(8,128)(2,1)S(1)}, bf16[128,768]{1,0:T(8,128)(2,1)S(1)}, u32[]{:S(2)}, u32[]{:S(2)}) collective-permute-start(bf16[128,768]{1,0:T(8,128)(2,1)S(1)} %add_convert_fusion.11), channel_id=1, source_target_pairs={{0,48},{1,49},{2,50},{3,51},{4,52},{5,53},{6,54},{7,55},{8,24},{9,... | collective-permute-start | bytes 589832 | tf_op jit(solution)/shard_map/ppermute | solution.py:443
  100.3 7.4 %collective-permute-start.24 = (bf16[128,768]{1,0:T(8,128)(2,1)S(1)}, bf16[128,768]{1,0:T(8,128)(2,1)S(1)}, u32[]{:S(2)}, u32[]{:S(2)}) collective-permute-start(bf16[128,768]{1,0:T(8,128)(2,1)S(1)} %add_convert_fusion.6), channel_id=1, source_target_pairs={{0,68},{1,69},{2,70},{3,71},{4,64},{5,65},{6,66},{7,67},{8,12},{9,... | collective-permute-start | bytes 589832 | tf_op jit(solution)/shard_map/ppermute | solution.py:443
  103.0 7.0 %collective-permute-start.9 = (bf16[128,768]{1,0:T(8,128)(2,1)S(1)}, bf16[128,768]{1,0:T(8,128)(2,1)S(1)}, u32[]{:S(2)}, u32[]{:S(2)}) collective-permute-start(bf16[128,768]{1,0:T(8,128)(2,1)S(1)} %add_convert_fusion.15), channel_id=1, source_target_pairs={{0,48},{1,49},{2,50},{3,51},{4,52},{5,53},{6,54},{7,55},{8,24},{9,... | collective-permute-start | bytes 589832 | tf_op jit(solution)/shard_map/ppermute | solution.py:443
  105.8 7.0 %collective-permute-start.17 = (bf16[128,768]{1,0:T(8,128)(2,1)S(1)}, bf16[128,768]{1,0:T(8,128)(2,1)S(1)}, u32[]{:S(2)}, u32[]{:S(2)}) collective-permute-start(bf16[128,768]{1,0:T(8,128)(2,1)S(1)} %add_convert_fusion.10), channel_id=1, source_target_pairs={{0,68},{1,69},{2,70},{3,71},{4,64},{5,65},{6,66},{7,67},{8,12},{9,... | collective-permute-start | bytes 589832 | tf_op jit(solution)/shard_map/ppermute | solution.py:443
  107.8 7.0 %collective-permute-start.25 = (bf16[128,768]{1,0:T(8,128)(2,1)S(1)}, bf16[128,768]{1,0:T(8,128)(2,1)S(1)}, u32[]{:S(2)}, u32[]{:S(2)}) collective-permute-start(bf16[128,768]{1,0:T(8,128)(2,1)S(1)} %add_convert_fusion.5), channel_id=1, source_target_pairs={{0,3},{1,2},{2,1},{3,0},{4,7},{5,6},{6,5},{7,4},{8,9},{9,8},{10,11... | collective-permute-start | bytes 589832 | tf_op jit(solution)/shard_map/ppermute | solution.py:443
  110.0 7.0 %collective-permute-start.10 = (bf16[128,768]{1,0:T(8,128)(2,1)S(1)}, bf16[128,768]{1,0:T(8,128)(2,1)S(1)}, u32[]{:S(2)}, u32[]{:S(2)}) collective-permute-start(bf16[128,768]{1,0:T(8,128)(2,1)S(1)} %add_convert_fusion.14), channel_id=1, source_target_pairs={{0,68},{1,69},{2,70},{3,71},{4,64},{5,65},{6,66},{7,67},{8,12},{9,... | collective-permute-start | bytes 589832 | tf_op jit(solution)/shard_map/ppermute | solution.py:443
  112.8 7.4 %collective-permute-start.18 = (bf16[128,768]{1,0:T(8,128)(2,1)S(1)}, bf16[128,768]{1,0:T(8,128)(2,1)S(1)}, u32[]{:S(2)}, u32[]{:S(2)}) collective-permute-start(bf16[128,768]{1,0:T(8,128)(2,1)S(1)} %add_convert_fusion.9), channel_id=1, source_target_pairs={{0,3},{1,2},{2,1},{3,0},{4,7},{5,6},{6,5},{7,4},{8,9},{9,8},{10,11... | collective-permute-start | bytes 589832 | tf_op jit(solution)/shard_map/ppermute | solution.py:443
  114.8 7.0 %collective-permute-start.26 = (bf16[128,768]{1,0:T(8,128)(2,1)S(1)}, bf16[128,768]{1,0:T(8,128)(2,1)S(1)}, u32[]{:S(2)}, u32[]{:S(2)}) collective-permute-start(bf16[128,768]{1,0:T(8,128)(2,1)S(1)} %add_convert_fusion.4), channel_id=1, source_target_pairs={{0,48},{1,49},{2,50},{3,51},{4,52},{5,53},{6,54},{7,55},{8,24},{9,... | collective-permute-start | bytes 589832 | tf_op jit(solution)/shard_map/ppermute | solution.py:443
  117.0 5.7 %collective-permute-start.11 = (bf16[128,768]{1,0:T(8,128)(2,1)S(1)}, bf16[128,768]{1,0:T(8,128)(2,1)S(1)}, u32[]{:S(2)}, u32[]{:S(2)}) collective-permute-start(bf16[128,768]{1,0:T(8,128)(2,1)S(1)} %add_convert_fusion.13.refs_0_), channel_id=1, source_target_pairs={{0,16},{1,17},{2,18},{3,19},{4,20},{5,21},{6,22},{7,23},{8,56},{9,... | collective-permute-start | bytes 589832 | tf_op jit(solution)/shard_map/ppermute | solution.py:443
  120.3 5.8 %collective-permute-start.19 = (bf16[128,768]{1,0:T(8,128)(2,1)S(1)}, bf16[128,768]{1,0:T(8,128)(2,1)S(1)}, u32[]{:S(2)}, u32[]{:S(2)}) collective-permute-start(bf16[128,768]{1,0:T(8,128)(2,1)S(1)} %add_convert_fusion.8.refs_0_), channel_id=1, source_target_pairs={{0,4},{1,5},{2,6},{3,7},{4,0},{5,1},{6,2},{7,3},{8,76},{9,77},{10,... | collective-permute-start | bytes 589832 | tf_op jit(solution)/shard_map/ppermute | solution.py:443
  122.8 9.0 %collective-permute-start.12 = (bf16[256,768]{1,0:T(8,128)(2,1)S(1)}, bf16[256,768]{1,0:T(8,128)(2,1)S(1)}, u32[]{:S(2)}, u32[]{:S(2)}) collective-permute-start(bf16[256,768]{1,0:T(8,128)(2,1)S(1)} %join.4.refs_0_), channel_id=1, source_target_pairs={{0,1},{1,0},{2,3},{3,2},{4,5},{5,4},{6,7},{7,6},{8,11},{9,10},{10,... | collective-permute-start | bytes 1179656 | tf_op jit(solution)/shard_map/ppermute | solution.py:443
  126.1 7.9 %collective-permute-start.20 = (bf16[256,768]{1,0:T(8,128)(2,1)S(1)}, bf16[256,768]{1,0:T(8,128)(2,1)S(1)}, u32[]{:S(2)}, u32[]{:S(2)}) collective-permute-start(bf16[256,768]{1,0:T(8,128)(2,1)S(1)} %join.5.refs_2_), channel_id=1, source_target_pairs={{0,16},{1,17},{2,18},{3,19},{4,20},{5,21},{6,22},{7,23},{8,56},{9,... | collective-permute-start | bytes 1179656 | tf_op jit(solution)/shard_map/ppermute | solution.py:443
  127.6 7.9 %collective-permute-start.28 = (bf16[256,768]{1,0:T(8,128)(2,1)S(1)}, bf16[256,768]{1,0:T(8,128)(2,1)S(1)}, u32[]{:S(2)}, u32[]{:S(2)}) collective-permute-start(bf16[256,768]{1,0:T(8,128)(2,1)S(1)} %join.6.refs_4_), channel_id=1, source_target_pairs={{0,4},{1,5},{2,6},{3,7},{4,0},{5,1},{6,2},{7,3},{8,76},{9,77},{10,... | collective-permute-start | bytes 1179656 | tf_op jit(solution)/shard_map/ppermute | solution.py:443
  136.3 18.5 %collective-permute-start.31 = (bf16[4,32,1536]{2,1,0:T(8,128)(2,1)S(1)}, bf16[4,32,1536]{2,1,0:T(8,128)(2,1)S(1)}, u32[]{:S(2)}, u32[]{:S(2)}) collective-permute-start(bf16[4,32,1536]{2,1,0:T(8,128)(2,1)S(1)} %copy-done.9), channel_id=1, source_target_pairs={{0,7},{1,0},{2,1},{3,2},{4,3},{5,4},{6,5},{7,6},{8,15},{9,8},{10,9... | collective-permute-start | bytes 1179656 | tf_op jit(solution)/shard_map/ppermute | solution.py:491
  137.3 17.6 %collective-permute-start.32 = (bf16[4,32,1536]{2,1,0:T(8,128)(2,1)S(1)}, bf16[4,32,1536]{2,1,0:T(8,128)(2,1)S(1)}, u32[]{:S(2)}, u32[]{:S(2)}) collective-permute-start(bf16[4,32,1536]{2,1,0:T(8,128)(2,1)S(1)} %copy-done.8), channel_id=1, source_target_pairs={{0,1},{1,2},{2,3},{3,4},{4,5},{5,6},{6,7},{7,0},{8,9},{9,10},{10,1... | collective-permute-start | bytes 1179656 | tf_op jit(solution)/shard_map/ppermute | solution.py:491
  138.4 16.4 %collective-permute-start.30 = (bf16[6,8,1536]{2,1,0:T(8,128)(2,1)S(1)}, bf16[6,8,1536]{2,1,0:T(8,128)(2,1)S(1)}, u32[]{:S(2)}, u32[]{:S(2)}) collective-permute-start(bf16[6,8,1536]{2,1,0:T(8,128)(2,1)S(1)} %copy-done.11), channel_id=1, source_target_pairs={{0,8},{1,9},{2,10},{3,11},{4,12},{5,13},{6,14},{7,15},{8,16},{9,17... | collective-permute-start | bytes 442376 | tf_op jit(solution)/shard_map/ppermute | solution.py:491
  138.5 16.4 %collective-permute-start.29 = (bf16[4,8,1536]{2,1,0:T(8,128)(2,1)S(1)}, bf16[4,8,1536]{2,1,0:T(8,128)(2,1)S(1)}, u32[]{:S(2)}, u32[]{:S(2)}) collective-permute-start(bf16[4,8,1536]{2,1,0:T(8,128)(2,1)S(1)} %copy-done.13), channel_id=1, source_target_pairs={{0,15},{1,8},{2,9},{3,10},{4,11},{5,12},{6,13},{7,14},{8,23},{9,16... | collective-permute-start | bytes 294920 | tf_op jit(solution)/shard_map/ppermute | solution.py:491
  (16 other events, 131.2 us)
